TPU v7x, 256 devices: a whole 4x4x8 slice. The times are simulated.
256 devices in a mesh: row: 8 (over z), col: 32 (over x, y, core).
Axes of the slice: x: 4, y: 4, z: 8, core: 2. Of those that a mesh axis runs over, the one named last changes fastest.
Arguments:
- rhs_super: bfloat16 [2, 2, 8, 128, 512], P(None, None, 'row'), may hold values from -6 to 6
- factor_super: bfloat16 [2, 2, 8, 128, 1, 32, 128], P(None, None, 'row', None, None, 'col'), may hold values from -0.125 to 0.125
- mask_super: int32 [2, 2, 8, 1, 32], P(None, None, 'row', None, 'col'), may hold values 0 or 1
- dinv_rows: bfloat16 [1, 32, 128, 2048], P(None, 'col'), may hold values from -0.125 to 0.125
- factor_trail: bfloat16 [32, 8, 128, 1, 32, 128], P(None, 'row', None, None, 'col'), may hold values from -0.125 to 0.125
- mask_trail: int32 [32, 8, 1, 32], P(None, 'row', None, 'col'), may hold values 0 or 1
- rhs_trail: bfloat16 [32, 1, 8, 128, 512], P('col', None, 'row'), may hold values from -6 to 6
Outputs:
- solved: bfloat16 [1, 32, 128, 512], P(None, 'col')
- remaining: bfloat16 [32, 1, 8, 128, 512], P('col', None, 'row')
All inputs are finite; a program needn't handle non-finite values. No bound on the sum of `mask_super` or of `mask_trail` on one device may be relied on, other than what follows from the above.
Results may differ from a plain program's by a relative error of at most 0.0048.
Values may be sent and summed in bfloat16 or wider, within the bound.
No kernel may reach another device: no remote copies, remote signals or barrier semaphores. Data moves between devices by JAX's collectives and lax.ppermute only.
A program may use at most 64 MiB of HBM per device.

v0:
```python
import jax
import jax.numpy as jnp
from jax import lax
from jax.sharding import Mesh
from jax.sharding import PartitionSpec as P

TB = 128
ST = 16
NSB = 2
COL = ("col_0", "col_1", "col_2")


def rows_for(lines, peers):
    spare = -len(lines) % peers
    return jnp.pad(lines, [(0, spare)] + [(0, 0)] * (lines.ndim - 1))


def in_order(tiles, dim):
    tiles = jnp.moveaxis(tiles, 0, dim)
    lengths = tiles.shape
    return tiles.reshape(*lengths[:dim], lengths[dim] * lengths[dim + 1], *lengths[dim + 2 :])


def copy_for_each(x, axis):
    copies = jnp.broadcast_to(x, (lax.axis_size(axis), *x.shape))
    return lax.all_to_all(copies, axis, split_axis=0, concat_axis=0, tiled=True)


def gathered_copies(x, axis, dim):
    return in_order(copy_for_each(x, axis), dim)


def cut_along(x, dim, peers):
    lengths = x.shape
    tiles = x.reshape(*lengths[:dim], peers, lengths[dim] // peers, *lengths[dim + 1 :])
    return jnp.moveaxis(tiles, dim, 0)


def sent_and_summed(x, axis, dim):
    tiles = cut_along(x, dim, lax.axis_size(axis))
    arrived = lax.all_to_all(tiles, axis, split_axis=0, concat_axis=0, tiled=True)
    return arrived.sum(axis=0)


def total_of(x, axes):
    lines = x.reshape(-1, x.shape[-1])
    padded = rows_for(lines, lax.axis_size(axes))
    whole = gathered_copies(sent_and_summed(padded, axes, 0), axes, 0)
    return lax.slice_in_dim(whole, 0, len(lines)).reshape(x.shape)


def whole_of(x, axes, dim):
    far, near = axes
    leading = copy_for_each(x, far)
    tiles = jnp.swapaxes(copy_for_each(leading, near), 0, 1)
    return in_order(tiles.reshape(-1, *x.shape), dim)


def body(rhs_super, factor_super, mask_super, dinv_rows, factor_trail, mask_trail, rhs_trail):
    width_k = rhs_super.shape[-1]
    per_col = dinv_rows.shape[0]
    per_row = rhs_super.shape[1]
    block_rows = dinv_rows.shape[-1]
    column_here = lax.axis_index(COL)
    owners = (jnp.arange(per_col, dtype=jnp.int32) * lax.axis_size(COL) + column_here) // ST
    solved = jnp.zeros((per_col, 1, TB, width_k), jnp.bfloat16)
    for block in range(NSB):
        due_rows = rhs_super[block]
        if block > 0:
            allowed = (owners < block).astype(jnp.int32)
            keep_tiles = (mask_super[block] * allowed[None, None, :, None]).astype(jnp.bfloat16)
            masked = factor_super[block] * keep_tiles[:, :, None, :, :, None]
            partial_sum = jnp.dot(
                masked.reshape(per_row * TB, per_col * TB),
                solved.reshape(per_col * TB, width_k),
                preferred_element_type=jnp.float32,
            )
            reached = total_of(partial_sum, COL)
            due_rows = (
                (due_rows.reshape(per_row * TB, width_k).astype(jnp.float32) - reached)
                .astype(jnp.bfloat16)
                .reshape(due_rows.shape)
            )
        gathered = gathered_copies(due_rows, "row", 1).reshape(block_rows, width_k)
        position = 0

        def compute(position=position):
            return jnp.dot(
                dinv_rows[position, 0], gathered, preferred_element_type=jnp.float32
            ).astype(jnp.bfloat16)

        def retain(position=position):
            return solved[position, 0]

        columns = [lax.cond(owners[position] == block, compute, retain)]
        solved = jnp.stack(columns)[:, None]
    keep_trail = mask_trail.astype(jnp.bfloat16)[:, :, None, :, :, None]
    masked_trail = factor_trail * keep_trail
    share = rhs_trail.shape[1]
    moved = lax.all_to_all(masked_trail, COL, split_axis=0, concat_axis=4, tiled=True)
    reached = jnp.dot(
        moved.reshape(share * TB, -1),
        whole_of(solved, (("col_0", "col_1"), "col_2"), 1).reshape(-1, width_k),
        preferred_element_type=jnp.float32,
    )
    remaining = (rhs_trail.reshape(share * TB, width_k).astype(jnp.float32) - reached).astype(
        jnp.bfloat16
    )
    return (solved, remaining.reshape(rhs_trail.shape))


def solution(mesh):
    torus = Mesh(
        mesh.devices.reshape(mesh.shape["row"], 4, 4, 2), ("row", "col_0", "col_1", "col_2")
    )
    placed = (
        P(None, None, "row", None, None),
        P(None, None, "row", None, None, COL, None),
        P(None, None, "row", None, COL),
        P(None, COL, None, None),
        P(None, "row", None, None, COL, None),
        P(None, "row", None, COL),
        P(COL, None, "row", None, None),
    )
    return jax.shard_map(
        body,
        mesh=torus,
        in_specs=placed,
        out_specs=(P(None, COL, None, None), P(COL, None, "row", None, None)),
        check_vma=False,
    )
```

profile of v0, /device:TPU:1, one launch (start us, length us, event | category | flops | bytes accessed | tf_op | source)
XLA Modules:
  0.0 226.5 jit_solution(17385901437570091863)
XLA Ops:
  0.6 1.0 slice_bitcast_fusion
  1.6 1.5 broadcast_in_dim.18
  3.2 9.1 %all-to-all-start = ((bf16[8,2,1,128,512]{4,3,2,1,0:T(8,128)(2,1)}), bf16[8,2,1,128,512]{4,3,2,1,0:T(8,128)(2,1)S(1)}, u32[]{:S(2)}, u32[]{:S(2)}) async-start(bf16[8,2,1,128,512]{4,3,2,1,0:T(8,128)(2,1)} %broadcast_in_dim.18), calls=%async_computation | async-start | bytes 4194304 | tf_op jit(solution)/shard_map/all_to_all | solution.py:26
  12.5 51.5 %all-to-all-done = bf16[8,2,1,128,512]{4,3,2,1,0:T(8,128)(2,1)S(1)} async-done(((bf16[8,2,1,128,512]{4,3,2,1,0:T(8,128)(2,1)}), bf16[8,2,1,128,512]{4,3,2,1,0:T(8,128)(2,1)S(1)}, u32[]{:S(2)}, u32[]{:S(2)}) %all-to-all-start) | async-done | bytes 2097184 | tf_op jit(solution)/shard_map/all_to_all | solution.py:26
  64.0 0.7 conditional.2
  64.0 0.2 copy.10
  64.2 0.5 convolution_convert_fusion
  64.8 0.3 fusion.5
  65.1 19.0 %all_to_all.48 = f32[32,8,512]{2,1,0:T(8,128)S(1)} all-to-all(f32[32,8,512]{2,1,0:T(8,128)S(1)} %fusion.5), channel_id=1, replica_groups=mesh['row'=8,'col_0'=4,'col_1'=4,'col_2'=2] {'col_0','col_1','col_2'}, dimensions={0} | all-to-all | bytes 1048576 | tf_op jit(solution)/shard_map/all_to_all | solution.py:41
  84.1 15.0 %all_to_all.49 = f32[32,8,512]{2,1,0:T(8,128)S(1)} all-to-all(f32[32,8,512]{2,1,0:T(8,128)S(1)} %broadcast_in_dim.19), channel_id=1, replica_groups=mesh['row'=8,'col_0'=4,'col_1'=4,'col_2'=2] {'col_0','col_1','col_2'}, dimensions={0} | all-to-all | bytes 1048576 | tf_op jit(solution)/shard_map/all_to_all | solution.py:26
  99.2 1.5 broadcast_in_dim.20
  100.8 3.6 %all-to-all-start.3 = ((bf16[8,2,1,128,512]{4,3,2,1,0:T(8,128)(2,1)}), bf16[8,2,1,128,512]{4,3,2,1,0:T(8,128)(2,1)S(1)}, u32[]{:S(2)}, u32[]{:S(2)}) async-start(bf16[8,2,1,128,512]{4,3,2,1,0:T(8,128)(2,1)} %broadcast_in_dim.20), calls=%async_computation.3 | async-start | bytes 4194304 | tf_op jit(solution)/shard_map/all_to_all | solution.py:26
  104.4 51.8 %all-to-all-done.3 = bf16[8,2,1,128,512]{4,3,2,1,0:T(8,128)(2,1)S(1)} async-done(((bf16[8,2,1,128,512]{4,3,2,1,0:T(8,128)(2,1)}), bf16[8,2,1,128,512]{4,3,2,1,0:T(8,128)(2,1)S(1)}, u32[]{:S(2)}, u32[]{:S(2)}) %all-to-all-start.3) | async-done | bytes 2097184 | tf_op jit(solution)/shard_map/all_to_all | solution.py:26
  156.2 1.5 broadcast_in_dim.21
  157.8 3.7 %all-to-all-start.5 = ((bf16[16,1,1,128,512]{4,3,2,1,0:T(8,128)(2,1)}), bf16[16,1,1,128,512]{4,3,2,1,0:T(8,128)(2,1)S(1)}, u32[]{:S(2)}, u32[]{:S(2)}) async-start(bf16[16,1,1,128,512]{4,3,2,1,0:T(8,128)(2,1)} %broadcast_in_dim.21), calls=%async_computation.5 | async-start | bytes 4194304 | tf_op jit(solution)/shard_map/all_to_all | solution.py:26
  161.5 1.6 copy.12
  163.2 1.2 broadcast_multiply_fusion
  164.4 26.5 %all-to-all-done.5 = bf16[16,1,1,128,512]{4,3,2,1,0:T(8,128)(2,1)S(1)} async-done(((bf16[16,1,1,128,512]{4,3,2,1,0:T(8,128)(2,1)}), bf16[16,1,1,128,512]{4,3,2,1,0:T(8,128)(2,1)S(1)}, u32[]{:S(2)}, u32[]{:S(2)}) %all-to-all-start.5) | async-done | bytes 2097184 | tf_op jit(solution)/shard_map/all_to_all | solution.py:26
  190.8 0.5 broadcast_in_dim.22
  191.3 10.3 %all_to_all.50 = bf16[2,16,1,1,128,512]{5,4,1,3,2,0:T(8,128)(2,1)} all-to-all(bf16[2,16,1,1,128,512]{5,4,1,3,2,0:T(8,128)(2,1)S(1)} %broadcast_in_dim.22), channel_id=1, replica_groups=mesh['row'=8,'col_0'=4,'col_1'=4,'col_2'=2] {'col_2'}, dimensions={0} | all-to-all | bytes 8388608 | tf_op jit(solution)/shard_map/all_to_all | solution.py:26
  201.6 4.4 %all-to-all-start.4 = ((bf16[32,1,128,1,1,128]{2,5,4,3,1,0:T(8,128)(2,1)}), bf16[32,1,128,1,1,128]{2,5,4,3,1,0:T(8,128)(2,1)S(1)}, u32[]{:S(2)}, u32[]{:S(2)}) async-start(bf16[32,1,128,1,1,128]{2,5,4,3,1,0:T(8,128)(2,1)} %broadcast_multiply_fusion), calls=%async_computation.4 | async-start | bytes 2097152 | tf_op jit(solution)/shard_map/all_to_all | solution.py:100
  206.0 4.6 %copy.13 = bf16[2,16,1,1,128,512]{5,4,0,1,3,2:T(8,128)(2,1)} copy(bf16[2,16,1,1,128,512]{5,4,1,3,2,0:T(8,128)(2,1)} %all_to_all.50) | data formatting | bytes 8388608 | tf_op jit(solution)/shard_map/all_to_all | solution.py:26
  210.6 12.3 %all-to-all-done.4 = bf16[32,1,128,1,1,128]{2,5,4,3,1,0:T(8,128)(2,1)S(1)} async-done(((bf16[32,1,128,1,1,128]{2,5,4,3,1,0:T(8,128)(2,1)}), bf16[32,1,128,1,1,128]{2,5,4,3,1,0:T(8,128)(2,1)S(1)}, u32[]{:S(2)}, u32[]{:S(2)}) %all-to-all-start.4) | async-done | bytes 1048608 | tf_op jit(solution)/shard_map/all_to_all | solution.py:100
  222.9 3.6 %fusion.3 = bf16[1,1,1,128,512]{4,3,2,1,0:T(8,128)(2,1)} fusion(bf16[128,4096]{0,1:T(8,128)(2,1)S(1)} %bitcast.57, bf16[4096,512]{1,0:T(8,128)(2,1)} %bitcast.51, bf16[1,1,1,128,512]{4,3,2,1,0:T(8,128)(2,1)S(1)} %copy-done.3), kind=kOutput, calls=%fused_computation.6 | convolution fusion | flops 537067520 | bytes 5505024 | tf_op jit(solution)/shard_map/dot_general | solution.py:101
  (22 shorter events, 0.5 us)
Async XLA Ops:
  3.2 9.1 %copy-start.4 = (s32[2,2,1,1,1]{1,4,3,2,0:T(1,128)S(1)}, s32[2,2,1,1,1]{1,4,3,2,0:T(1,128)}, u32[]{:S(2)}) copy-start(s32[2,2,1,1,1]{1,4,3,2,0:T(1,128)} %param.13) | copy-start | bytes 52
  3.2 60.8 %copy-start = (bf16[1,1,128,2048]{3,2,1,0:T(8,128)(2,1)S(1)}, bf16[1,1,128,2048]{3,2,1,0:T(8,128)(2,1)}, u32[]{:S(2)}) copy-start(bf16[1,1,128,2048]{3,2,1,0:T(8,128)(2,1)} %param.14) | copy-start | bytes 1572868
  3.2 60.8 %all-to-all-start = ((bf16[8,2,1,128,512]{4,3,2,1,0:T(8,128)(2,1)}), bf16[8,2,1,128,512]{4,3,2,1,0:T(8,128)(2,1)S(1)}, u32[]{:S(2)}, u32[]{:S(2)}) async-start(bf16[8,2,1,128,512]{4,3,2,1,0:T(8,128)(2,1)} %broadcast_in_dim.18), calls=%async_computation | async-start | bytes 4194304 | tf_op jit(solution)/shard_map/all_to_all | solution.py:26
  64.0 0.8 slice-start
  64.6 34.5 %copy-start.2 = (bf16[2,2,1,128,512]{4,3,2,1,0:T(8,128)(2,1)S(1)}, bf16[2,2,1,128,512]{4,3,2,1,0:T(8,128)(2,1)}, u32[]{:S(2)}) copy-start(bf16[2,2,1,128,512]{4,3,2,1,0:T(8,128)(2,1)} %param.11) | copy-start | bytes 1572868
  100.8 55.4 %all-to-all-start.3 = ((bf16[8,2,1,128,512]{4,3,2,1,0:T(8,128)(2,1)}), bf16[8,2,1,128,512]{4,3,2,1,0:T(8,128)(2,1)S(1)}, u32[]{:S(2)}, u32[]{:S(2)}) async-start(bf16[8,2,1,128,512]{4,3,2,1,0:T(8,128)(2,1)} %broadcast_in_dim.20), calls=%async_computation.3 | async-start | bytes 4194304 | tf_op jit(solution)/shard_map/all_to_all | solution.py:26
  156.2 1.6 copy-start.1
  157.8 33.0 %all-to-all-start.5 = ((bf16[16,1,1,128,512]{4,3,2,1,0:T(8,128)(2,1)}), bf16[16,1,1,128,512]{4,3,2,1,0:T(8,128)(2,1)S(1)}, u32[]{:S(2)}, u32[]{:S(2)}) async-start(bf16[16,1,1,128,512]{4,3,2,1,0:T(8,128)(2,1)} %broadcast_in_dim.21), calls=%async_computation.5 | async-start | bytes 4194304 | tf_op jit(solution)/shard_map/all_to_all | solution.py:26
  161.5 1.6 copy-start.5
  201.6 21.3 %all-to-all-start.4 = ((bf16[32,1,128,1,1,128]{2,5,4,3,1,0:T(8,128)(2,1)}), bf16[32,1,128,1,1,128]{2,5,4,3,1,0:T(8,128)(2,1)S(1)}, u32[]{:S(2)}, u32[]{:S(2)}) async-start(bf16[32,1,128,1,1,128]{2,5,4,3,1,0:T(8,128)(2,1)} %broadcast_multiply_fusion), calls=%async_computation.4 | async-start | bytes 2097152 | tf_op jit(solution)/shard_map/all_to_all | solution.py:100
  206.0 16.9 %copy-start.3 = (bf16[1,1,1,128,512]{4,3,2,1,0:T(8,128)(2,1)S(1)}, bf16[1,1,1,128,512]{4,3,2,1,0:T(8,128)(2,1)}, u32[]{:S(2)}) copy-start(bf16[1,1,1,128,512]{4,3,2,1,0:T(8,128)(2,1)} %param.17) | copy-start | bytes 393220
where the time goes:
time: 227 us; the launch traced here: 226 us
  waiting for transfers between devices  142 us (63%)
  blocking collectives  44.3 us (20%)
  starting transfers between devices  20.8 us (9%)
  local copies, waits for them, and re-layouts  13 us (6%)
  matrix products  4.31 us (2%)
    all_to_all x3, waiting for transfers between devices, copy_for_each(): return lax.all_to_all(copies, axis, split_axis=0, concat_axis=0, tiled=True)  130 us
    all_to_all x2, blocking collectives, copy_for_each(): return lax.all_to_all(copies, axis, split_axis=0, concat_axis=0, tiled=True)  25.3 us
    all_to_all x1, blocking collectives, sent_and_summed(): lax.all_to_all(tiles, axis, split_axis=0, concat_axis=0, tiled=True)  19 us
    all_to_all x3, starting transfers between devices, copy_for_each(): return lax.all_to_all(copies, axis, split_axis=0, concat_axis=0, tiled=True)  16.5 us
    all_to_all x1, waiting for transfers between devices, body(): lax.all_to_all(masked_trail, COL, split_axis=0, concat_axis=4, tiled=True)  12.3 us
    broadcast_in_dim x5, local copies, waits for them, and re-layouts, copy_for_each(): copies = jnp.broadcast_to(x, (lax.axis_size(axis), *x.shape))  5.19 us
    all_to_all x1, local copies, waits for them, and re-layouts, copy_for_each(): return lax.all_to_all(copies, axis, split_axis=0, concat_axis=0, tiled=True)  4.62 us
  transfers between devices with their start and end apart: 4, of which 4 were waited for; matrix products, arithmetic and copies ran while one was open for 3% of the time, Pallas kernels for 0%

commit v1 on v0

v1 whole, which is shorter than its diff:
```python
import jax
import jax.numpy as jnp
from jax import lax
from jax.sharding import Mesh
from jax.sharding import PartitionSpec as P

TB = 128
COL = ("x", "y", "core")
CHIP = ("x", "y")
ROWS = 8
CHIPS = 16
KH = 256
F32 = jnp.float32
BF16 = jnp.bfloat16


def exchange(x, axis):
    return lax.all_to_all(x, axis, split_axis=0, concat_axis=0, tiled=True)


def copies(x, axis, n):
    return exchange(jnp.broadcast_to(x, (n, *x.shape)), axis)


def partner(x):
    return lax.ppermute(x, "core", [(0, 1), (1, 0)])


def across(x):
    return lax.ppermute(x, CHIP, [(i, (i + 8) % CHIPS) for i in range(CHIPS)])


def dot_nt(a, b):
    return lax.dot_general(a, b, (((1,), (1,)), ((), ())), preferred_element_type=F32)


def natural(x, core):
    return jnp.where(core == 0, x, jnp.roll(x, TB, axis=1))


def body(rhs_super, factor_super, mask_super, dinv_rows, factor_trail, mask_trail, rhs_trail):
    core = lax.axis_index("core")
    chip = lax.axis_index(CHIP)
    dinv = dinv_rows[0, 0]

    rhs0 = rhs_super[0, :, 0].reshape(2 * TB, 512)
    rhs0_t = lax.dynamic_slice(rhs0, (0, core * KH), (2 * TB, KH)).T
    due0 = exchange(rhs0_t.reshape(ROWS, 32, 2 * TB), "row")
    due0 = due0.reshape(ROWS, 32, 2, TB).transpose(1, 2, 0, 3).reshape(32, 2048)
    dinv_other = partner(dinv)
    solved0 = jnp.concatenate([dot_nt(due0, dinv), dot_nt(due0, dinv_other)], 1).astype(BF16)
    solved0 = copies(solved0, "row", ROWS).reshape(KH, 2 * TB)

    keep = mask_super[1].astype(BF16).reshape(2, 1, 1)
    tiles10 = (factor_super[1].reshape(2, TB, TB) * keep).reshape(2 * TB, TB)
    tiles10 = jnp.concatenate([tiles10, partner(tiles10)], 1)
    reached = dot_nt(solved0, tiles10)
    reached = exchange(reached.reshape(CHIPS, 16, 2 * TB), CHIP)[:8].sum(0)
    rhs1 = rhs_super[1, :, 0].reshape(2 * TB, 512)
    rhs1_t = lax.dynamic_slice(rhs1, (0, core * KH + chip * 16), (2 * TB, 16)).T
    due1 = (rhs1_t.astype(F32) - reached).astype(BF16)

    row = lax.axis_index("row")
    d1 = lax.dynamic_index_in_dim(dinv.reshape(TB, 2, ROWS, TB), row, 2, False).reshape(TB, 2 * TB)
    d1_low = across(d1[TB // 2 :])
    d1_sent = jnp.where(chip >= 8, d1[: TB // 2], d1_low)
    d1_all = copies(d1_sent, CHIP, CHIPS)
    d1_own = jnp.concatenate([d1_all[8:], d1_all[:8]], 1).reshape(8 * TB, 2 * TB)
    d1_other = partner(d1_own)
    part = jnp.concatenate(
        [dot_nt(due1, d1_own).reshape(16, 8, TB), dot_nt(due1, d1_other).reshape(16, 8, TB)], 2
    ).transpose(1, 0, 2)
    solved1 = exchange(part, "row").sum(0).astype(BF16)
    solved1 = copies(natural(solved1, core), "row", ROWS)
    solved1 = solved1.transpose(1, 0, 2).reshape(16, 2048)
    solved1 = copies(solved1, CHIP, CHIPS).reshape(KH, 2048)

    keep_trail = mask_trail.astype(BF16).reshape(32, 1, 1)
    tiles = exchange(factor_trail.reshape(32, TB, TB) * keep_trail, COL)
    tiles0 = tiles[:16].reshape(8, 2, TB, TB).transpose(2, 1, 0, 3).reshape(TB, 2048)
    tiles1 = tiles[16:].transpose(1, 0, 2).reshape(TB, 2048)
    tiles0 = jnp.concatenate([tiles0, partner(tiles0)], 0)
    tiles1 = jnp.concatenate([tiles1, partner(tiles1)], 0)
    solved0 = natural(solved0, core)
    sent0 = jnp.where(chip < 8, solved0[:, :TB], across(solved0[:, TB:]))
    all0 = copies(sent0, CHIP, CHIPS).transpose(1, 0, 2).reshape(KH, 2048)
    total = dot_nt(tiles0, all0) + dot_nt(tiles1, solved1)
    given = rhs_trail.reshape(TB, 512)
    mine = lax.dynamic_slice(given, (0, core * KH), (TB, KH))
    theirs = partner(lax.dynamic_slice(given, (0, (1 - core) * KH), (TB, KH)))
    left = (jnp.concatenate([mine, theirs], 0).astype(F32) - total).astype(BF16)
    mine, theirs = left[:TB], partner(left[TB:])
    remaining = jnp.where(
        core == 0, jnp.concatenate([mine, theirs], 1), jnp.concatenate([theirs, mine], 1)
    )

    pair1 = lax.dynamic_slice(solved1, (0, jnp.maximum(chip - 8, 0) * 2 * TB), (KH, 2 * TB))
    pair = jnp.where(chip < 8, solved0, pair1)
    mine = lax.dynamic_slice(pair, (0, core * TB), (KH, TB))
    theirs = partner(lax.dynamic_slice(pair, (0, (1 - core) * TB), (KH, TB)))
    solved = jnp.where(
        core == 0, jnp.concatenate([mine, theirs], 0), jnp.concatenate([theirs, mine], 0)
    ).T
    return solved.reshape(1, 1, TB, 512), remaining.reshape(rhs_trail.shape)


def solution(mesh):
    torus = Mesh(mesh.devices.reshape(mesh.shape["row"], 4, 4, 2), ("row", *COL))
    placed = (
        P(None, None, "row", None, None),
        P(None, None, "row", None, None, COL, None),
        P(None, None, "row", None, COL),
        P(None, COL, None, None),
        P(None, "row", None, None, COL, None),
        P(None, "row", None, COL),
        P(COL, None, "row", None, None),
    )
    return jax.shard_map(
        body,
        mesh=torus,
        in_specs=placed,
        out_specs=(P(None, COL, None, None), P(COL, None, "row", None, None)),
        check_vma=False,
    )
```

time: 227 us -> 160 us (0.70)
  waiting for transfers between devices: 142 us -> 70.6 us
  starting transfers between devices: 20.8 us -> 61.1 us
  blocking collectives: 44.3 us -> 9.6 us
  local copies, waits for them, and re-layouts: 13 us -> 9.3 us
    all_to_all x4 -> x8, waiting for transfers between devices: 142 us -> 56.9 us  [exchange(): return lax.all_to_all(x, axis, split_axis=0, concat_axis=0, tiled=True)]
    all_to_all x3 -> x1, blocking collectives: 44.3 us -> 9.6 us  [exchange(): return lax.all_to_all(x, axis, split_axis=0, concat_axis=0, tiled=True)]
    all_to_all x4 -> x8, starting transfers between devices: 20.8 us -> 43.8 us  [exchange(): return lax.all_to_all(x, axis, split_axis=0, concat_axis=0, tiled=True)]
    ppermute x0 -> x10, starting transfers between devices: none -> 17.3 us  [the longest x8 10.6 us: partner(): return lax.ppermute(x, 'core', [(0, 1), (1, 0)])]
    ppermute x0 -> x10, waiting for transfers between devices: none -> 13.6 us  [the longest x2 13.2 us: across(): return lax.ppermute(x, CHIP, [(i, (i + 8) % CHIPS) for i in range(CHIPS)])]
    all_to_all x1 -> x0, local copies, waits for them, and re-layouts: 4.62 us -> none  [copy_for_each(): return lax.all_to_all(copies, axis, split_axis=0, concat_axis=0, tiled=True)]
    dot_general x3 -> x7, matrix products: 4.31 us -> 5.17 us  [dot_nt(): lax.dot_general(a, b, (((1,), (1,)), ((), ())), preferred_element_type=F32)]
  transfers between devices with their start and end apart: 4 -> 18, of which waited for: 4 -> 11; matrix products, arithmetic and copies ran while one was open for 3% -> 6% of each run, Pallas kernels for 0% -> 0%
where the time goes in v1:
time: 160 us; the launch traced here: 159 us
  waiting for transfers between devices  70.6 us (44%)
  starting transfers between devices  61.1 us (38%)
  blocking collectives  9.6 us (6%)
  local copies, waits for them, and re-layouts  9.3 us (6%)
  matrix products  5.17 us (3%)
  other arithmetic  2.16 us (1%)
    all_to_all x8, waiting for transfers between devices, exchange(): return lax.all_to_all(x, axis, split_axis=0, concat_axis=0, tiled=True)  56.9 us
    all_to_all x8, starting transfers between devices, exchange(): return lax.all_to_all(x, axis, split_axis=0, concat_axis=0, tiled=True)  43.8 us
    ppermute x2, waiting for transfers between devices, across(): return lax.ppermute(x, CHIP, [(i, (i + 8) % CHIPS) for i in range(CHIPS)])  13.2 us
    ppermute x8, starting transfers between devices, partner(): return lax.ppermute(x, 'core', [(0, 1), (1, 0)])  10.6 us
    all_to_all x1, blocking collectives, exchange(): return lax.all_to_all(x, axis, split_axis=0, concat_axis=0, tiled=True)  9.6 us
    ppermute x2, starting transfers between devices, across(): return lax.ppermute(x, CHIP, [(i, (i + 8) % CHIPS) for i in range(CHIPS)])  6.69 us
    dot_general x7, matrix products, dot_nt(): lax.dot_general(a, b, (((1,), (1,)), ((), ())), preferred_element_type=F32)  5.17 us
    broadcast_in_dim x5, local copies, waits for them, and re-layouts, copies(): return exchange(jnp.broadcast_to(x, (n, *x.shape)), axis)  3.71 us
  transfers between devices with their start and end apart: 18, of which 11 were waited for; matrix products, arithmetic and copies ran while one was open for 6% of the time, Pallas kernels for 0%

profile of v1, /device:TPU:1, one launch (start us, length us, event | category | flops | bytes accessed | tf_op | source)
XLA Modules:
  0.0 159.0 jit_solution(332892716022509370)
XLA Ops:
  0.7 1.2 copy.72
  2.4 3.6 %collective-permute-start.2 = (bf16[64,256]{1,0:T(8,128)(2,1)S(1)}, bf16[64,256]{1,0:T(8,128)(2,1)S(1)}, u32[]{:S(2)}, u32[]{:S(2)}) collective-permute-start(bf16[64,256]{1,0:T(8,128)(2,1)S(1)} %bitcast.117), channel_id=1, source_target_pairs={{0,16},{2,18},{4,20},{6,22},{8,24},{10,26},{12,28},{14,30},{16,0},... | collective-permute-start | bytes 98312 | tf_op jit(solution)/shard_map/ppermute | solution.py:30
  7.8 8.2 %all-to-all-start = ((bf16[8,32,256]{2,1,0:T(8,128)(2,1)}), bf16[8,32,256]{2,1,0:T(8,128)(2,1)S(1)}, u32[]{:S(2)}, u32[]{:S(2)}) async-start(bf16[8,32,256]{2,1,0:T(8,128)(2,1)} %bitcast.2), calls=%async_computation | async-start | bytes 262144 | tf_op jit(solution)/shard_map/all_to_all | solution.py:18
  16.6 7.9 %all-to-all-done = bf16[8,32,256]{2,1,0:T(8,128)(2,1)S(1)} async-done(((bf16[8,32,256]{2,1,0:T(8,128)(2,1)}), bf16[8,32,256]{2,1,0:T(8,128)(2,1)S(1)}, u32[]{:S(2)}, u32[]{:S(2)}) %all-to-all-start) | async-done | bytes 131104 | tf_op jit(solution)/shard_map/all_to_all | solution.py:18
  25.3 4.9 %all-to-all-start.3 = ((bf16[16,64,256]{2,1,0:T(8,128)(2,1)}), bf16[16,64,256]{2,1,0:T(8,128)(2,1)S(1)}, u32[]{:S(2)}, u32[]{:S(2)}) async-start(bf16[16,64,256]{2,1,0:T(8,128)(2,1)} %broadcast_in_dim.16), calls=%async_computation.3 | async-start | bytes 1048576 | tf_op jit(solution)/shard_map/all_to_all | solution.py:18
  31.0 8.4 %all-to-all-done.3 = bf16[16,64,256]{2,1,0:T(8,128)(2,1)S(1)} async-done(((bf16[16,64,256]{2,1,0:T(8,128)(2,1)}), bf16[16,64,256]{2,1,0:T(8,128)(2,1)S(1)}, u32[]{:S(2)}, u32[]{:S(2)}) %all-to-all-start.3) | async-done | bytes 524320 | tf_op jit(solution)/shard_map/all_to_all | solution.py:18
  40.1 3.4 %all-to-all-start.1 = ((bf16[8,32,256]{2,1,0:T(8,128)(2,1)}), bf16[8,32,256]{2,1,0:T(8,128)(2,1)S(1)}, u32[]{:S(2)}, u32[]{:S(2)}) async-start(bf16[8,32,256]{2,1,0:T(8,128)(2,1)} %broadcast_in_dim.15), calls=%async_computation.1 | async-start | bytes 262144 | tf_op jit(solution)/shard_map/all_to_all | solution.py:18
  43.5 7.9 %all-to-all-done.1 = bf16[8,32,256]{2,1,0:T(8,128)(2,1)S(1)} async-done(((bf16[8,32,256]{2,1,0:T(8,128)(2,1)}), bf16[8,32,256]{2,1,0:T(8,128)(2,1)S(1)}, u32[]{:S(2)}, u32[]{:S(2)}) %all-to-all-start.1) | async-done | bytes 131104 | tf_op jit(solution)/shard_map/all_to_all | solution.py:18
  52.3 3.6 %all-to-all-start.2 = ((f32[16,16,256]{2,1,0:T(8,128)}), f32[16,16,256]{2,1,0:T(8,128)S(1)}, u32[]{:S(2)}, u32[]{:S(2)}) async-start(f32[16,16,256]{2,1,0:T(8,128)} %fusion.9), calls=%async_computation.2 | async-start | bytes 524288 | tf_op jit(solution)/shard_map/all_to_all | solution.py:18
  56.0 4.3 %collective-permute-start.3 = (bf16[1024,256]{1,0:T(8,128)(2,1)S(1)}, bf16[1024,256]{1,0:T(8,128)(2,1)S(1)}, u32[]{:S(2)}, u32[]{:S(2)}) collective-permute-start(bf16[1024,256]{1,0:T(8,128)(2,1)S(1)} %bitcast.107), channel_id=1, source_target_pairs={{0,1},{1,0},{2,3},{3,2},{4,5},{5,4},{6,7},{7,6},{8,9},{9,8},{10,11... | collective-permute-start | bytes 1572872 | tf_op jit(solution)/shard_map/ppermute | solution.py:26
  60.4 2.8 %all-to-all-done.2 = f32[16,16,256]{2,1,0:T(8,128)S(1)} async-done(((f32[16,16,256]{2,1,0:T(8,128)}), f32[16,16,256]{2,1,0:T(8,128)S(1)}, u32[]{:S(2)}, u32[]{:S(2)}) %all-to-all-start.2) | async-done | bytes 262176 | tf_op jit(solution)/shard_map/all_to_all | solution.py:18
  64.5 3.4 %all-to-all-start.4 = ((f32[8,16,256]{2,1,0:T(8,128)}), f32[8,16,256]{2,1,0:T(8,128)S(1)}, u32[]{:S(2)}, u32[]{:S(2)}) async-start(f32[8,16,256]{2,1,0:T(8,128)} %maximum_bitcast_fusion.2), calls=%async_computation.4 | async-start | bytes 262144 | tf_op jit(solution)/shard_map/all_to_all | solution.py:18
  67.8 7.8 %all-to-all-done.4 = f32[8,16,256]{2,1,0:T(8,128)S(1)} async-done(((f32[8,16,256]{2,1,0:T(8,128)}), f32[8,16,256]{2,1,0:T(8,128)S(1)}, u32[]{:S(2)}, u32[]{:S(2)}) %all-to-all-start.4) | async-done | bytes 131104 | tf_op jit(solution)/shard_map/all_to_all | solution.py:18
  75.7 9.6 %all_to_all.45 = bf16[8,16,256]{2,1,0:T(8,128)(2,1)S(1)} all-to-all(bf16[8,16,256]{2,1,0:T(8,128)(2,1)S(1)} %broadcast_in_dim.17), channel_id=1, replica_groups=mesh['row'=8,'x'=4,'y'=4,'core'=2] {'row'}, dimensions={0} | all-to-all | bytes 131072 | tf_op jit(solution)/shard_map/all_to_all | solution.py:18
  86.4 5.3 %all-to-all-start.6 = ((bf16[16,16,2048]{2,1,0:T(8,128)(2,1)}), bf16[16,16,2048]{2,1,0:T(8,128)(2,1)S(1)}, u32[]{:S(2)}, u32[]{:S(2)}) async-start(bf16[16,16,2048]{2,1,0:T(8,128)(2,1)} %broadcast_in_dim.18), calls=%async_computation.6 | async-start | bytes 2097152 | tf_op jit(solution)/shard_map/all_to_all | solution.py:18
  92.9 10.7 %all-to-all-done.6 = bf16[16,16,2048]{2,1,0:T(8,128)(2,1)S(1)} async-done(((bf16[16,16,2048]{2,1,0:T(8,128)(2,1)}), bf16[16,16,2048]{2,1,0:T(8,128)(2,1)S(1)}, u32[]{:S(2)}, u32[]{:S(2)}) %all-to-all-start.6) | async-done | bytes 1048608 | tf_op jit(solution)/shard_map/all_to_all | solution.py:18
  103.6 10.8 %all-to-all-start.7 = ((bf16[32,128,128]{2,1,0:T(8,128)(2,1)}), bf16[32,128,128]{2,1,0:T(8,128)(2,1)S(1)}, u32[]{:S(2)}, u32[]{:S(2)}) async-start(bf16[32,128,128]{2,1,0:T(8,128)(2,1)} %bitcast_multiply_fusion), calls=%async_computation.7 | async-start | bytes 2097152 | tf_op jit(solution)/shard_map/all_to_all | solution.py:18
  114.5 3.0 %collective-permute-start.7 = (bf16[256,128]{1,0:T(8,128)(2,1)S(1)}, bf16[256,128]{1,0:T(8,128)(2,1)S(1)}, u32[]{:S(2)}, u32[]{:S(2)}) collective-permute-start(bf16[256,128]{1,0:T(8,128)(2,1)S(1)} %slice.99), channel_id=1, source_target_pairs={{0,16},{2,18},{4,20},{6,22},{8,24},{10,26},{12,28},{14,30},{16,0},... | collective-permute-start | bytes 196616 | tf_op jit(solution)/shard_map/ppermute | solution.py:30
  117.5 13.2 %collective-permute-done.7 = bf16[256,128]{1,0:T(8,128)(2,1)S(1)} collective-permute-done((bf16[256,128]{1,0:T(8,128)(2,1)S(1)}, bf16[256,128]{1,0:T(8,128)(2,1)S(1)}, u32[]{:S(2)}, u32[]{:S(2)}) %collective-permute-start.7) | collective-permute-done | bytes 65568 | tf_op jit(solution)/shard_map/ppermute | solution.py:30
  132.5 4.4 %all-to-all-start.8 = ((bf16[16,256,128]{1,2,0:T(8,128)(2,1)}), bf16[16,256,128]{1,2,0:T(8,128)(2,1)}, u32[]{:S(2)}, u32[]{:S(2)}) async-start(bf16[16,256,128]{1,2,0:T(8,128)(2,1)} %broadcast_in_dim.19), calls=%async_computation.8 | async-start | bytes 2097152 | tf_op jit(solution)/shard_map/all_to_all | solution.py:18
  140.1 1.5 fusion.3
  141.6 10.9 %all-to-all-done.8 = bf16[16,256,128]{1,2,0:T(8,128)(2,1)} async-done(((bf16[16,256,128]{1,2,0:T(8,128)(2,1)}), bf16[16,256,128]{1,2,0:T(8,128)(2,1)}, u32[]{:S(2)}, u32[]{:S(2)}) %all-to-all-start.8) | async-done | bytes 1048608 | tf_op jit(solution)/shard_map/all_to_all | solution.py:18
  152.5 1.7 %subtract_convert_fusion = bf16[256,256]{0,1:T(8,128)(2,1)S(1)} fusion(bf16[128,256]{0,1:T(8,128)(2,1)S(1)} %collective-permute-done.5, bf16[128,256]{0,1:T(8,128)(2,1)S(1)} %bitcast.115, f32[256,256]{0,1:T(8,128)S(1)} %fusion.3, bf16[256,2048]{0,1:T(8,128)(2,1)} %bitcast.28, bf16[128,2048]{0,1:T(8,128)(2,1)S(1)} %collective-permute-done.6, ...), kind=kOutput, calls=%fused_computation.14 | convolution fusion | flops 270991360 | bytes 2621440 | tf_op jit(solution)/shard_map/dot_general | solution.py:34
  154.2 3.0 %collective-permute-start.9 = (bf16[128,256]{0,1:T(8,128)(2,1)S(1)}, bf16[128,256]{0,1:T(8,128)(2,1)S(1)}, u32[]{:S(2)}, u32[]{:S(2)}) collective-permute-start(bf16[128,256]{0,1:T(8,128)(2,1)S(1)} %get-tuple-element.23), channel_id=1, source_target_pairs={{0,1},{1,0},{2,3},{3,2},{4,5},{5,4},{6,7},{7,6},{8,9},{9,8},{10,11... | collective-permute-start | bytes 196616 | tf_op jit(solution)/shard_map/ppermute | solution.py:26
  (82 shorter events, 16.4 us)
Async XLA Ops:
  0.6 5.4 %copy-start = (bf16[1,1,128,2048]{3,2,1,0:T(8,128)(2,1)S(1)}, bf16[1,1,128,2048]{3,2,1,0:T(8,128)(2,1)}, u32[]{:S(2)}) copy-start(bf16[1,1,128,2048]{3,2,1,0:T(8,128)(2,1)} %param.10) | copy-start | bytes 1572868
  0.6 6.4 %copy-start.2 = (bf16[2,2,1,128,512]{4,3,2,1,0:T(8,128)(2,1)S(1)}, bf16[2,2,1,128,512]{4,3,2,1,0:T(8,128)(2,1)}, u32[]{:S(2)}) copy-start(bf16[2,2,1,128,512]{4,3,2,1,0:T(8,128)(2,1)} %param.7) | copy-start | bytes 1572868
  2.3 13.7 %copy-start.4 = (s32[2,2,1,1,1]{1,4,3,2,0:T(1,128)S(1)}, s32[2,2,1,1,1]{1,4,3,2,0:T(1,128)}, u32[]{:S(2)}) copy-start(s32[2,2,1,1,1]{1,4,3,2,0:T(1,128)} %param.9) | copy-start | bytes 52
  2.4 13.7 %slice-start = ((bf16[2,2,1,128,1,1,128]{6,3,5,4,2,1,0:T(8,128)(2,1)}), bf16[1,2,1,128,1,1,128]{6,3,5,4,2,1,0:T(8,128)(2,1)S(1)}, s32[]{:S(2)}) async-start(bf16[2,2,1,128,1,1,128]{6,3,5,4,2,1,0:T(8,128)(2,1)} %param.8), calls=%async_computation.9 | async-start | bytes 131072 | tf_op jit(solution)/shard_map/slice | solution.py:55
  2.4 14.2 %collective-permute-start.2 = (bf16[64,256]{1,0:T(8,128)(2,1)S(1)}, bf16[64,256]{1,0:T(8,128)(2,1)S(1)}, u32[]{:S(2)}, u32[]{:S(2)}) collective-permute-start(bf16[64,256]{1,0:T(8,128)(2,1)S(1)} %bitcast.117), channel_id=1, source_target_pairs={{0,16},{2,18},{4,20},{6,22},{8,24},{10,26},{12,28},{14,30},{16,0},... | collective-permute-start | bytes 98312 | tf_op jit(solution)/shard_map/ppermute | solution.py:30
  6.0 24.7 %collective-permute-start = (bf16[128,2048]{1,0:T(8,128)(2,1)S(1)}, bf16[128,2048]{1,0:T(8,128)(2,1)S(1)}, u32[]{:S(2)}, u32[]{:S(2)}) collective-permute-start(bf16[128,2048]{1,0:T(8,128)(2,1)S(1)} %bitcast.93), channel_id=1, source_target_pairs={{0,1},{1,0},{2,3},{3,2},{4,5},{5,4},{6,7},{7,6},{8,9},{9,8},{10,11... | collective-permute-start | bytes 1572872 | tf_op jit(solution)/shard_map/ppermute | solution.py:26
  7.8 16.7 %all-to-all-start = ((bf16[8,32,256]{2,1,0:T(8,128)(2,1)}), bf16[8,32,256]{2,1,0:T(8,128)(2,1)S(1)}, u32[]{:S(2)}, u32[]{:S(2)}) async-start(bf16[8,32,256]{2,1,0:T(8,128)(2,1)} %bitcast.2), calls=%async_computation | async-start | bytes 262144 | tf_op jit(solution)/shard_map/all_to_all | solution.py:18
  16.2 27.3 %collective-permute-start.1 = (bf16[256,128]{1,0:T(8,128)(2,1)S(1)}, bf16[256,128]{1,0:T(8,128)(2,1)S(1)}, u32[]{:S(2)}, u32[]{:S(2)}) collective-permute-start(bf16[256,128]{1,0:T(8,128)(2,1)S(1)} %bitcast_multiply_fusion.1), channel_id=1, source_target_pairs={{0,1},{1,0},{2,3},{3,2},{4,5},{5,4},{6,7},{7,6},{8,9},{9,8},{10,11... | collective-permute-start | bytes 196616 | tf_op jit(solution)/shard_map/ppermute | solution.py:26
  25.3 14.1 %all-to-all-start.3 = ((bf16[16,64,256]{2,1,0:T(8,128)(2,1)}), bf16[16,64,256]{2,1,0:T(8,128)(2,1)S(1)}, u32[]{:S(2)}, u32[]{:S(2)}) async-start(bf16[16,64,256]{2,1,0:T(8,128)(2,1)} %broadcast_in_dim.16), calls=%async_computation.3 | async-start | bytes 1048576 | tf_op jit(solution)/shard_map/all_to_all | solution.py:18
  40.1 11.3 %all-to-all-start.1 = ((bf16[8,32,256]{2,1,0:T(8,128)(2,1)}), bf16[8,32,256]{2,1,0:T(8,128)(2,1)S(1)}, u32[]{:S(2)}, u32[]{:S(2)}) async-start(bf16[8,32,256]{2,1,0:T(8,128)(2,1)} %broadcast_in_dim.15), calls=%async_computation.1 | async-start | bytes 262144 | tf_op jit(solution)/shard_map/all_to_all | solution.py:18
  52.3 10.9 %all-to-all-start.2 = ((f32[16,16,256]{2,1,0:T(8,128)}), f32[16,16,256]{2,1,0:T(8,128)S(1)}, u32[]{:S(2)}, u32[]{:S(2)}) async-start(f32[16,16,256]{2,1,0:T(8,128)} %fusion.9), calls=%async_computation.2 | async-start | bytes 524288 | tf_op jit(solution)/shard_map/all_to_all | solution.py:18
  56.0 7.5 %collective-permute-start.3 = (bf16[1024,256]{1,0:T(8,128)(2,1)S(1)}, bf16[1024,256]{1,0:T(8,128)(2,1)S(1)}, u32[]{:S(2)}, u32[]{:S(2)}) collective-permute-start(bf16[1024,256]{1,0:T(8,128)(2,1)S(1)} %bitcast.107), channel_id=1, source_target_pairs={{0,1},{1,0},{2,3},{3,2},{4,5},{5,4},{6,7},{7,6},{8,9},{9,8},{10,11... | collective-permute-start | bytes 1572872 | tf_op jit(solution)/shard_map/ppermute | solution.py:26
  64.5 11.2 %all-to-all-start.4 = ((f32[8,16,256]{2,1,0:T(8,128)}), f32[8,16,256]{2,1,0:T(8,128)S(1)}, u32[]{:S(2)}, u32[]{:S(2)}) async-start(f32[8,16,256]{2,1,0:T(8,128)} %maximum_bitcast_fusion.2), calls=%async_computation.4 | async-start | bytes 262144 | tf_op jit(solution)/shard_map/all_to_all | solution.py:18
  86.4 5.3 %copy-start.5 = (s32[32,1,1,1]{0,3,2,1:T(1,128)S(1)}, s32[32,1,1,1]{0,3,2,1:T(1,128)}, u32[]{:S(2)}) copy-start(s32[32,1,1,1]{0,3,2,1:T(1,128)} %param.12) | copy-start | bytes 388
  86.4 5.3 %copy-start.1 = (bf16[32,1,128,1,1,128]{5,2,4,3,1,0:T(8,128)(2,1)S(1)}, bf16[32,1,128,1,1,128]{5,2,4,3,1,0:T(8,128)(2,1)}, u32[]{:S(2)}) copy-start(bf16[32,1,128,1,1,128]{5,2,4,3,1,0:T(8,128)(2,1)} %param.11) | copy-start | bytes 3145732
  86.4 17.1 %all-to-all-start.6 = ((bf16[16,16,2048]{2,1,0:T(8,128)(2,1)}), bf16[16,16,2048]{2,1,0:T(8,128)(2,1)S(1)}, u32[]{:S(2)}, u32[]{:S(2)}) async-start(bf16[16,16,2048]{2,1,0:T(8,128)(2,1)} %broadcast_in_dim.18), calls=%async_computation.6 | async-start | bytes 2097152 | tf_op jit(solution)/shard_map/all_to_all | solution.py:18
  103.6 27.8 %all-to-all-start.7 = ((bf16[32,128,128]{2,1,0:T(8,128)(2,1)}), bf16[32,128,128]{2,1,0:T(8,128)(2,1)S(1)}, u32[]{:S(2)}, u32[]{:S(2)}) async-start(bf16[32,128,128]{2,1,0:T(8,128)(2,1)} %bitcast_multiply_fusion), calls=%async_computation.7 | async-start | bytes 2097152 | tf_op jit(solution)/shard_map/all_to_all | solution.py:18
  114.5 16.2 %collective-permute-start.7 = (bf16[256,128]{1,0:T(8,128)(2,1)S(1)}, bf16[256,128]{1,0:T(8,128)(2,1)S(1)}, u32[]{:S(2)}, u32[]{:S(2)}) collective-permute-start(bf16[256,128]{1,0:T(8,128)(2,1)S(1)} %slice.99), channel_id=1, source_target_pairs={{0,16},{2,18},{4,20},{6,22},{8,24},{10,26},{12,28},{14,30},{16,0},... | collective-permute-start | bytes 196616 | tf_op jit(solution)/shard_map/ppermute | solution.py:30
  132.5 20.0 %all-to-all-start.8 = ((bf16[16,256,128]{1,2,0:T(8,128)(2,1)}), bf16[16,256,128]{1,2,0:T(8,128)(2,1)}, u32[]{:S(2)}, u32[]{:S(2)}) async-start(bf16[16,256,128]{1,2,0:T(8,128)(2,1)} %broadcast_in_dim.19), calls=%async_computation.8 | async-start | bytes 2097152 | tf_op jit(solution)/shard_map/all_to_all | solution.py:18
  137.2 2.8 %collective-permute-start.8 = (bf16[128,2048]{0,1:T(8,128)(2,1)S(1)}, bf16[128,2048]{0,1:T(8,128)(2,1)}, u32[]{:S(2)}, u32[]{:S(2)}) collective-permute-start(bf16[128,2048]{0,1:T(8,128)(2,1)S(1)} %bitcast.105), channel_id=1, source_target_pairs={{0,1},{1,0},{2,3},{3,2},{4,5},{5,4},{6,7},{7,6},{8,9},{9,8},{10,11... | collective-permute-start | bytes 1572872 | tf_op jit(solution)/shard_map/ppermute | solution.py:26
  138.7 2.9 %collective-permute-start.6 = (bf16[128,2048]{0,1:T(8,128)(2,1)S(1)}, bf16[128,2048]{0,1:T(8,128)(2,1)S(1)}, u32[]{:S(2)}, u32[]{:S(2)}) collective-permute-start(bf16[128,2048]{0,1:T(8,128)(2,1)S(1)} %bitcast.103), channel_id=1, source_target_pairs={{0,1},{1,0},{2,3},{3,2},{4,5},{5,4},{6,7},{7,6},{8,9},{9,8},{10,11... | collective-permute-start | bytes 1572872 | tf_op jit(solution)/shard_map/ppermute | solution.py:26
  138.9 2.6 %collective-permute-start.5 = (bf16[128,256]{0,1:T(8,128)(2,1)S(1)}, bf16[128,256]{0,1:T(8,128)(2,1)S(1)}, u32[]{:S(2)}, u32[]{:S(2)}) collective-permute-start(bf16[128,256]{0,1:T(8,128)(2,1)S(1)} %bitcast.114), channel_id=1, source_target_pairs={{0,1},{1,0},{2,3},{3,2},{4,5},{5,4},{6,7},{7,6},{8,9},{9,8},{10,11... | collective-permute-start | bytes 196616 | tf_op jit(solution)/shard_map/ppermute | solution.py:26
  139.6 17.6 %collective-permute-start.4 = (bf16[256,128]{1,0:T(8,128)(2,1)S(1)}, bf16[256,128]{1,0:T(8,128)(2,1)S(1)}, u32[]{:S(2)}, u32[]{:S(2)}) collective-permute-start(bf16[256,128]{1,0:T(8,128)(2,1)S(1)} %get-tuple-element.27), channel_id=1, source_target_pairs={{0,1},{1,0},{2,3},{3,2},{4,5},{5,4},{6,7},{7,6},{8,9},{9,8},{10,11... | collective-permute-start | bytes 196616 | tf_op jit(solution)/shard_map/ppermute | solution.py:26
  154.2 3.9 %collective-permute-start.9 = (bf16[128,256]{0,1:T(8,128)(2,1)S(1)}, bf16[128,256]{0,1:T(8,128)(2,1)S(1)}, u32[]{:S(2)}, u32[]{:S(2)}) collective-permute-start(bf16[128,256]{0,1:T(8,128)(2,1)S(1)} %get-tuple-element.23), channel_id=1, source_target_pairs={{0,1},{1,0},{2,3},{3,2},{4,5},{5,4},{6,7},{7,6},{8,9},{9,8},{10,11... | collective-permute-start | bytes 196616 | tf_op jit(solution)/shard_map/ppermute | solution.py:26
  (1 other events, 1.9 us)

commit v2 on v1

--- a/solution.py
+++ b/solution.py
@@ -26,8 +26,8 @@
     return lax.ppermute(x, "core", [(0, 1), (1, 0)])
 
 
-def across(x):
-    return lax.ppermute(x, CHIP, [(i, (i + 8) % CHIPS) for i in range(CHIPS)])
+def shifted(x, axis, step, sources):
+    return lax.ppermute(x, axis, [(i, (i + step) % 4) for i in sources])
 
 
 def dot_nt(a, b):
@@ -38,16 +38,58 @@
     return jnp.where(core == 0, x, jnp.roll(x, TB, axis=1))
 
 
-def body(rhs_super, factor_super, mask_super, dinv_rows, factor_trail, mask_trail, rhs_trail):
+def placed_at(parts, slots):
+    whole = jnp.zeros((len(parts), *parts[0].shape), parts[0].dtype)
+    for part, slot in zip(parts, slots):
+        whole = lax.dynamic_update_index_in_dim(whole, part, slot, 0)
+    return whole
+
+
+def gathered_in_plane(x, here_x, here_y, first):
+    sources = (first, first + 1)
+    arrived = [x] + [shifted(x, "x", d, sources) for d in (1, 2, 3)]
+    stacked = jnp.stack(arrived)
+    pair = jnp.stack(
+        [
+            lax.dynamic_index_in_dim(stacked, (here_x - s) % 4, 0, keepdims=False)
+            for s in sources
+        ]
+    )
+    along = [pair] + [shifted(pair, "y", d, range(4)) for d in (1, 2, 3)]
+    return placed_at(along, [(here_y - d) % 4 for d in range(4)])
+
+
+def tiles_of_rows(tiles, here_x, here_y):
+    by_x = tiles.reshape(4, 8, TB, TB)
+    sent = [lax.dynamic_index_in_dim(by_x, (here_x + d) % 4, 0, keepdims=False) for d in range(4)]
+    came = [sent[0]] + [shifted(sent[d], "x", d, range(4)) for d in (1, 2, 3)]
+    by_y = placed_at(came, [(here_x - d) % 4 for d in range(4)]).reshape(4, 4, 2, TB, TB)
+    sent = [lax.dynamic_index_in_dim(by_y, (here_y + d) % 4, 1, keepdims=False) for d in range(4)]
+    came = [sent[0]] + [shifted(sent[d], "y", d, range(4)) for d in (1, 2, 3)]
+    return placed_at(came, [(here_y - d) % 4 for d in range(4)])
+
+
+def steps(rhs_super, factor_super, mask_super, dinv_rows, factor_trail, mask_trail, rhs_trail):
     core = lax.axis_index("core")
+    here_x = lax.axis_index("x")
+    here_y = lax.axis_index("y")
     chip = lax.axis_index(CHIP)
-    dinv = dinv_rows[0, 0]
+    row = lax.axis_index("row")
 
     rhs0 = rhs_super[0, :, 0].reshape(2 * TB, 512)
     rhs0_t = lax.dynamic_slice(rhs0, (0, core * KH), (2 * TB, KH)).T
+    rhs0_t, dinv, factor_trail = lax.optimization_barrier((rhs0_t, dinv_rows[0, 0], factor_trail))
     due0 = exchange(rhs0_t.reshape(ROWS, 32, 2 * TB), "row")
     due0 = due0.reshape(ROWS, 32, 2, TB).transpose(1, 2, 0, 3).reshape(32, 2048)
     dinv_other = partner(dinv)
+
+    keep_trail = mask_trail.astype(BF16).reshape(32, 1, 1)
+    tiles = tiles_of_rows(factor_trail.reshape(32, TB, TB) * keep_trail, here_x, here_y)
+    d1 = lax.dynamic_index_in_dim(dinv.reshape(TB, 2, ROWS, TB), row, 2, False).reshape(TB, 2 * TB)
+    d1_own = gathered_in_plane(d1, here_x, here_y, 2)
+    d1_own = d1_own.transpose(1, 0, 2, 3).reshape(8 * TB, 2 * TB)
+    d1_other = partner(d1_own)
+
     solved0 = jnp.concatenate([dot_nt(due0, dinv), dot_nt(due0, dinv_other)], 1).astype(BF16)
     solved0 = copies(solved0, "row", ROWS).reshape(KH, 2 * TB)
 
@@ -60,13 +102,6 @@
     rhs1_t = lax.dynamic_slice(rhs1, (0, core * KH + chip * 16), (2 * TB, 16)).T
     due1 = (rhs1_t.astype(F32) - reached).astype(BF16)
 
-    row = lax.axis_index("row")
-    d1 = lax.dynamic_index_in_dim(dinv.reshape(TB, 2, ROWS, TB), row, 2, False).reshape(TB, 2 * TB)
-    d1_low = across(d1[TB // 2 :])
-    d1_sent = jnp.where(chip >= 8, d1[: TB // 2], d1_low)
-    d1_all = copies(d1_sent, CHIP, CHIPS)
-    d1_own = jnp.concatenate([d1_all[8:], d1_all[:8]], 1).reshape(8 * TB, 2 * TB)
-    d1_other = partner(d1_own)
     part = jnp.concatenate(
         [dot_nt(due1, d1_own).reshape(16, 8, TB), dot_nt(due1, d1_other).reshape(16, 8, TB)], 2
     ).transpose(1, 0, 2)
@@ -75,21 +110,21 @@
     solved1 = solved1.transpose(1, 0, 2).reshape(16, 2048)
     solved1 = copies(solved1, CHIP, CHIPS).reshape(KH, 2048)
 
-    keep_trail = mask_trail.astype(BF16).reshape(32, 1, 1)
-    tiles = exchange(factor_trail.reshape(32, TB, TB) * keep_trail, COL)
-    tiles0 = tiles[:16].reshape(8, 2, TB, TB).transpose(2, 1, 0, 3).reshape(TB, 2048)
-    tiles1 = tiles[16:].transpose(1, 0, 2).reshape(TB, 2048)
-    tiles0 = jnp.concatenate([tiles0, partner(tiles0)], 0)
-    tiles1 = jnp.concatenate([tiles1, partner(tiles1)], 0)
-    solved0 = natural(solved0, core)
-    sent0 = jnp.where(chip < 8, solved0[:, :TB], across(solved0[:, TB:]))
-    all0 = copies(sent0, CHIP, CHIPS).transpose(1, 0, 2).reshape(KH, 2048)
-    total = dot_nt(tiles0, all0) + dot_nt(tiles1, solved1)
+    both = jnp.where(
+        core == 0, jnp.stack([tiles, partner(tiles)]), jnp.stack([partner(tiles), tiles])
+    )
+    both = both.transpose(3, 4, 2, 1, 0, 5).reshape(2 * TB, 4096)
+    solved0 = lax.optimization_barrier(natural(solved0, core))
+    all0 = gathered_in_plane(solved0, here_x, here_y, 0)
+    all0 = all0.transpose(2, 1, 0, 3).reshape(KH, 2048)
+    early = lax.optimization_barrier(dot_nt(both[:, :2048], all0))
+    total = early + dot_nt(both[:, 2048:], solved1)
     given = rhs_trail.reshape(TB, 512)
     mine = lax.dynamic_slice(given, (0, core * KH), (TB, KH))
     theirs = partner(lax.dynamic_slice(given, (0, (1 - core) * KH), (TB, KH)))
-    left = (jnp.concatenate([mine, theirs], 0).astype(F32) - total).astype(BF16)
-    mine, theirs = left[:TB], partner(left[TB:])
+    mine = mine.astype(F32) - total_rows(total, core)
+    theirs = theirs.astype(F32) - total_rows(total, 1 - core)
+    mine, theirs = mine.astype(BF16), partner(theirs.astype(BF16))
     remaining = jnp.where(
         core == 0, jnp.concatenate([mine, theirs], 1), jnp.concatenate([theirs, mine], 1)
     )
@@ -104,6 +139,10 @@
     return solved.reshape(1, 1, TB, 512), remaining.reshape(rhs_trail.shape)
 
 
+def total_rows(total, which):
+    return lax.dynamic_slice(total, (which * TB, 0), (TB, KH))
+
+
 def solution(mesh):
     torus = Mesh(mesh.devices.reshape(mesh.shape["row"], 4, 4, 2), ("row", *COL))
     placed = (
@@ -116,7 +155,7 @@
         P(COL, None, "row", None, None),
     )
     return jax.shard_map(
-        body,
+        steps,
         mesh=torus,
         in_specs=placed,
         out_specs=(P(None, COL, None, None), P(COL, None, "row", None, None)),

time: 160 us -> 145 us (0.906)
  waiting for transfers between devices: 70.6 us -> 24.4 us
  local copies, waits for them, and re-layouts: 9.3 us -> 26.2 us
  starting transfers between devices: 61.1 us -> 77.6 us
  blocking collectives: 9.6 us -> 0 us
  matrix products: 5.17 us -> 8.56 us
  other arithmetic: 2.16 us -> 4.09 us
    all_to_all x8 -> x6, waiting for transfers between devices: 56.9 us -> 13.1 us  [exchange(): return lax.all_to_all(x, axis, split_axis=0, concat_axis=0, tiled=True)]
    ppermute x2 -> x18, starting transfers between devices: 6.69 us -> 31.2 us  [shifted(): return lax.ppermute(x, axis, [(i, (i + step) % 4) for i in sources])]
    all_to_all x8 -> x6, starting transfers between devices: 43.8 us -> 30.7 us  [exchange(): return lax.all_to_all(x, axis, split_axis=0, concat_axis=0, tiled=True)]
    all_to_all x1 -> x0, blocking collectives: 9.6 us -> none  [exchange(): return lax.all_to_all(x, axis, split_axis=0, concat_axis=0, tiled=True)]
    dynamic_update_slice x0 -> x15, local copies, waits for them, and re-layouts: none -> 7.52 us  [placed_at(): whole = lax.dynamic_update_index_in_dim(whole, part, slot, 0)]
    ppermute x8 -> x7, starting transfers between devices: 10.6 us -> 15.7 us  [partner(): return lax.ppermute(x, 'core', [(0, 1), (1, 0)])]
    dot_general x7, matrix products: 5.17 us -> 8.56 us  [dot_nt(): lax.dot_general(a, b, (((1,), (1,)), ((), ())), preferred_element_type=F32)]
    broadcast_in_dim x0 -> x9, local copies, waits for them, and re-layouts: none -> 3.13 us  [the longest x5 2.54 us: placed_at(): whole = lax.dynamic_update_index_in_dim(whole, part, slot, 0)]
  transfers between devices with their start and end apart: 18 -> 31, of which waited for: 11 -> 8; matrix products, arithmetic and copies ran while one was open for 6% -> 24% of each run, Pallas kernels for 0% -> 0%
where the time goes in v2:
time: 145 us; the launch traced here: 142 us
  starting transfers between devices  77.6 us (54%)
  local copies, waits for them, and re-layouts  26.2 us (18%)
  waiting for transfers between devices  24.4 us (17%)
  matrix products  8.56 us (6%)
  other arithmetic  4.09 us (3%)
  between operations  1.56 us (1%)
    ppermute x18, starting transfers between devices, shifted(): return lax.ppermute(x, axis, [(i, (i + step) % 4) for i in sources])  31.2 us
    all_to_all x6, starting transfers between devices, exchange(): return lax.all_to_all(x, axis, split_axis=0, concat_axis=0, tiled=True)  30.7 us
    ppermute x7, starting transfers between devices, partner(): return lax.ppermute(x, 'core', [(0, 1), (1, 0)])  15.7 us
    all_to_all x6, waiting for transfers between devices, exchange(): return lax.all_to_all(x, axis, split_axis=0, concat_axis=0, tiled=True)  13.1 us
    ppermute x18, waiting for transfers between devices, shifted(): return lax.ppermute(x, axis, [(i, (i + step) % 4) for i in sources])  11.2 us
    dot_general x7, matrix products, dot_nt(): lax.dot_general(a, b, (((1,), (1,)), ((), ())), preferred_element_type=F32)  8.56 us
    dynamic_update_slice x15, local copies, waits for them, and re-layouts, placed_at(): whole = lax.dynamic_update_index_in_dim(whole, part, slot, 0)  7.52 us
    unnamed x16, local copies, waits for them, and re-layouts  4 us
  transfers between devices with their start and end apart: 31, of which 8 were waited for; matrix products, arithmetic and copies ran while one was open for 24% of the time, Pallas kernels for 0%

profile of v2, /device:TPU:1, one launch (start us, length us, event | category | flops | bytes accessed | tf_op | source)
XLA Modules:
  0.0 142.4 jit_solution(6132719892170194555)
XLA Ops:
  3.9 3.3 %collective-permute-start = (bf16[128,2048]{0,1:T(8,128)(2,1)S(1)}, bf16[128,2048]{0,1:T(8,128)(2,1)}, u32[]{:S(2)}, u32[]{:S(2)}) collective-permute-start(bf16[128,2048]{0,1:T(8,128)(2,1)S(1)} %bitcast.131), channel_id=1, source_target_pairs={{0,1},{1,0},{2,3},{3,2},{4,5},{5,4},{6,7},{7,6},{8,9},{9,8},{10,11... | collective-permute-start | bytes 1572872 | tf_op jit(solution)/shard_map/ppermute | solution.py:26
  12.0 7.7 %all-to-all-start = ((bf16[8,32,256]{2,1,0:T(8,128)(2,1)}), bf16[8,32,256]{2,1,0:T(8,128)(2,1)S(1)}, u32[]{:S(2)}, u32[]{:S(2)}) async-start(bf16[8,32,256]{2,1,0:T(8,128)(2,1)} %bitcast.3), calls=%async_computation | async-start | bytes 262144 | tf_op jit(solution)/shard_map/all_to_all | solution.py:18
  19.9 5.9 %collective-permute-start.11 = (bf16[8,128,128]{2,1,0:T(8,128)(2,1)}, bf16[8,128,128]{2,1,0:T(8,128)(2,1)}, u32[]{:S(2)}, u32[]{:S(2)}) collective-permute-start(bf16[8,128,128]{2,1,0:T(8,128)(2,1)} %get-tuple-element.22), channel_id=1, source_target_pairs={{0,16},{8,24},{16,0},{24,8},{1,17},{9,25},{17,1},{25,9},{2,18},{10... | collective-permute-start | bytes 786440 | tf_op jit(solution)/shard_map/ppermute | solution.py:30
  28.3 3.8 %collective-permute-done.5 = bf16[2,128,256]{1,2,0:T(8,128)(2,1)S(1)} collective-permute-done((bf16[2,128,256]{1,2,0:T(8,128)(2,1)S(1)}, bf16[2,128,256]{1,2,0:T(8,128)(2,1)S(1)}, u32[]{:S(2)}, u32[]{:S(2)}) %collective-permute-start.5) | collective-permute-done | bytes 131104 | tf_op jit(solution)/shard_map/ppermute | solution.py:30
  33.8 3.7 %collective-permute-done.6 = bf16[2,128,256]{1,2,0:T(8,128)(2,1)S(1)} collective-permute-done((bf16[2,128,256]{1,2,0:T(8,128)(2,1)S(1)}, bf16[2,128,256]{1,2,0:T(8,128)(2,1)S(1)}, u32[]{:S(2)}, u32[]{:S(2)}) %collective-permute-start.6) | collective-permute-done | bytes 131104 | tf_op jit(solution)/shard_map/ppermute | solution.py:30
  39.1 2.1 %collective-permute-done.7 = bf16[2,128,256]{1,2,0:T(8,128)(2,1)S(1)} collective-permute-done((bf16[2,128,256]{1,2,0:T(8,128)(2,1)S(1)}, bf16[2,128,256]{1,2,0:T(8,128)(2,1)S(1)}, u32[]{:S(2)}, u32[]{:S(2)}) %collective-permute-start.7) | collective-permute-done | bytes 131104 | tf_op jit(solution)/shard_map/ppermute | solution.py:30
  41.2 4.4 %collective-permute-start.1 = (bf16[256,128]{1,0:T(8,128)(2,1)S(1)}, bf16[256,128]{1,0:T(8,128)(2,1)}, u32[]{:S(2)}, u32[]{:S(2)}) collective-permute-start(bf16[256,128]{1,0:T(8,128)(2,1)S(1)} %bitcast_multiply_fusion), channel_id=1, source_target_pairs={{0,1},{1,0},{2,3},{3,2},{4,5},{5,4},{6,7},{7,6},{8,9},{9,8},{10,11... | collective-permute-start | bytes 196616 | tf_op jit(solution)/shard_map/ppermute | solution.py:26
  50.3 3.8 %collective-permute-start.14 = (bf16[4,2,128,128]{3,2,1,0:T(8,128)(2,1)}, bf16[4,2,128,128]{3,2,1,0:T(8,128)(2,1)}, u32[]{:S(2)}, u32[]{:S(2)}) collective-permute-start(bf16[4,2,128,128]{3,2,1,0:T(8,128)(2,1)} %get-tuple-element.19), channel_id=1, source_target_pairs={{0,4},{2,6},{4,0},{6,2},{1,5},{3,7},{5,1},{7,3},{8,12},{10,14},{12... | collective-permute-start | bytes 786440 | tf_op jit(solution)/shard_map/ppermute | solution.py:30
  56.5 6.9 %all-to-all-start.1 = ((bf16[8,32,256]{2,1,0:T(8,128)(2,1)}), bf16[8,32,256]{2,1,0:T(8,128)(2,1)S(1)}, u32[]{:S(2)}, u32[]{:S(2)}) async-start(bf16[8,32,256]{2,1,0:T(8,128)(2,1)} %broadcast_in_dim.71), calls=%async_computation.1 | async-start | bytes 262144 | tf_op jit(solution)/shard_map/all_to_all | solution.py:18
  68.5 2.9 %all-to-all-done.1 = bf16[8,32,256]{2,1,0:T(8,128)(2,1)S(1)} async-done(((bf16[8,32,256]{2,1,0:T(8,128)(2,1)}), bf16[8,32,256]{2,1,0:T(8,128)(2,1)S(1)}, u32[]{:S(2)}, u32[]{:S(2)}) %all-to-all-start.1) | async-done | bytes 131104 | tf_op jit(solution)/shard_map/all_to_all | solution.py:18
  73.2 3.6 %all-to-all-start.2 = ((f32[16,16,256]{2,1,0:T(8,128)}), f32[16,16,256]{2,1,0:T(8,128)S(1)}, u32[]{:S(2)}, u32[]{:S(2)}) async-start(f32[16,16,256]{2,1,0:T(8,128)} %fusion.6), calls=%async_computation.2 | async-start | bytes 524288 | tf_op jit(solution)/shard_map/all_to_all | solution.py:18
  76.9 3.3 %collective-permute-start.17 = (bf16[256,256]{1,0:T(8,128)(2,1)S(1)}, bf16[256,256]{1,0:T(8,128)(2,1)S(1)}, u32[]{:S(2)}, u32[]{:S(2)}) collective-permute-start(bf16[256,256]{1,0:T(8,128)(2,1)S(1)} %maximum_select_fusion.1), channel_id=1, source_target_pairs={{0,8},{8,16},{1,9},{9,17},{2,10},{10,18},{3,11},{11,19},{4,12},{12... | collective-permute-start | bytes 393224 | tf_op jit(solution)/shard_map/ppermute | solution.py:30
  80.2 3.0 %collective-permute-start.18 = (bf16[256,256]{1,0:T(8,128)(2,1)S(1)}, bf16[256,256]{1,0:T(8,128)(2,1)S(1)}, u32[]{:S(2)}, u32[]{:S(2)}) collective-permute-start(bf16[256,256]{1,0:T(8,128)(2,1)S(1)} %maximum_select_fusion.1), channel_id=1, source_target_pairs={{0,16},{8,24},{1,17},{9,25},{2,18},{10,26},{3,19},{11,27},{4,20},{... | collective-permute-start | bytes 393224 | tf_op jit(solution)/shard_map/ppermute | solution.py:30
  83.1 1.9 %collective-permute-start.19 = (bf16[256,256]{1,0:T(8,128)(2,1)S(1)}, bf16[256,256]{1,0:T(8,128)(2,1)S(1)}, u32[]{:S(2)}, u32[]{:S(2)}) collective-permute-start(bf16[256,256]{1,0:T(8,128)(2,1)S(1)} %maximum_select_fusion.1), channel_id=1, source_target_pairs={{0,24},{8,0},{1,25},{9,1},{2,26},{10,2},{3,27},{11,3},{4,28},{12,4... | collective-permute-start | bytes 393224 | tf_op jit(solution)/shard_map/ppermute | solution.py:30
  87.3 3.8 %all-to-all-start.3 = ((f32[8,16,256]{2,1,0:T(8,128)}), f32[8,16,256]{2,1,0:T(8,128)S(1)}, u32[]{:S(2)}, u32[]{:S(2)}) async-start(f32[8,16,256]{2,1,0:T(8,128)} %maximum_bitcast_fusion.2), calls=%async_computation.3 | async-start | bytes 262144 | tf_op jit(solution)/shard_map/all_to_all | solution.py:18
  91.3 7.9 %all-to-all-done.3 = f32[8,16,256]{2,1,0:T(8,128)S(1)} async-done(((f32[8,16,256]{2,1,0:T(8,128)}), f32[8,16,256]{2,1,0:T(8,128)S(1)}, u32[]{:S(2)}, u32[]{:S(2)}) %all-to-all-start.3) | async-done | bytes 131104 | tf_op jit(solution)/shard_map/all_to_all | solution.py:18
  99.9 3.4 %all-to-all-start.4 = ((bf16[8,16,256]{2,1,0:T(8,128)(2,1)}), bf16[8,16,256]{2,1,0:T(8,128)(2,1)S(1)}, u32[]{:S(2)}, u32[]{:S(2)}) async-start(bf16[8,16,256]{2,1,0:T(8,128)(2,1)} %broadcast_in_dim.77), calls=%async_computation.4 | async-start | bytes 131072 | tf_op jit(solution)/shard_map/all_to_all | solution.py:18
  104.5 2.4 %collective-permute-start.21 = (bf16[2,256,256]{2,1,0:T(8,128)(2,1)S(1)}, bf16[2,256,256]{2,1,0:T(8,128)(2,1)}, u32[]{:S(2)}, u32[]{:S(2)}) collective-permute-start(bf16[2,256,256]{2,1,0:T(8,128)(2,1)S(1)} %get-tuple-element.31), channel_id=1, source_target_pairs={{0,4},{2,6},{4,0},{6,2},{1,5},{3,7},{5,1},{7,3},{8,12},{10,14},{12... | collective-permute-start | bytes 786440 | tf_op jit(solution)/shard_map/ppermute | solution.py:30
  108.1 2.2 %all-to-all-done.4 = bf16[8,16,256]{2,1,0:T(8,128)(2,1)S(1)} async-done(((bf16[8,16,256]{2,1,0:T(8,128)(2,1)}), bf16[8,16,256]{2,1,0:T(8,128)(2,1)S(1)}, u32[]{:S(2)}, u32[]{:S(2)}) %all-to-all-start.4) | async-done | bytes 65568 | tf_op jit(solution)/shard_map/all_to_all | solution.py:18
  111.5 5.3 %all-to-all-start.5 = ((bf16[16,16,2048]{2,1,0:T(8,128)(2,1)}), bf16[16,16,2048]{2,1,0:T(8,128)(2,1)}, u32[]{:S(2)}, u32[]{:S(2)}) async-start(bf16[16,16,2048]{2,1,0:T(8,128)(2,1)} %broadcast_in_dim.78), calls=%async_computation.5 | async-start | bytes 2097152 | tf_op jit(solution)/shard_map/all_to_all | solution.py:18
  117.4 5.8 %collective-permute-start.23 = (bf16[128,256]{1,0:T(8,128)(2,1)}, bf16[128,256]{1,0:T(8,128)(2,1)}, u32[]{:S(2)}, u32[]{:S(2)}) collective-permute-start(bf16[128,256]{1,0:T(8,128)(2,1)} %dynamic-slice_bitcast_fusion.6), channel_id=1, source_target_pairs={{0,1},{1,0},{2,3},{3,2},{4,5},{5,4},{6,7},{7,6},{8,9},{9,8},{10,11... | collective-permute-start | bytes 196616 | tf_op jit(solution)/shard_map/ppermute | solution.py:26
  129.4 2.2 %copy.78 = bf16[2,128,4,4,2,128]{5,4,3,2,1,0:T(2,128)(2,1)S(1)} copy(bf16[2,128,4,4,2,128]{5,1,0,2,3,4:T(8,128)(2,1)S(1)} %fusion) | data formatting | bytes 4194304 | tf_op jit(solution)/shard_map/transpose | solution.py:116
  131.5 2.8 %reshape.151 = bf16[256,4096]{1,0:T(8,128)(2,1)} reshape(bf16[2,128,4,4,2,128]{5,4,3,2,1,0:T(2,128)(2,1)S(1)} %copy.78) | data formatting | bytes 4194304 | tf_op jit(solution)/shard_map/reshape | solution.py:116
  134.4 2.1 %fusion.2 = f32[256,256]{1,0:T(8,128)S(1)} fusion(bf16[256,2048]{0,1:T(8,128)(2,1)} %bitcast.142, bf16[256,4096]{1,0:T(8,128)(2,1)} %reshape.151), kind=kOutput, calls=%fused_computation.7 | convolution fusion | flops 268435456 | bytes 2359296 | tf_op jit(solution)/shard_map/dot_general | solution.py:34
  (130 shorter events, 46.7 us)
Async XLA Ops:
  3.9 50.5 %collective-permute-start = (bf16[128,2048]{0,1:T(8,128)(2,1)S(1)}, bf16[128,2048]{0,1:T(8,128)(2,1)}, u32[]{:S(2)}, u32[]{:S(2)}) collective-permute-start(bf16[128,2048]{0,1:T(8,128)(2,1)S(1)} %bitcast.131), channel_id=1, source_target_pairs={{0,1},{1,0},{2,3},{3,2},{4,5},{5,4},{6,7},{7,6},{8,9},{9,8},{10,11... | collective-permute-start | bytes 1572872 | tf_op jit(solution)/shard_map/ppermute | solution.py:26
  7.2 12.7 %collective-permute-start.2 = (bf16[128,256]{0,1:T(8,128)(2,1)S(1)}, bf16[128,256]{0,1:T(8,128)(2,1)S(1)}, u32[]{:S(2)}, u32[]{:S(2)}) collective-permute-start(bf16[128,256]{0,1:T(8,128)(2,1)S(1)} %bitcast.150), channel_id=1, source_target_pairs={{16,24},{24,0},{17,25},{25,1},{18,26},{26,2},{19,27},{27,3},{20,28... | collective-permute-start | bytes 196616 | tf_op jit(solution)/shard_map/ppermute | solution.py:30
  8.5 17.3 %collective-permute-start.3 = (bf16[128,256]{0,1:T(8,128)(2,1)S(1)}, bf16[128,256]{0,1:T(8,128)(2,1)S(1)}, u32[]{:S(2)}, u32[]{:S(2)}) collective-permute-start(bf16[128,256]{0,1:T(8,128)(2,1)S(1)} %bitcast.151), channel_id=1, source_target_pairs={{16,0},{24,8},{17,1},{25,9},{18,2},{26,10},{19,3},{27,11},{20,4},{... | collective-permute-start | bytes 196616 | tf_op jit(solution)/shard_map/ppermute | solution.py:30
  9.8 16.6 %collective-permute-start.4 = (bf16[128,256]{0,1:T(8,128)(2,1)S(1)}, bf16[128,256]{0,1:T(8,128)(2,1)S(1)}, u32[]{:S(2)}, u32[]{:S(2)}) collective-permute-start(bf16[128,256]{0,1:T(8,128)(2,1)S(1)} %bitcast.152), channel_id=1, source_target_pairs={{16,8},{24,16},{17,9},{25,17},{18,10},{26,18},{19,11},{27,19},{20,... | collective-permute-start | bytes 196616 | tf_op jit(solution)/shard_map/ppermute | solution.py:30
  12.0 34.2 %collective-permute-start.10 = (bf16[8,128,128]{2,1,0:T(8,128)(2,1)}, bf16[8,128,128]{2,1,0:T(8,128)(2,1)}, u32[]{:S(2)}, u32[]{:S(2)}) collective-permute-start(bf16[8,128,128]{2,1,0:T(8,128)(2,1)} %get-tuple-element.23), channel_id=1, source_target_pairs={{0,8},{8,16},{16,24},{24,0},{1,9},{9,17},{17,25},{25,1},{2,10},{10... | collective-permute-start | bytes 786440 | tf_op jit(solution)/shard_map/ppermute | solution.py:30
  12.0 33.8 %all-to-all-start = ((bf16[8,32,256]{2,1,0:T(8,128)(2,1)}), bf16[8,32,256]{2,1,0:T(8,128)(2,1)S(1)}, u32[]{:S(2)}, u32[]{:S(2)}) async-start(bf16[8,32,256]{2,1,0:T(8,128)(2,1)} %bitcast.3), calls=%async_computation | async-start | bytes 262144 | tf_op jit(solution)/shard_map/all_to_all | solution.py:18
  19.9 27.4 %collective-permute-start.11 = (bf16[8,128,128]{2,1,0:T(8,128)(2,1)}, bf16[8,128,128]{2,1,0:T(8,128)(2,1)}, u32[]{:S(2)}, u32[]{:S(2)}) collective-permute-start(bf16[8,128,128]{2,1,0:T(8,128)(2,1)} %get-tuple-element.22), channel_id=1, source_target_pairs={{0,16},{8,24},{16,0},{24,8},{1,17},{9,25},{17,1},{25,9},{2,18},{10... | collective-permute-start | bytes 786440 | tf_op jit(solution)/shard_map/ppermute | solution.py:30
  25.8 22.5 %collective-permute-start.12 = (bf16[8,128,128]{2,1,0:T(8,128)(2,1)S(1)}, bf16[8,128,128]{2,1,0:T(8,128)(2,1)}, u32[]{:S(2)}, u32[]{:S(2)}) collective-permute-start(bf16[8,128,128]{2,1,0:T(8,128)(2,1)S(1)} %get-tuple-element.21), channel_id=1, source_target_pairs={{0,24},{8,0},{16,8},{24,16},{1,25},{9,1},{17,9},{25,17},{2,26},{10... | collective-permute-start | bytes 786440 | tf_op jit(solution)/shard_map/ppermute | solution.py:30
  41.2 27.2 %collective-permute-start.1 = (bf16[256,128]{1,0:T(8,128)(2,1)S(1)}, bf16[256,128]{1,0:T(8,128)(2,1)}, u32[]{:S(2)}, u32[]{:S(2)}) collective-permute-start(bf16[256,128]{1,0:T(8,128)(2,1)S(1)} %bitcast_multiply_fusion), channel_id=1, source_target_pairs={{0,1},{1,0},{2,3},{3,2},{4,5},{5,4},{6,7},{7,6},{8,9},{9,8},{10,11... | collective-permute-start | bytes 196616 | tf_op jit(solution)/shard_map/ppermute | solution.py:26
  46.2 39.1 %collective-permute-start.8 = (bf16[1024,256]{1,0:T(8,128)(2,1)S(1)}, bf16[1024,256]{1,0:T(8,128)(2,1)}, u32[]{:S(2)}, u32[]{:S(2)}) collective-permute-start(bf16[1024,256]{1,0:T(8,128)(2,1)S(1)} %bitcast.134), channel_id=1, source_target_pairs={{0,1},{1,0},{2,3},{3,2},{4,5},{5,4},{6,7},{7,6},{8,9},{9,8},{10,11... | collective-permute-start | bytes 1572872 | tf_op jit(solution)/shard_map/ppermute | solution.py:26
  50.2 13.2 %collective-permute-start.13 = (bf16[4,2,128,128]{3,2,1,0:T(8,128)(2,1)}, bf16[4,2,128,128]{3,2,1,0:T(8,128)(2,1)}, u32[]{:S(2)}, u32[]{:S(2)}) collective-permute-start(bf16[4,2,128,128]{3,2,1,0:T(8,128)(2,1)} %get-tuple-element.20), channel_id=1, source_target_pairs={{0,2},{2,4},{4,6},{6,0},{1,3},{3,5},{5,7},{7,1},{8,10},{10,12},{12... | collective-permute-start | bytes 786440 | tf_op jit(solution)/shard_map/ppermute | solution.py:30
  50.3 15.7 %collective-permute-start.14 = (bf16[4,2,128,128]{3,2,1,0:T(8,128)(2,1)}, bf16[4,2,128,128]{3,2,1,0:T(8,128)(2,1)}, u32[]{:S(2)}, u32[]{:S(2)}) collective-permute-start(bf16[4,2,128,128]{3,2,1,0:T(8,128)(2,1)} %get-tuple-element.19), channel_id=1, source_target_pairs={{0,4},{2,6},{4,0},{6,2},{1,5},{3,7},{5,1},{7,3},{8,12},{10,14},{12... | collective-permute-start | bytes 786440 | tf_op jit(solution)/shard_map/ppermute | solution.py:30
  54.4 12.5 %collective-permute-start.15 = (bf16[4,2,128,128]{3,2,1,0:T(8,128)(2,1)S(1)}, bf16[4,2,128,128]{3,2,1,0:T(8,128)(2,1)S(1)}, u32[]{:S(2)}, u32[]{:S(2)}) collective-permute-start(bf16[4,2,128,128]{3,2,1,0:T(8,128)(2,1)S(1)} %get-tuple-element.18), channel_id=1, source_target_pairs={{0,6},{2,0},{4,2},{6,4},{1,7},{3,1},{5,3},{7,5},{8,14},{10,8},{12,... | collective-permute-start | bytes 786440 | tf_op jit(solution)/shard_map/ppermute | solution.py:30
  56.5 15.0 %all-to-all-start.1 = ((bf16[8,32,256]{2,1,0:T(8,128)(2,1)}), bf16[8,32,256]{2,1,0:T(8,128)(2,1)S(1)}, u32[]{:S(2)}, u32[]{:S(2)}) async-start(bf16[8,32,256]{2,1,0:T(8,128)(2,1)} %broadcast_in_dim.71), calls=%async_computation.1 | async-start | bytes 262144 | tf_op jit(solution)/shard_map/all_to_all | solution.py:18
  67.0 62.0 %collective-permute-start.16 = (bf16[4,4,2,128,128]{4,3,2,1,0:T(8,128)(2,1)S(1)}, bf16[4,4,2,128,128]{4,3,2,1,0:T(8,128)(2,1)S(1)}, u32[]{:S(2)}, u32[]{:S(2)}) collective-permute-start(bf16[4,4,2,128,128]{4,3,2,1,0:T(8,128)(2,1)S(1)} %bitcast_dynamic-update-slice_fusion), channel_id=1, source_target_pairs={{0,1},{1,0},{2,3},{3,2},{4,5},{5,4},{6,7},{7,6},{8,9},{9,8},{10,11... | collective-permute-start | bytes 3145736 | tf_op jit(solution)/shard_map/ppermute | solution.py:26
  73.2 11.9 %all-to-all-start.2 = ((f32[16,16,256]{2,1,0:T(8,128)}), f32[16,16,256]{2,1,0:T(8,128)S(1)}, u32[]{:S(2)}, u32[]{:S(2)}) async-start(f32[16,16,256]{2,1,0:T(8,128)} %fusion.6), calls=%async_computation.2 | async-start | bytes 524288 | tf_op jit(solution)/shard_map/all_to_all | solution.py:18
  76.9 14.3 %collective-permute-start.17 = (bf16[256,256]{1,0:T(8,128)(2,1)S(1)}, bf16[256,256]{1,0:T(8,128)(2,1)S(1)}, u32[]{:S(2)}, u32[]{:S(2)}) collective-permute-start(bf16[256,256]{1,0:T(8,128)(2,1)S(1)} %maximum_select_fusion.1), channel_id=1, source_target_pairs={{0,8},{8,16},{1,9},{9,17},{2,10},{10,18},{3,11},{11,19},{4,12},{12... | collective-permute-start | bytes 393224 | tf_op jit(solution)/shard_map/ppermute | solution.py:30
  80.2 11.0 %collective-permute-start.18 = (bf16[256,256]{1,0:T(8,128)(2,1)S(1)}, bf16[256,256]{1,0:T(8,128)(2,1)S(1)}, u32[]{:S(2)}, u32[]{:S(2)}) collective-permute-start(bf16[256,256]{1,0:T(8,128)(2,1)S(1)} %maximum_select_fusion.1), channel_id=1, source_target_pairs={{0,16},{8,24},{1,17},{9,25},{2,18},{10,26},{3,19},{11,27},{4,20},{... | collective-permute-start | bytes 393224 | tf_op jit(solution)/shard_map/ppermute | solution.py:30
  87.3 11.9 %all-to-all-start.3 = ((f32[8,16,256]{2,1,0:T(8,128)}), f32[8,16,256]{2,1,0:T(8,128)S(1)}, u32[]{:S(2)}, u32[]{:S(2)}) async-start(f32[8,16,256]{2,1,0:T(8,128)} %maximum_bitcast_fusion.2), calls=%async_computation.3 | async-start | bytes 262144 | tf_op jit(solution)/shard_map/all_to_all | solution.py:18
  103.3 20.2 %collective-permute-start.20 = (bf16[2,256,256]{2,1,0:T(8,128)(2,1)S(1)}, bf16[2,256,256]{2,1,0:T(8,128)(2,1)}, u32[]{:S(2)}, u32[]{:S(2)}) collective-permute-start(bf16[2,256,256]{2,1,0:T(8,128)(2,1)S(1)} %get-tuple-element.31), channel_id=1, source_target_pairs={{0,2},{2,4},{4,6},{6,0},{1,3},{3,5},{5,7},{7,1},{8,10},{10,12},{12... | collective-permute-start | bytes 786440 | tf_op jit(solution)/shard_map/ppermute | solution.py:30
  104.5 21.0 %collective-permute-start.21 = (bf16[2,256,256]{2,1,0:T(8,128)(2,1)S(1)}, bf16[2,256,256]{2,1,0:T(8,128)(2,1)}, u32[]{:S(2)}, u32[]{:S(2)}) collective-permute-start(bf16[2,256,256]{2,1,0:T(8,128)(2,1)S(1)} %get-tuple-element.31), channel_id=1, source_target_pairs={{0,4},{2,6},{4,0},{6,2},{1,5},{3,7},{5,1},{7,3},{8,12},{10,14},{12... | collective-permute-start | bytes 786440 | tf_op jit(solution)/shard_map/ppermute | solution.py:30
  107.0 19.7 %collective-permute-start.22 = (bf16[2,256,256]{2,1,0:T(8,128)(2,1)S(1)}, bf16[2,256,256]{2,1,0:T(8,128)(2,1)S(1)}, u32[]{:S(2)}, u32[]{:S(2)}) collective-permute-start(bf16[2,256,256]{2,1,0:T(8,128)(2,1)S(1)} %get-tuple-element.31), channel_id=1, source_target_pairs={{0,6},{2,0},{4,2},{6,4},{1,7},{3,1},{5,3},{7,5},{8,14},{10,8},{12,... | collective-permute-start | bytes 786440 | tf_op jit(solution)/shard_map/ppermute | solution.py:30
  111.5 25.0 %all-to-all-start.5 = ((bf16[16,16,2048]{2,1,0:T(8,128)(2,1)}), bf16[16,16,2048]{2,1,0:T(8,128)(2,1)}, u32[]{:S(2)}, u32[]{:S(2)}) async-start(bf16[16,16,2048]{2,1,0:T(8,128)(2,1)} %broadcast_in_dim.78), calls=%async_computation.5 | async-start | bytes 2097152 | tf_op jit(solution)/shard_map/all_to_all | solution.py:18
  117.4 21.9 %collective-permute-start.23 = (bf16[128,256]{1,0:T(8,128)(2,1)}, bf16[128,256]{1,0:T(8,128)(2,1)}, u32[]{:S(2)}, u32[]{:S(2)}) collective-permute-start(bf16[128,256]{1,0:T(8,128)(2,1)} %dynamic-slice_bitcast_fusion.6), channel_id=1, source_target_pairs={{0,1},{1,0},{2,3},{3,2},{4,5},{5,4},{6,7},{7,6},{8,9},{9,8},{10,11... | collective-permute-start | bytes 196616 | tf_op jit(solution)/shard_map/ppermute | solution.py:26
  (14 other events, 90.8 us)

commit v3 on v1

v3 whole, which is shorter than its diff:
```python
import functools
import math

import jax
import jax.numpy as jnp
from jax import lax
from jax.experimental import pallas as pl
from jax.experimental.pallas import tpu as pltpu
from jax.sharding import Mesh
from jax.sharding import PartitionSpec as P


TB = 128
COL = ("x", "y", "core")
CHIP = ("x", "y")
ROWS = 8
CHIPS = 16
K = 512
F32 = jnp.float32
BF16 = jnp.bfloat16
SHIFTS = (0, 1, 2, 3)


def exchange(x, axis):
    return lax.all_to_all(x, axis, split_axis=0, concat_axis=0, tiled=True)


def partner(x):
    return lax.ppermute(x, "core", [(0, 1), (1, 0)])


def shifted(x, axis, step, sources):
    return lax.ppermute(x, axis, [(i, (i + step) % 4) for i in sources])


def dot_nt(a, b):
    return lax.dot_general(a, b, (((1,), (1,)), ((), ())), preferred_element_type=F32)


def here():
    return lax.axis_index("x"), lax.axis_index("y")


def back(index, step):
    return lax.rem(index - step + 4, 4)


def local(kernel, outs, *args, smem=(), flops=1_000_000):
    size = sum(a.size * a.dtype.itemsize for a in args)
    kept = size + sum(math.prod(shape) * jnp.dtype(dtype).itemsize for shape, dtype in outs)
    specs = [
        pl.BlockSpec(memory_space=pltpu.SMEM if i in smem else pltpu.VMEM)
        for i in range(len(args))
    ]
    return pl.pallas_call(
        kernel,
        out_shape=[jax.ShapeDtypeStruct(shape, dtype) for shape, dtype in outs],
        in_specs=specs,
        out_specs=[pl.BlockSpec(memory_space=pltpu.VMEM) for _ in outs],
        cost_estimate=pl.CostEstimate(flops=flops, bytes_accessed=2 * size, transcendentals=0),
        compiler_params=pltpu.CompilerParams(vmem_limit_bytes=kept + 2**21),
    )(*args)


def turned(given, out):
    lines = jnp.concatenate([given[0, 0, 0].T, given[0, 1, 0].T], axis=1)
    lines = lines.reshape(16, 2, 16, 2 * TB)
    lines = jnp.where(lax.axis_index("core") == 0, lines[:, 0], lines[:, 1])
    out[...] = lines.reshape(ROWS, 32, 2 * TB)


def send_x(factor, mask, *outs):
    x, _ = here()
    for d, out in enumerate(outs):
        base = lax.rem(x + d, 4) * 8
        for i in range(8):
            out[i] = jnp.where(mask[base + i] == 1, factor[base + i], jnp.zeros((TB, TB), BF16))


def pack_y(*refs):
    came, outs = refs[:4], refs[4:]
    _, y = here()
    for e, out in enumerate(outs):
        base = lax.rem(y + e, 4) * 2
        for d in SHIFTS:
            out[2 * d] = came[d][base]
            out[2 * d + 1] = came[d][base + 1]


def pick(first, *refs):
    came, out = refs[:4], refs[4]
    x, _ = here()
    for d in SHIFTS:
        side = back(x, d) - first

        @pl.when(jnp.logical_and(side >= 0, side < 2))
        def _(d=d, side=side):
            out[side] = came[d][...]


def first_rows(due, own, other, out):
    lines = jnp.concatenate(
        [due[r][:, a * TB : (a + 1) * TB] for a in range(2) for r in range(ROWS)], axis=1
    )
    both = jnp.concatenate([dot_nt(lines, own[...]), dot_nt(lines, other[...])], axis=1)
    both = both.astype(BF16)
    for r in range(ROWS):
        out[r] = both


def update(solved, own, other, out):
    tiles = jnp.concatenate([own[...], other[...]], axis=1)
    reached = dot_nt(solved[...].reshape(256, 256), tiles)
    out[...] = reached.reshape(CHIPS, 16, 2 * TB)


def due_rows(came, given, out):
    reached = came[0]
    for chip in range(1, 8):
        reached = reached + came[chip]
    out[...] = (given[...].astype(F32) - reached).astype(BF16)


def second_rows(mine, theirs, *refs):
    pieces, out = refs[:4], refs[4]
    _, y = here()
    first = lax.axis_index("core") == 0
    a, b = mine[...], theirs[...]
    due = jnp.concatenate([jnp.where(first, a, b), jnp.where(first, b, a)], axis=0)
    for e in SHIFTS:
        for side in range(2):
            out[side * 4 + back(y, e)] = dot_nt(due, pieces[e][side])


def spread(given, out):
    for chip in range(CHIPS):
        out[chip] = given[...]


def second_sum(came, out):
    total = came[0]
    for r in range(1, ROWS):
        total = total + came[r]
    total = total.astype(BF16)
    for r in range(ROWS):
        out[r] = total


def early_part(*refs):
    tiles, solved, out = refs[:4], refs[4:8], refs[8]
    x, _ = here()
    total = jnp.zeros((2 * TB, K), F32)
    for e in SHIFTS:
        for side in range(2):
            block = tiles[e][pl.ds(back(x, side) * 2, 2)].reshape(2 * TB, TB)
            total = total + dot_nt(block, solved[e][side])
    out[...] = total.reshape(2, TB, K)


def late_part(tiles, solved, which):
    x, y = here()
    total = jnp.zeros((TB, K), F32)
    for e in SHIFTS:
        for side in range(2):
            block = tiles[e][back(x, 2 + side) * 2 + which]
            lines = solved[:, side * 4 + back(y, e)].reshape(K, TB)
            total = total + dot_nt(block, lines)
    return total


def part_of_partner(*refs):
    tiles, solved, early, out = refs[:4], *refs[4:]
    which = 1 - lax.axis_index("core")
    out[...] = early[which] + late_part(tiles, solved, which)


def own_part(*refs):
    tiles, solved, early, solved0, given, left, result = refs[:4], *refs[4:]
    which = lax.axis_index("core")
    left[...] = given[...].astype(F32) - (early[which] + late_part(tiles, solved, which))
    chip = lax.axis_index("x") * 4 + lax.axis_index("y")

    @pl.when(chip < 8)
    def _():
        result[...] = solved0[...].T

    @pl.when(chip >= 8)
    def _():
        result[...] = solved[:, chip - 8].reshape(K, TB).T


def steps(rhs_super, factor_super, mask_super, dinv_rows, factor_trail, mask_trail, rhs_trail):
    core = lax.axis_index("core")
    chip = lax.axis_index(CHIP)

    rhs0 = pl.pallas_call(
        turned,
        grid=(1,),
        out_shape=jax.ShapeDtypeStruct((ROWS, 32, 2 * TB), BF16),
        in_specs=[pl.BlockSpec((1, 2, 1, TB, K), lambda i: (0, 0, 0, 0, 0))],
        out_specs=pl.BlockSpec((ROWS, 32, 2 * TB), lambda i: (0, 0, 0)),
        compiler_params=pltpu.CompilerParams(vmem_limit_bytes=2**22),
        name="turn",
    )(rhs_super)
    rhs0, dinv, factor_trail, rhs_super = lax.optimization_barrier(
        (rhs0, dinv_rows[0, 0], factor_trail, rhs_super)
    )
    due0 = exchange(rhs0, "row")
    dinv_other = partner(dinv)
    row = lax.axis_index("row")
    d1 = jnp.concatenate(
        [lax.dynamic_slice(dinv, (0, (a * ROWS + row) * TB), (TB, TB)) for a in range(2)], 1
    )
    came = [d1] + [shifted(d1, "x", d, (2, 3)) for d in (1, 2, 3)]
    [d1] = local(functools.partial(pick, 2), [((2, TB, 2 * TB), BF16)], *came)
    d1 = [d1] + [shifted(d1, "y", e, SHIFTS) for e in (1, 2, 3)]

    mask = mask_trail.reshape(32)
    sent = local(
        send_x, [((8, TB, TB), BF16)] * 4, factor_trail.reshape(32, TB, TB), mask,
        smem=(1,),
    )
    came = [sent[0]] + [shifted(sent[d], "x", d, SHIFTS) for d in (1, 2, 3)]
    sent = local(pack_y, [((8, TB, TB), BF16)] * 4, *came)
    tiles = [sent[0]] + [shifted(sent[e], "y", e, SHIFTS) for e in (1, 2, 3)]

    [solved0] = local(
        first_rows, [((ROWS, 32, 2 * TB), BF16)], due0, dinv, dinv_other,
        flops=2**26,
    )
    solved0 = exchange(solved0, "row")

    keep = mask_super[1].astype(BF16).reshape(2, 1, 1)
    tiles10 = (factor_super[1].reshape(2, TB, TB) * keep).reshape(2 * TB, TB)
    [reached] = local(
        update, [((CHIPS, 16, 2 * TB), F32)], solved0, tiles10, partner(tiles10),
        flops=2**25,
    )
    reached = exchange(reached, CHIP)
    rhs1 = rhs_super[1, :, 0].reshape(2 * TB, K)
    rhs1 = lax.dynamic_slice(rhs1, (0, chip * 32 + core * 16), (2 * TB, 16)).T
    [due1] = local(due_rows, [((16, 2 * TB), BF16)], reached, rhs1)
    [part] = local(
        second_rows, [((ROWS, 32, TB), F32)], due1, partner(due1), *d1,
        flops=2**25,
    )
    part = exchange(part, "row")
    [solved1] = local(second_sum, [((ROWS, 32, TB), BF16)], part)
    solved1 = exchange(solved1, "row")
    [solved1] = local(spread, [((CHIPS, ROWS, 32, TB), BF16)], solved1)
    solved1 = exchange(solved1, CHIP)

    pairs = solved0.reshape(2 * K // 4, 2 * TB)
    mine, theirs = pairs[:, :TB], partner(pairs[:, TB:])
    mine, theirs = mine.reshape(16, 16, TB), theirs.reshape(16, 16, TB)
    own0 = jnp.where(
        core == 0, jnp.stack([mine, theirs], 1), jnp.stack([theirs, mine], 1)
    ).reshape(K, TB)
    came = [own0] + [shifted(own0, "x", d, (0, 1)) for d in (1, 2, 3)]
    [pair] = local(functools.partial(pick, 0), [((2, K, TB), BF16)], *came)
    all0 = [pair] + [shifted(pair, "y", e, SHIFTS) for e in (1, 2, 3)]

    [early] = local(early_part, [((2, TB, K), F32)], *tiles, *all0, flops=2**28)
    [theirs] = local(part_of_partner, [((TB, K), F32)], *tiles, solved1, early, flops=2**27)
    theirs = partner(theirs)
    left, solved = local(
        own_part, [((TB, K), F32), ((TB, K), BF16)], *tiles, solved1, early, own0,
        rhs_trail.reshape(TB, K), flops=2**27,
    )
    remaining = (left - theirs).astype(BF16)
    return solved.reshape(1, 1, TB, K), remaining.reshape(rhs_trail.shape)


def solution(mesh):
    torus = Mesh(mesh.devices.reshape(mesh.shape["row"], 4, 4, 2), ("row", *COL))
    placed = (
        P(None, None, "row", None, None),
        P(None, None, "row", None, None, COL, None),
        P(None, None, "row", None, COL),
        P(None, COL, None, None),
        P(None, "row", None, None, COL, None),
        P(None, "row", None, COL),
        P(COL, None, "row", None, None),
    )
    return jax.shard_map(
        steps,
        mesh=torus,
        in_specs=placed,
        out_specs=(P(None, COL, None, None), P(COL, None, "row", None, None)),
        check_vma=False,
    )
```

time: 160 us -> 147 us (0.919)
  waiting for transfers between devices: 70.6 us -> 38.5 us
  starting transfers between devices: 61.1 us -> 75 us
  blocking collectives: 9.6 us -> 20 us
  Pallas kernels: 0 us -> 7.5 us
  local copies, waits for them, and re-layouts: 9.3 us -> 3.21 us
  matrix products: 5.17 us -> 0 us
    all_to_all x8 -> x4, waiting for transfers between devices: 56.9 us -> 13.4 us  [exchange(): return lax.all_to_all(x, axis, split_axis=0, concat_axis=0, tiled=True)]
    ppermute x2 -> x18, starting transfers between devices: 6.69 us -> 28.8 us  [shifted(): return lax.ppermute(x, axis, [(i, (i + step) % 4) for i in sources])]
    all_to_all x8 -> x4, starting transfers between devices: 43.8 us -> 21.9 us  [exchange(): return lax.all_to_all(x, axis, split_axis=0, concat_axis=0, tiled=True)]
    ppermute x8 -> x5, starting transfers between devices: 10.6 us -> 24.3 us  [partner(): return lax.ppermute(x, 'core', [(0, 1), (1, 0)])]
    all_to_all x1 -> x2, blocking collectives: 9.6 us -> 20 us  [exchange(): return lax.all_to_all(x, axis, split_axis=0, concat_axis=0, tiled=True)]
    ppermute x2 -> x18, waiting for transfers between devices: 13.2 us -> 23.4 us  [shifted(): return lax.ppermute(x, axis, [(i, (i + step) % 4) for i in sources])]
    pallas_call x0 -> x14, Pallas kernels: none -> 7.5 us  [the longest x13 6.72 us: local(): pl.pallas_call(kernel, out_shape=[jax.ShapeDtypeStruct(shape, dtype) for...]
    dot_general x7 -> x0, matrix products: 5.17 us -> none  [dot_nt(): lax.dot_general(a, b, (((1,), (1,)), ((), ())), preferred_element_type=F32)]
  transfers between devices with their start and end apart: 18 -> 27, of which waited for: 11 -> 13; matrix products, arithmetic and copies ran while one was open for 6% -> 0% of each run, Pallas kernels for 0% -> 2%
where the time goes in v3:
time: 147 us; the launch traced here: 146 us
  starting transfers between devices  75 us (51%)
  waiting for transfers between devices  38.5 us (26%)
  blocking collectives  20 us (14%)
  Pallas kernels  7.5 us (5%)
  local copies, waits for them, and re-layouts  3.21 us (2%)
    ppermute x18, starting transfers between devices, shifted(): return lax.ppermute(x, axis, [(i, (i + step) % 4) for i in sources])  28.8 us
    ppermute x5, starting transfers between devices, partner(): return lax.ppermute(x, 'core', [(0, 1), (1, 0)])  24.3 us
    ppermute x18, waiting for transfers between devices, shifted(): return lax.ppermute(x, axis, [(i, (i + step) % 4) for i in sources])  23.4 us
    all_to_all x4, starting transfers between devices, exchange(): return lax.all_to_all(x, axis, split_axis=0, concat_axis=0, tiled=True)  21.9 us
    all_to_all x2, blocking collectives, exchange(): return lax.all_to_all(x, axis, split_axis=0, concat_axis=0, tiled=True)  20 us
    all_to_all x4, waiting for transfers between devices, exchange(): return lax.all_to_all(x, axis, split_axis=0, concat_axis=0, tiled=True)  13.4 us
    pallas_call x13, Pallas kernels, local(): pl.pallas_call(kernel, out_shape=[jax.ShapeDtypeStruct(shape, dtype) for...  6.72 us
  transfers between devices with their start and end apart: 27, of which 13 were waited for; matrix products, arithmetic and copies ran while one was open for 0% of the time, Pallas kernels for 2%

profile of v3, /device:TPU:1, one launch (start us, length us, event | category | flops | bytes accessed | tf_op | source)
XLA Modules:
  0.0 145.9 jit_solution(2747521457136293643)
XLA Ops:
  2.8 3.2 %collective-permute-start.6 = (bf16[128,2048]{1,0:T(8,128)(2,1)S(1)}, bf16[128,2048]{1,0:T(8,128)(2,1)S(1)}, u32[]{:S(2)}, u32[]{:S(2)}) collective-permute-start(bf16[128,2048]{1,0:T(8,128)(2,1)S(1)} %bitcast.27), channel_id=1, source_target_pairs={{0,1},{1,0},{2,3},{3,2},{4,5},{5,4},{6,7},{7,6},{8,9},{9,8},{10,11... | collective-permute-start | bytes 1572872 | tf_op jit(solution)/shard_map/ppermute | solution.py:29
  6.0 6.5 %all-to-all-start = ((bf16[8,32,256]{2,1,0:T(8,128)(2,1)}), bf16[8,32,256]{2,1,0:T(8,128)(2,1)S(1)}, u32[]{:S(2)}, u32[]{:S(2)}) async-start(bf16[8,32,256]{2,1,0:T(8,128)(2,1)} %turn.1), calls=%async_computation | async-start | bytes 262144 | tf_op jit(solution)/shard_map/all_to_all | solution.py:25
  12.5 8.3 %all-to-all-done.due = bf16[8,32,256]{2,1,0:T(8,128)(2,1)S(1)} async-done(((bf16[8,32,256]{2,1,0:T(8,128)(2,1)}), bf16[8,32,256]{2,1,0:T(8,128)(2,1)S(1)}, u32[]{:S(2)}, u32[]{:S(2)}) %all-to-all-start) | async-done | bytes 131104 | tf_op jit(solution)/shard_map/all_to_all | solution.py:25
  21.9 3.5 %all-to-all-start.1 = ((bf16[8,32,256]{2,1,0:T(8,128)(2,1)}), bf16[8,32,256]{2,1,0:T(8,128)(2,1)S(1)}, u32[]{:S(2)}, u32[]{:S(2)}) async-start(bf16[8,32,256]{2,1,0:T(8,128)(2,1)} %shard_map.88), calls=%async_computation.1 | async-start | bytes 262144 | tf_op jit(solution)/shard_map/all_to_all | solution.py:25
  28.2 5.1 %all-to-all-done.1.solved = bf16[8,32,256]{2,1,0:T(8,128)(2,1)S(1)} async-done(((bf16[8,32,256]{2,1,0:T(8,128)(2,1)}), bf16[8,32,256]{2,1,0:T(8,128)(2,1)S(1)}, u32[]{:S(2)}, u32[]{:S(2)}) %all-to-all-start.1) | async-done | bytes 131104 | tf_op jit(solution)/shard_map/all_to_all | solution.py:25
  34.2 6.8 %all-to-all-start.2 = ((f32[16,16,256]{2,1,0:T(8,128)}), f32[16,16,256]{2,1,0:T(8,128)S(1)}, u32[]{:S(2)}, u32[]{:S(2)}) async-start(f32[16,16,256]{2,1,0:T(8,128)} %shard_map.89), calls=%async_computation.2 | async-start | bytes 524288 | tf_op jit(solution)/shard_map/all_to_all | solution.py:25
  44.3 2.9 %collective-permute-done.9.refs_1_ = bf16[128,256]{1,0:T(8,128)(2,1)S(1)} collective-permute-done((bf16[128,256]{1,0:T(8,128)(2,1)S(1)}, bf16[128,256]{1,0:T(8,128)(2,1)S(1)}, u32[]{:S(2)}, u32[]{:S(2)}) %collective-permute-start.9) | collective-permute-done | bytes 65568 | tf_op jit(solution)/shard_map/ppermute | solution.py:33
  47.2 3.4 %collective-permute-done.10.refs_2_ = bf16[128,256]{1,0:T(8,128)(2,1)S(1)} collective-permute-done((bf16[128,256]{1,0:T(8,128)(2,1)S(1)}, bf16[128,256]{1,0:T(8,128)(2,1)S(1)}, u32[]{:S(2)}, u32[]{:S(2)}) %collective-permute-start.10) | collective-permute-done | bytes 65568 | tf_op jit(solution)/shard_map/ppermute | solution.py:33
  51.9 2.4 %collective-permute-start.13 = (bf16[2,128,256]{2,1,0:T(8,128)(2,1)S(1)}, bf16[2,128,256]{2,1,0:T(8,128)(2,1)S(1)}, u32[]{:S(2)}, u32[]{:S(2)}) collective-permute-start(bf16[2,128,256]{2,1,0:T(8,128)(2,1)S(1)} %shard_map.91.refs_0_), channel_id=1, source_target_pairs={{0,4},{2,6},{4,0},{6,2},{1,5},{3,7},{5,1},{7,3},{8,12},{10,14},{12... | collective-permute-start | bytes 393224 | tf_op jit(solution)/shard_map/ppermute | solution.py:33
  56.6 4.4 %collective-permute-start.8 = (bf16[16,256]{1,0:T(8,128)(2,1)S(1)}, bf16[16,256]{1,0:T(8,128)(2,1)S(1)}, u32[]{:S(2)}, u32[]{:S(2)}) collective-permute-start(bf16[16,256]{1,0:T(8,128)(2,1)S(1)} %shard_map.90.mine), channel_id=1, source_target_pairs={{0,1},{1,0},{2,3},{3,2},{4,5},{5,4},{6,7},{7,6},{8,9},{9,8},{10,11... | collective-permute-start | bytes 24584 | tf_op jit(solution)/shard_map/ppermute | solution.py:29
  62.2 10.4 %all_to_all.30.came = f32[8,32,128]{2,1,0:T(8,128)S(1)} all-to-all(f32[8,32,128]{2,1,0:T(8,128)S(1)} %shard_map.92), channel_id=1, replica_groups=mesh['row'=8,'x'=4,'y'=4,'core'=2] {'row'}, dimensions={0} | all-to-all | bytes 262144 | tf_op jit(solution)/shard_map/all_to_all | solution.py:25
  72.6 9.6 %all_to_all.31.given = bf16[8,32,128]{2,1,0:T(8,128)(2,1)S(1)} all-to-all(bf16[8,32,128]{2,1,0:T(8,128)(2,1)S(1)} %shard_map.93), channel_id=1, replica_groups=mesh['row'=8,'x'=4,'y'=4,'core'=2] {'row'}, dimensions={0} | all-to-all | bytes 131072 | tf_op jit(solution)/shard_map/all_to_all | solution.py:25
  83.3 5.2 %all-to-all-start.5 = ((bf16[16,8,32,128]{3,2,1,0:T(8,128)(2,1)}), bf16[16,8,32,128]{3,2,1,0:T(8,128)(2,1)S(1)}, u32[]{:S(2)}, u32[]{:S(2)}) async-start(bf16[16,8,32,128]{3,2,1,0:T(8,128)(2,1)} %shard_map.94), calls=%async_computation.5 | async-start | bytes 2097152 | tf_op jit(solution)/shard_map/all_to_all | solution.py:25
  91.4 2.4 %collective-permute-start.1 = (bf16[8,128,128]{2,1,0:T(8,128)(2,1)S(1)}, bf16[8,128,128]{2,1,0:T(8,128)(2,1)S(1)}, u32[]{:S(2)}, u32[]{:S(2)}) collective-permute-start(bf16[8,128,128]{2,1,0:T(8,128)(2,1)S(1)} %get-tuple-element.19), channel_id=1, source_target_pairs={{0,16},{8,24},{16,0},{24,8},{1,17},{9,25},{17,1},{25,9},{2,18},{10... | collective-permute-start | bytes 786440 | tf_op jit(solution)/shard_map/ppermute | solution.py:33
  95.0 7.2 %collective-permute-start.15 = (bf16[256,128]{1,0:T(8,128)(2,1)S(1)}, bf16[256,128]{1,0:T(8,128)(2,1)S(1)}, u32[]{:S(2)}, u32[]{:S(2)}) collective-permute-start(bf16[256,128]{1,0:T(8,128)(2,1)S(1)} %get-tuple-element.33), channel_id=1, source_target_pairs={{0,1},{1,0},{2,3},{3,2},{4,5},{5,4},{6,7},{7,6},{8,9},{9,8},{10,11... | collective-permute-start | bytes 196616 | tf_op jit(solution)/shard_map/ppermute | solution.py:29
  102.2 2.9 %collective-permute-done.refs_1_ = bf16[8,128,128]{2,1,0:T(8,128)(2,1)S(1)} collective-permute-done((bf16[8,128,128]{2,1,0:T(8,128)(2,1)S(1)}, bf16[8,128,128]{2,1,0:T(8,128)(2,1)S(1)}, u32[]{:S(2)}, u32[]{:S(2)}) %collective-permute-start) | collective-permute-done | bytes 262176 | tf_op jit(solution)/shard_map/ppermute | solution.py:33
  105.2 3.8 %collective-permute-done.1.refs_2_ = bf16[8,128,128]{2,1,0:T(8,128)(2,1)S(1)} collective-permute-done((bf16[8,128,128]{2,1,0:T(8,128)(2,1)S(1)}, bf16[8,128,128]{2,1,0:T(8,128)(2,1)S(1)}, u32[]{:S(2)}, u32[]{:S(2)}) %collective-permute-start.1) | collective-permute-done | bytes 262176 | tf_op jit(solution)/shard_map/ppermute | solution.py:33
  110.4 2.0 %collective-permute-start.16 = (bf16[512,128]{1,0:T(8,128)(2,1)S(1)}, bf16[512,128]{1,0:T(8,128)(2,1)S(1)}, u32[]{:S(2)}, u32[]{:S(2)}) collective-permute-start(bf16[512,128]{1,0:T(8,128)(2,1)S(1)} %bitcast.20), channel_id=1, source_target_pairs={{0,8},{8,16},{1,9},{9,17},{2,10},{10,18},{3,11},{11,19},{4,12},{12... | collective-permute-start | bytes 393224 | tf_op jit(solution)/shard_map/ppermute | solution.py:33
  112.3 2.1 %collective-permute-start.17 = (bf16[512,128]{1,0:T(8,128)(2,1)S(1)}, bf16[512,128]{1,0:T(8,128)(2,1)S(1)}, u32[]{:S(2)}, u32[]{:S(2)}) collective-permute-start(bf16[512,128]{1,0:T(8,128)(2,1)S(1)} %bitcast.21), channel_id=1, source_target_pairs={{0,16},{8,24},{1,17},{9,25},{2,18},{10,26},{3,19},{11,27},{4,20},{... | collective-permute-start | bytes 393224 | tf_op jit(solution)/shard_map/ppermute | solution.py:33
  114.5 1.9 %collective-permute-start.18 = (bf16[512,128]{1,0:T(8,128)(2,1)S(1)}, bf16[512,128]{1,0:T(8,128)(2,1)S(1)}, u32[]{:S(2)}, u32[]{:S(2)}) collective-permute-start(bf16[512,128]{1,0:T(8,128)(2,1)S(1)} %bitcast.22), channel_id=1, source_target_pairs={{0,24},{8,0},{1,25},{9,1},{2,26},{10,2},{3,27},{11,3},{4,28},{12,4... | collective-permute-start | bytes 393224 | tf_op jit(solution)/shard_map/ppermute | solution.py:33
  116.4 2.5 %collective-permute-start.4 = (bf16[8,128,128]{2,1,0:T(8,128)(2,1)S(1)}, bf16[8,128,128]{2,1,0:T(8,128)(2,1)S(1)}, u32[]{:S(2)}, u32[]{:S(2)}) collective-permute-start(bf16[8,128,128]{2,1,0:T(8,128)(2,1)S(1)} %get-tuple-element.23), channel_id=1, source_target_pairs={{0,4},{2,6},{4,0},{6,2},{1,5},{3,7},{5,1},{7,3},{8,12},{10,14},{12... | collective-permute-start | bytes 786440 | tf_op jit(solution)/shard_map/ppermute | solution.py:33
  125.5 3.5 %collective-permute-done.19.refs_5_ = bf16[2,512,128]{2,1,0:T(8,128)(2,1)S(1)} collective-permute-done((bf16[2,512,128]{2,1,0:T(8,128)(2,1)S(1)}, bf16[2,512,128]{2,1,0:T(8,128)(2,1)S(1)}, u32[]{:S(2)}, u32[]{:S(2)}) %collective-permute-start.19) | collective-permute-done | bytes 262176 | tf_op jit(solution)/shard_map/ppermute | solution.py:33
  129.0 6.0 %collective-permute-done.20.refs_6_ = bf16[2,512,128]{2,1,0:T(8,128)(2,1)S(1)} collective-permute-done((bf16[2,512,128]{2,1,0:T(8,128)(2,1)S(1)}, bf16[2,512,128]{2,1,0:T(8,128)(2,1)S(1)}, u32[]{:S(2)}, u32[]{:S(2)}) %collective-permute-start.20) | collective-permute-done | bytes 262176 | tf_op jit(solution)/shard_map/ppermute | solution.py:33
  136.3 7.7 %collective-permute-start.22 = (f32[128,512]{1,0:T(8,128)S(1)}, f32[128,512]{1,0:T(8,128)S(1)}, u32[]{:S(2)}, u32[]{:S(2)}) collective-permute-start(f32[128,512]{1,0:T(8,128)S(1)} %shard_map.98), channel_id=1, source_target_pairs={{0,1},{1,0},{2,3},{3,2},{4,5},{5,4},{6,7},{7,6},{8,9},{9,8},{10,11... | collective-permute-start | bytes 786440 | tf_op jit(solution)/shard_map/ppermute | solution.py:29
  (72 shorter events, 31.3 us)
Async XLA Ops:
  2.8 18.1 %collective-permute-start.6 = (bf16[128,2048]{1,0:T(8,128)(2,1)S(1)}, bf16[128,2048]{1,0:T(8,128)(2,1)S(1)}, u32[]{:S(2)}, u32[]{:S(2)}) collective-permute-start(bf16[128,2048]{1,0:T(8,128)(2,1)S(1)} %bitcast.27), channel_id=1, source_target_pairs={{0,1},{1,0},{2,3},{3,2},{4,5},{5,4},{6,7},{7,6},{8,9},{9,8},{10,11... | collective-permute-start | bytes 1572872 | tf_op jit(solution)/shard_map/ppermute | solution.py:29
  6.0 14.9 %all-to-all-start = ((bf16[8,32,256]{2,1,0:T(8,128)(2,1)}), bf16[8,32,256]{2,1,0:T(8,128)(2,1)S(1)}, u32[]{:S(2)}, u32[]{:S(2)}) async-start(bf16[8,32,256]{2,1,0:T(8,128)(2,1)} %turn.1), calls=%async_computation | async-start | bytes 262144 | tf_op jit(solution)/shard_map/all_to_all | solution.py:25
  21.9 11.4 %all-to-all-start.1 = ((bf16[8,32,256]{2,1,0:T(8,128)(2,1)}), bf16[8,32,256]{2,1,0:T(8,128)(2,1)S(1)}, u32[]{:S(2)}, u32[]{:S(2)}) async-start(bf16[8,32,256]{2,1,0:T(8,128)(2,1)} %shard_map.88), calls=%async_computation.1 | async-start | bytes 262144 | tf_op jit(solution)/shard_map/all_to_all | solution.py:25
  34.2 22.4 %all-to-all-start.2 = ((f32[16,16,256]{2,1,0:T(8,128)}), f32[16,16,256]{2,1,0:T(8,128)S(1)}, u32[]{:S(2)}, u32[]{:S(2)}) async-start(f32[16,16,256]{2,1,0:T(8,128)} %shard_map.89), calls=%async_computation.2 | async-start | bytes 524288 | tf_op jit(solution)/shard_map/all_to_all | solution.py:25
  41.0 6.2 %collective-permute-start.9 = (bf16[128,256]{1,0:T(8,128)(2,1)S(1)}, bf16[128,256]{1,0:T(8,128)(2,1)S(1)}, u32[]{:S(2)}, u32[]{:S(2)}) collective-permute-start(bf16[128,256]{1,0:T(8,128)(2,1)S(1)} %pad_maximum_fusion.refs_0_), channel_id=1, source_target_pairs={{16,24},{24,0},{17,25},{25,1},{18,26},{26,2},{19,27},{27,3},{20,28... | collective-permute-start | bytes 196616 | tf_op jit(solution)/shard_map/ppermute | solution.py:33
  42.3 8.3 %collective-permute-start.10 = (bf16[128,256]{1,0:T(8,128)(2,1)S(1)}, bf16[128,256]{1,0:T(8,128)(2,1)S(1)}, u32[]{:S(2)}, u32[]{:S(2)}) collective-permute-start(bf16[128,256]{1,0:T(8,128)(2,1)S(1)} %pad_maximum_fusion.refs_0_), channel_id=1, source_target_pairs={{16,0},{24,8},{17,1},{25,9},{18,2},{26,10},{19,3},{27,11},{20,4},{... | collective-permute-start | bytes 196616 | tf_op jit(solution)/shard_map/ppermute | solution.py:33
  43.6 7.0 %collective-permute-start.11 = (bf16[128,256]{1,0:T(8,128)(2,1)S(1)}, bf16[128,256]{1,0:T(8,128)(2,1)S(1)}, u32[]{:S(2)}, u32[]{:S(2)}) collective-permute-start(bf16[128,256]{1,0:T(8,128)(2,1)S(1)} %pad_maximum_fusion.refs_0_), channel_id=1, source_target_pairs={{16,8},{24,16},{17,9},{25,17},{18,10},{26,18},{19,11},{27,19},{20,... | collective-permute-start | bytes 196616 | tf_op jit(solution)/shard_map/ppermute | solution.py:33
  50.6 10.4 %collective-permute-start.12 = (bf16[2,128,256]{2,1,0:T(8,128)(2,1)S(1)}, bf16[2,128,256]{2,1,0:T(8,128)(2,1)S(1)}, u32[]{:S(2)}, u32[]{:S(2)}) collective-permute-start(bf16[2,128,256]{2,1,0:T(8,128)(2,1)S(1)} %shard_map.91.refs_0_), channel_id=1, source_target_pairs={{0,2},{2,4},{4,6},{6,0},{1,3},{3,5},{5,7},{7,1},{8,10},{10,12},{12... | collective-permute-start | bytes 393224 | tf_op jit(solution)/shard_map/ppermute | solution.py:33
  51.9 9.2 %collective-permute-start.13 = (bf16[2,128,256]{2,1,0:T(8,128)(2,1)S(1)}, bf16[2,128,256]{2,1,0:T(8,128)(2,1)S(1)}, u32[]{:S(2)}, u32[]{:S(2)}) collective-permute-start(bf16[2,128,256]{2,1,0:T(8,128)(2,1)S(1)} %shard_map.91.refs_0_), channel_id=1, source_target_pairs={{0,4},{2,6},{4,0},{6,2},{1,5},{3,7},{5,1},{7,3},{8,12},{10,14},{12... | collective-permute-start | bytes 393224 | tf_op jit(solution)/shard_map/ppermute | solution.py:33
  54.3 6.8 %collective-permute-start.14 = (bf16[2,128,256]{2,1,0:T(8,128)(2,1)S(1)}, bf16[2,128,256]{2,1,0:T(8,128)(2,1)S(1)}, u32[]{:S(2)}, u32[]{:S(2)}) collective-permute-start(bf16[2,128,256]{2,1,0:T(8,128)(2,1)S(1)} %shard_map.91.refs_0_), channel_id=1, source_target_pairs={{0,6},{2,0},{4,2},{6,4},{1,7},{3,1},{5,3},{7,5},{8,14},{10,8},{12,... | collective-permute-start | bytes 393224 | tf_op jit(solution)/shard_map/ppermute | solution.py:33
  83.3 52.5 %all-to-all-start.5 = ((bf16[16,8,32,128]{3,2,1,0:T(8,128)(2,1)}), bf16[16,8,32,128]{3,2,1,0:T(8,128)(2,1)S(1)}, u32[]{:S(2)}, u32[]{:S(2)}) async-start(bf16[16,8,32,128]{3,2,1,0:T(8,128)(2,1)} %shard_map.94), calls=%async_computation.5 | async-start | bytes 2097152 | tf_op jit(solution)/shard_map/all_to_all | solution.py:25
  90.0 15.2 %collective-permute-start = (bf16[8,128,128]{2,1,0:T(8,128)(2,1)S(1)}, bf16[8,128,128]{2,1,0:T(8,128)(2,1)S(1)}, u32[]{:S(2)}, u32[]{:S(2)}) collective-permute-start(bf16[8,128,128]{2,1,0:T(8,128)(2,1)S(1)} %get-tuple-element.18), channel_id=1, source_target_pairs={{0,8},{8,16},{16,24},{24,0},{1,9},{9,17},{17,25},{25,1},{2,10},{10... | collective-permute-start | bytes 786440 | tf_op jit(solution)/shard_map/ppermute | solution.py:33
  91.4 17.6 %collective-permute-start.1 = (bf16[8,128,128]{2,1,0:T(8,128)(2,1)S(1)}, bf16[8,128,128]{2,1,0:T(8,128)(2,1)S(1)}, u32[]{:S(2)}, u32[]{:S(2)}) collective-permute-start(bf16[8,128,128]{2,1,0:T(8,128)(2,1)S(1)} %get-tuple-element.19), channel_id=1, source_target_pairs={{0,16},{8,24},{16,0},{24,8},{1,17},{9,25},{17,1},{25,9},{2,18},{10... | collective-permute-start | bytes 786440 | tf_op jit(solution)/shard_map/ppermute | solution.py:33
  93.8 15.2 %collective-permute-start.2 = (bf16[8,128,128]{2,1,0:T(8,128)(2,1)S(1)}, bf16[8,128,128]{2,1,0:T(8,128)(2,1)S(1)}, u32[]{:S(2)}, u32[]{:S(2)}) collective-permute-start(bf16[8,128,128]{2,1,0:T(8,128)(2,1)S(1)} %get-tuple-element.20), channel_id=1, source_target_pairs={{0,24},{8,0},{16,8},{24,16},{1,25},{9,1},{17,9},{25,17},{2,26},{10... | collective-permute-start | bytes 786440 | tf_op jit(solution)/shard_map/ppermute | solution.py:33
  95.0 15.4 %collective-permute-start.15 = (bf16[256,128]{1,0:T(8,128)(2,1)S(1)}, bf16[256,128]{1,0:T(8,128)(2,1)S(1)}, u32[]{:S(2)}, u32[]{:S(2)}) collective-permute-start(bf16[256,128]{1,0:T(8,128)(2,1)S(1)} %get-tuple-element.33), channel_id=1, source_target_pairs={{0,1},{1,0},{2,3},{3,2},{4,5},{5,4},{6,7},{7,6},{8,9},{9,8},{10,11... | collective-permute-start | bytes 196616 | tf_op jit(solution)/shard_map/ppermute | solution.py:29
  109.1 14.4 %collective-permute-start.3 = (bf16[8,128,128]{2,1,0:T(8,128)(2,1)S(1)}, bf16[8,128,128]{2,1,0:T(8,128)(2,1)S(1)}, u32[]{:S(2)}, u32[]{:S(2)}) collective-permute-start(bf16[8,128,128]{2,1,0:T(8,128)(2,1)S(1)} %get-tuple-element.22), channel_id=1, source_target_pairs={{0,2},{2,4},{4,6},{6,0},{1,3},{3,5},{5,7},{7,1},{8,10},{10,12},{12... | collective-permute-start | bytes 786440 | tf_op jit(solution)/shard_map/ppermute | solution.py:33
  110.4 8.5 %collective-permute-start.16 = (bf16[512,128]{1,0:T(8,128)(2,1)S(1)}, bf16[512,128]{1,0:T(8,128)(2,1)S(1)}, u32[]{:S(2)}, u32[]{:S(2)}) collective-permute-start(bf16[512,128]{1,0:T(8,128)(2,1)S(1)} %bitcast.20), channel_id=1, source_target_pairs={{0,8},{8,16},{1,9},{9,17},{2,10},{10,18},{3,11},{11,19},{4,12},{12... | collective-permute-start | bytes 393224 | tf_op jit(solution)/shard_map/ppermute | solution.py:33
  112.3 7.7 %collective-permute-start.17 = (bf16[512,128]{1,0:T(8,128)(2,1)S(1)}, bf16[512,128]{1,0:T(8,128)(2,1)S(1)}, u32[]{:S(2)}, u32[]{:S(2)}) collective-permute-start(bf16[512,128]{1,0:T(8,128)(2,1)S(1)} %bitcast.21), channel_id=1, source_target_pairs={{0,16},{8,24},{1,17},{9,25},{2,18},{10,26},{3,19},{11,27},{4,20},{... | collective-permute-start | bytes 393224 | tf_op jit(solution)/shard_map/ppermute | solution.py:33
  116.4 9.1 %collective-permute-start.4 = (bf16[8,128,128]{2,1,0:T(8,128)(2,1)S(1)}, bf16[8,128,128]{2,1,0:T(8,128)(2,1)S(1)}, u32[]{:S(2)}, u32[]{:S(2)}) collective-permute-start(bf16[8,128,128]{2,1,0:T(8,128)(2,1)S(1)} %get-tuple-element.23), channel_id=1, source_target_pairs={{0,4},{2,6},{4,0},{6,2},{1,5},{3,7},{5,1},{7,3},{8,12},{10,14},{12... | collective-permute-start | bytes 786440 | tf_op jit(solution)/shard_map/ppermute | solution.py:33
  118.9 6.6 %collective-permute-start.5 = (bf16[8,128,128]{2,1,0:T(8,128)(2,1)S(1)}, bf16[8,128,128]{2,1,0:T(8,128)(2,1)S(1)}, u32[]{:S(2)}, u32[]{:S(2)}) collective-permute-start(bf16[8,128,128]{2,1,0:T(8,128)(2,1)S(1)} %get-tuple-element.24), channel_id=1, source_target_pairs={{0,6},{2,0},{4,2},{6,4},{1,7},{3,1},{5,3},{7,5},{8,14},{10,8},{12,... | collective-permute-start | bytes 786440 | tf_op jit(solution)/shard_map/ppermute | solution.py:33
  120.5 8.5 %collective-permute-start.19 = (bf16[2,512,128]{2,1,0:T(8,128)(2,1)S(1)}, bf16[2,512,128]{2,1,0:T(8,128)(2,1)S(1)}, u32[]{:S(2)}, u32[]{:S(2)}) collective-permute-start(bf16[2,512,128]{2,1,0:T(8,128)(2,1)S(1)} %shard_map.95.refs_4_), channel_id=1, source_target_pairs={{0,2},{2,4},{4,6},{6,0},{1,3},{3,5},{5,7},{7,1},{8,10},{10,12},{12... | collective-permute-start | bytes 786440 | tf_op jit(solution)/shard_map/ppermute | solution.py:33
  122.0 13.0 %collective-permute-start.20 = (bf16[2,512,128]{2,1,0:T(8,128)(2,1)S(1)}, bf16[2,512,128]{2,1,0:T(8,128)(2,1)S(1)}, u32[]{:S(2)}, u32[]{:S(2)}) collective-permute-start(bf16[2,512,128]{2,1,0:T(8,128)(2,1)S(1)} %shard_map.95.refs_4_), channel_id=1, source_target_pairs={{0,4},{2,6},{4,0},{6,2},{1,5},{3,7},{5,1},{7,3},{8,12},{10,14},{12... | collective-permute-start | bytes 786440 | tf_op jit(solution)/shard_map/ppermute | solution.py:33
  123.5 11.7 %collective-permute-start.21 = (bf16[2,512,128]{2,1,0:T(8,128)(2,1)S(1)}, bf16[2,512,128]{2,1,0:T(8,128)(2,1)S(1)}, u32[]{:S(2)}, u32[]{:S(2)}) collective-permute-start(bf16[2,512,128]{2,1,0:T(8,128)(2,1)S(1)} %shard_map.95.refs_4_), channel_id=1, source_target_pairs={{0,6},{2,0},{4,2},{6,4},{1,7},{3,1},{5,3},{7,5},{8,14},{10,8},{12,... | collective-permute-start | bytes 786440 | tf_op jit(solution)/shard_map/ppermute | solution.py:33
  136.3 8.9 %collective-permute-start.22 = (f32[128,512]{1,0:T(8,128)S(1)}, f32[128,512]{1,0:T(8,128)S(1)}, u32[]{:S(2)}, u32[]{:S(2)}) collective-permute-start(f32[128,512]{1,0:T(8,128)S(1)} %shard_map.98), channel_id=1, source_target_pairs={{0,1},{1,0},{2,3},{3,2},{4,5},{5,4},{6,7},{7,6},{8,9},{9,8},{10,11... | collective-permute-start | bytes 786440 | tf_op jit(solution)/shard_map/ppermute | solution.py:29
  (11 other events, 44.2 us)

commit v4 on v3

--- a/solution.py
+++ b/solution.py
@@ -31,6 +31,21 @@
 
 def shifted(x, axis, step, sources):
     return lax.ppermute(x, axis, [(i, (i + step) % 4) for i in sources])
+
+
+def crossed(x, step, phase):
+    pairs = []
+    for i in range(32):
+        at = [i // 8, i // 2 % 4, i % 2]
+        at[(i + phase) % 2] = (at[(i + phase) % 2] + step) % 4
+        pairs.append((i, at[0] * 8 + at[1] * 2 + at[2]))
+    return lax.ppermute(x, COL, pairs)
+
+
+def crossed_here():
+    first = lax.axis_index("core") == 0
+    x, y = here()
+    return jnp.where(first, x, y), jnp.where(first, y, x), first
 
 
 def dot_nt(a, b):
@@ -69,19 +84,22 @@
     out[...] = lines.reshape(ROWS, 32, 2 * TB)
 
 
-def send_x(factor, mask, *outs):
-    x, _ = here()
+def send_first(factor, mask, *outs):
+    u, _, first = crossed_here()
+    far, near = jnp.where(first, 8, 2), jnp.where(first, 2, 8)
     for d, out in enumerate(outs):
-        base = lax.rem(x + d, 4) * 8
-        for i in range(8):
-            out[i] = jnp.where(mask[base + i] == 1, factor[base + i], jnp.zeros((TB, TB), BF16))
-
-
-def pack_y(*refs):
+        base = lax.rem(u + d, 4) * far
+        for v in range(4):
+            for kk in range(2):
+                t = base + v * near + kk
+                out[2 * v + kk] = jnp.where(mask[t] == 1, factor[t], jnp.zeros((TB, TB), BF16))
+
+
+def send_second(*refs):
     came, outs = refs[:4], refs[4:]
-    _, y = here()
+    _, v, _ = crossed_here()
     for e, out in enumerate(outs):
-        base = lax.rem(y + e, 4) * 2
+        base = lax.rem(v + e, 4) * 2
         for d in SHIFTS:
             out[2 * d] = came[d][base]
             out[2 * d + 1] = came[d][base + 1]
@@ -132,9 +150,11 @@
             out[side * 4 + back(y, e)] = dot_nt(due, pieces[e][side])
 
 
-def spread(given, out):
-    for chip in range(CHIPS):
-        out[chip] = given[...]
+def pack_lines(*refs):
+    came, out = refs[:4], refs[4]
+    u, _, _ = crossed_here()
+    for d in SHIFTS:
+        out[back(u, d)] = came[d][...]
 
 
 def second_sum(came, out):
@@ -147,35 +167,40 @@
 
 
 def early_part(*refs):
-    tiles, solved, out = refs[:4], refs[4:8], refs[8]
-    x, _ = here()
+    came, solved, out, tiles = refs[:4], refs[4:8], *refs[8:]
+    _, y = here()
+    u, v, first = crossed_here()
+    for e in SHIFTS:
+        for d in SHIFTS:
+            at_u, at_v = back(u, d), back(v, e)
+            tiles[jnp.where(first, at_u * 4 + at_v, at_v * 4 + at_u)] = came[e][2 * d : 2 * d + 2]
     total = jnp.zeros((2 * TB, K), F32)
     for e in SHIFTS:
         for side in range(2):
-            block = tiles[e][pl.ds(back(x, side) * 2, 2)].reshape(2 * TB, TB)
+            block = tiles[side * 4 + back(y, e)].reshape(2 * TB, TB)
             total = total + dot_nt(block, solved[e][side])
     out[...] = total.reshape(2, TB, K)
 
 
 def late_part(tiles, solved, which):
-    x, y = here()
     total = jnp.zeros((TB, K), F32)
+    for tile in range(8):
+        total = total + dot_nt(tiles[8 + tile, which], solved[:, tile].reshape(K, TB))
+    return total
+
+
+def part_of_partner(*refs):
+    tiles, pieces, early, out, solved = refs[0], refs[1:5], *refs[5:]
+    _, v, first = crossed_here()
     for e in SHIFTS:
-        for side in range(2):
-            block = tiles[e][back(x, 2 + side) * 2 + which]
-            lines = solved[:, side * 4 + back(y, e)].reshape(K, TB)
-            total = total + dot_nt(block, lines)
-    return total
-
-
-def part_of_partner(*refs):
-    tiles, solved, early, out = refs[:4], *refs[4:]
+        source = back(v, e)
+        for u in range(4):
+            solved[jnp.where(first, u * 4 + source, source * 4 + u)] = pieces[e][u]
     which = 1 - lax.axis_index("core")
     out[...] = early[which] + late_part(tiles, solved, which)
 
 
-def own_part(*refs):
-    tiles, solved, early, solved0, given, left, result = refs[:4], *refs[4:]
+def own_part(tiles, solved, early, solved0, given, left, result):
     which = lax.axis_index("core")
     left[...] = given[...].astype(F32) - (early[which] + late_part(tiles, solved, which))
     chip = lax.axis_index("x") * 4 + lax.axis_index("y")
@@ -199,7 +224,7 @@
         out_shape=jax.ShapeDtypeStruct((ROWS, 32, 2 * TB), BF16),
         in_specs=[pl.BlockSpec((1, 2, 1, TB, K), lambda i: (0, 0, 0, 0, 0))],
         out_specs=pl.BlockSpec((ROWS, 32, 2 * TB), lambda i: (0, 0, 0)),
-        compiler_params=pltpu.CompilerParams(vmem_limit_bytes=2**22),
+        compiler_params=pltpu.CompilerParams(vmem_limit_bytes=62 * 2**20),
         name="turn",
     )(rhs_super)
     rhs0, dinv, factor_trail, rhs_super = lax.optimization_barrier(
@@ -211,18 +236,18 @@
     d1 = jnp.concatenate(
         [lax.dynamic_slice(dinv, (0, (a * ROWS + row) * TB), (TB, TB)) for a in range(2)], 1
     )
-    came = [d1] + [shifted(d1, "x", d, (2, 3)) for d in (1, 2, 3)]
+    came = [d1] + [shifted(d1, "x", d, SHIFTS) for d in (1, 2, 3)]
     [d1] = local(functools.partial(pick, 2), [((2, TB, 2 * TB), BF16)], *came)
     d1 = [d1] + [shifted(d1, "y", e, SHIFTS) for e in (1, 2, 3)]
 
     mask = mask_trail.reshape(32)
     sent = local(
-        send_x, [((8, TB, TB), BF16)] * 4, factor_trail.reshape(32, TB, TB), mask,
+        send_first, [((8, TB, TB), BF16)] * 4, factor_trail.reshape(32, TB, TB), mask,
         smem=(1,),
     )
-    came = [sent[0]] + [shifted(sent[d], "x", d, SHIFTS) for d in (1, 2, 3)]
-    sent = local(pack_y, [((8, TB, TB), BF16)] * 4, *came)
-    tiles = [sent[0]] + [shifted(sent[e], "y", e, SHIFTS) for e in (1, 2, 3)]
+    came = [sent[0]] + [crossed(sent[d], d, 0) for d in (1, 2, 3)]
+    sent = local(send_second, [((8, TB, TB), BF16)] * 4, *came)
+    tiles = [sent[0]] + [crossed(sent[e], e, 1) for e in (1, 2, 3)]
 
     [solved0] = local(
         first_rows, [((ROWS, 32, 2 * TB), BF16)], due0, dinv, dinv_other,
@@ -247,8 +272,10 @@
     part = exchange(part, "row")
     [solved1] = local(second_sum, [((ROWS, 32, TB), BF16)], part)
     solved1 = exchange(solved1, "row")
-    [solved1] = local(spread, [((CHIPS, ROWS, 32, TB), BF16)], solved1)
-    solved1 = exchange(solved1, CHIP)
+    came = {d: crossed(solved1, d, 0) for d in (2, 1, 3)}
+    [lines] = local(pack_lines, [((4, ROWS, 32, TB), BF16)], solved1, came[1], came[2], came[3])
+    came = {e: crossed(lines, e, 1) for e in (2, 1, 3)}
+    pieces = [lines, came[1], came[2], came[3]]
 
     pairs = solved0.reshape(2 * K // 4, 2 * TB)
     mine, theirs = pairs[:, :TB], partner(pairs[:, TB:])
@@ -256,15 +283,21 @@
     own0 = jnp.where(
         core == 0, jnp.stack([mine, theirs], 1), jnp.stack([theirs, mine], 1)
     ).reshape(K, TB)
-    came = [own0] + [shifted(own0, "x", d, (0, 1)) for d in (1, 2, 3)]
+    came = [own0] + [shifted(own0, "x", d, SHIFTS) for d in (1, 2, 3)]
     [pair] = local(functools.partial(pick, 0), [((2, K, TB), BF16)], *came)
     all0 = [pair] + [shifted(pair, "y", e, SHIFTS) for e in (1, 2, 3)]
 
-    [early] = local(early_part, [((2, TB, K), F32)], *tiles, *all0, flops=2**28)
-    [theirs] = local(part_of_partner, [((TB, K), F32)], *tiles, solved1, early, flops=2**27)
+    early, tiles = local(
+        early_part, [((2, TB, K), F32), ((CHIPS, 2, TB, TB), BF16)], *tiles, *all0,
+        flops=2**28,
+    )
+    theirs, solved1 = local(
+        part_of_partner, [((TB, K), F32), ((CHIPS, ROWS, 32, TB), BF16)], tiles, *pieces, early,
+        flops=2**27,
+    )
     theirs = partner(theirs)
     left, solved = local(
-        own_part, [((TB, K), F32), ((TB, K), BF16)], *tiles, solved1, early, own0,
+        own_part, [((TB, K), F32), ((TB, K), BF16)], tiles, solved1, early, own0,
         rhs_trail.reshape(TB, K), flops=2**27,
     )
     remaining = (left - theirs).astype(BF16)

time: 147 us -> 115 us (0.78)
  blocking collectives: 20 us -> 0 us
  starting transfers between devices: 75 us -> 64 us
  local copies, waits for them, and re-layouts: 3.21 us -> 0.94 us
    all_to_all x2 -> x0, blocking collectives: 20 us -> none  [exchange(): return lax.all_to_all(x, axis, split_axis=0, concat_axis=0, tiled=True)]
    ppermute x18 -> x12, starting transfers between devices: 28.8 us -> 10.5 us  [shifted(): return lax.ppermute(x, axis, [(i, (i + step) % 4) for i in sources])]
    ppermute x18 -> x12, waiting for transfers between devices: 23.4 us -> 9.13 us  [shifted(): return lax.ppermute(x, axis, [(i, (i + step) % 4) for i in sources])]
    ppermute x0 -> x12, starting transfers between devices: none -> 13.6 us  [crossed(): return lax.ppermute(x, COL, pairs)]
    ppermute x0 -> x12, waiting for transfers between devices: none -> 10.4 us  [crossed(): return lax.ppermute(x, COL, pairs)]
    ppermute x5, starting transfers between devices: 24.3 us -> 14.5 us  [partner(): return lax.ppermute(x, 'core', [(0, 1), (1, 0)])]
    all_to_all x4 -> x5, waiting for transfers between devices: 13.4 us -> 18.5 us  [exchange(): return lax.all_to_all(x, axis, split_axis=0, concat_axis=0, tiled=True)]
    all_to_all x4 -> x5, starting transfers between devices: 21.9 us -> 25.4 us  [exchange(): return lax.all_to_all(x, axis, split_axis=0, concat_axis=0, tiled=True)]
  transfers between devices with their start and end apart: 27 -> 34, of which waited for: 13 -> 12; matrix products, arithmetic and copies ran while one was open for 0% -> 0% of each run, Pallas kernels for 2% -> 6%
where the time goes in v4:
time: 115 us; the launch traced here: 114 us
  starting transfers between devices  64 us (56%)
  waiting for transfers between devices  38.9 us (34%)
  Pallas kernels  8.8 us (8%)
    all_to_all x5, starting transfers between devices, exchange(): return lax.all_to_all(x, axis, split_axis=0, concat_axis=0, tiled=True)  25.4 us
    all_to_all x5, waiting for transfers between devices, exchange(): return lax.all_to_all(x, axis, split_axis=0, concat_axis=0, tiled=True)  18.5 us
    ppermute x5, starting transfers between devices, partner(): return lax.ppermute(x, 'core', [(0, 1), (1, 0)])  14.5 us
    ppermute x12, starting transfers between devices, crossed(): return lax.ppermute(x, COL, pairs)  13.6 us
    ppermute x12, starting transfers between devices, shifted(): return lax.ppermute(x, axis, [(i, (i + step) % 4) for i in sources])  10.5 us
    ppermute x12, waiting for transfers between devices, crossed(): return lax.ppermute(x, COL, pairs)  10.4 us
    ppermute x12, waiting for transfers between devices, shifted(): return lax.ppermute(x, axis, [(i, (i + step) % 4) for i in sources])  9.13 us
    pallas_call x13, Pallas kernels, local(): pl.pallas_call(kernel, out_shape=[jax.ShapeDtypeStruct(shape, dtype) for...  7.01 us
  transfers between devices with their start and end apart: 34, of which 12 were waited for; matrix products, arithmetic and copies ran while one was open for 0% of the time, Pallas kernels for 6%

profile of v4, /device:TPU:1, one launch (start us, length us, event | category | flops | bytes accessed | tf_op | source)
XLA Modules:
  0.0 114.3 jit_solution(3574873776553161566)
XLA Ops:
  0.6 1.8 %turn.1 = bf16[8,32,256]{2,1,0:T(8,128)(2,1)} custom-call(bf16[2,2,1,128,512]{4,3,2,1,0:T(8,128)(2,1)} %given.1), custom_call_target="tpu_custom_call" | custom-call | tf_op jit(solution)/shard_map/turn/pallas_call | solution.py:221
  2.4 3.2 %collective-permute-start.6 = (bf16[128,2048]{1,0:T(8,128)(2,1)S(1)}, bf16[128,2048]{1,0:T(8,128)(2,1)S(1)}, u32[]{:S(2)}, u32[]{:S(2)}) collective-permute-start(bf16[128,2048]{1,0:T(8,128)(2,1)S(1)} %bitcast.26), channel_id=1, source_target_pairs={{0,1},{1,0},{2,3},{3,2},{4,5},{5,4},{6,7},{7,6},{8,9},{9,8},{10,11... | collective-permute-start | bytes 1572872 | tf_op jit(solution)/shard_map/ppermute | solution.py:29
  5.8 1.9 %collective-permute-start.17 = (bf16[128,256]{1,0:T(8,128)(2,1)S(1)}, bf16[128,256]{1,0:T(8,128)(2,1)S(1)}, u32[]{:S(2)}, u32[]{:S(2)}) collective-permute-start(bf16[128,256]{1,0:T(8,128)(2,1)S(1)} %pad_maximum_fusion.refs_0_), channel_id=1, source_target_pairs={{0,16},{8,24},{16,0},{24,8},{1,17},{9,25},{17,1},{25,9},{2,18},{10... | collective-permute-start | bytes 196616 | tf_op jit(solution)/shard_map/ppermute | solution.py:33
  8.9 8.2 %all-to-all-start = ((bf16[8,32,256]{2,1,0:T(8,128)(2,1)}), bf16[8,32,256]{2,1,0:T(8,128)(2,1)S(1)}, u32[]{:S(2)}, u32[]{:S(2)}) async-start(bf16[8,32,256]{2,1,0:T(8,128)(2,1)} %turn.1), calls=%async_computation | async-start | bytes 262144 | tf_op jit(solution)/shard_map/all_to_all | solution.py:25
  17.2 7.7 %all-to-all-done.due = bf16[8,32,256]{2,1,0:T(8,128)(2,1)S(1)} async-done(((bf16[8,32,256]{2,1,0:T(8,128)(2,1)}), bf16[8,32,256]{2,1,0:T(8,128)(2,1)S(1)}, u32[]{:S(2)}, u32[]{:S(2)}) %all-to-all-start) | async-done | bytes 131104 | tf_op jit(solution)/shard_map/all_to_all | solution.py:25
  25.9 3.5 %all-to-all-start.1 = ((bf16[8,32,256]{2,1,0:T(8,128)(2,1)}), bf16[8,32,256]{2,1,0:T(8,128)(2,1)S(1)}, u32[]{:S(2)}, u32[]{:S(2)}) async-start(bf16[8,32,256]{2,1,0:T(8,128)(2,1)} %shard_map.88), calls=%async_computation.1 | async-start | bytes 262144 | tf_op jit(solution)/shard_map/all_to_all | solution.py:25
  29.6 2.5 %collective-permute-start.14 = (bf16[256,128]{1,0:T(8,128)(2,1)S(1)}, bf16[256,128]{1,0:T(8,128)(2,1)S(1)}, u32[]{:S(2)}, u32[]{:S(2)}) collective-permute-start(bf16[256,128]{1,0:T(8,128)(2,1)S(1)} %bitcast_multiply_fusion.own), channel_id=1, source_target_pairs={{0,1},{1,0},{2,3},{3,2},{4,5},{5,4},{6,7},{7,6},{8,9},{9,8},{10,11... | collective-permute-start | bytes 196616 | tf_op jit(solution)/shard_map/ppermute | solution.py:29
  34.9 2.6 %collective-permute-start.1 = (bf16[8,128,128]{2,1,0:T(8,128)(2,1)S(1)}, bf16[8,128,128]{2,1,0:T(8,128)(2,1)S(1)}, u32[]{:S(2)}, u32[]{:S(2)}) collective-permute-start(bf16[8,128,128]{2,1,0:T(8,128)(2,1)S(1)} %get-tuple-element.23), channel_id=1, source_target_pairs={{0,16},{1,5},{2,18},{3,7},{4,20},{5,1},{6,22},{7,3},{8,24},{9,13},... | collective-permute-start | bytes 786440 | tf_op jit(solution)/shard_map/ppermute | solution.py:42
  37.7 2.2 %collective-permute-start.20 = (bf16[2,128,256]{2,1,0:T(8,128)(2,1)S(1)}, bf16[2,128,256]{2,1,0:T(8,128)(2,1)S(1)}, u32[]{:S(2)}, u32[]{:S(2)}) collective-permute-start(bf16[2,128,256]{2,1,0:T(8,128)(2,1)S(1)} %shard_map.93.refs_0_), channel_id=1, source_target_pairs={{0,4},{2,6},{4,0},{6,2},{1,5},{3,7},{5,1},{7,3},{8,12},{10,14},{12... | collective-permute-start | bytes 393224 | tf_op jit(solution)/shard_map/ppermute | solution.py:33
  41.3 3.8 %all-to-all-start.2 = ((f32[16,16,256]{2,1,0:T(8,128)}), f32[16,16,256]{2,1,0:T(8,128)S(1)}, u32[]{:S(2)}, u32[]{:S(2)}) async-start(f32[16,16,256]{2,1,0:T(8,128)} %shard_map.91), calls=%async_computation.2 | async-start | bytes 524288 | tf_op jit(solution)/shard_map/all_to_all | solution.py:25
  45.1 2.1 %collective-permute-done.19.refs_1_ = bf16[2,128,256]{2,1,0:T(8,128)(2,1)S(1)} collective-permute-done((bf16[2,128,256]{2,1,0:T(8,128)(2,1)S(1)}, bf16[2,128,256]{2,1,0:T(8,128)(2,1)S(1)}, u32[]{:S(2)}, u32[]{:S(2)}) %collective-permute-start.19) | collective-permute-done | bytes 131104 | tf_op jit(solution)/shard_map/ppermute | solution.py:33
  47.2 1.8 %collective-permute-start.2 = (bf16[8,128,128]{2,1,0:T(8,128)(2,1)S(1)}, bf16[8,128,128]{2,1,0:T(8,128)(2,1)S(1)}, u32[]{:S(2)}, u32[]{:S(2)}) collective-permute-start(bf16[8,128,128]{2,1,0:T(8,128)(2,1)S(1)} %get-tuple-element.24), channel_id=1, source_target_pairs={{0,24},{1,7},{2,26},{3,1},{4,28},{5,3},{6,30},{7,5},{8,0},{9,15},{... | collective-permute-start | bytes 786440 | tf_op jit(solution)/shard_map/ppermute | solution.py:42
  50.1 2.4 %all-to-all-done.2.came = f32[16,16,256]{2,1,0:T(8,128)S(1)} async-done(((f32[16,16,256]{2,1,0:T(8,128)}), f32[16,16,256]{2,1,0:T(8,128)S(1)}, u32[]{:S(2)}, u32[]{:S(2)}) %all-to-all-start.2) | async-done | bytes 262176 | tf_op jit(solution)/shard_map/all_to_all | solution.py:25
  52.5 2.6 %collective-permute-start.15 = (bf16[16,256]{1,0:T(8,128)(2,1)S(1)}, bf16[16,256]{1,0:T(8,128)(2,1)S(1)}, u32[]{:S(2)}, u32[]{:S(2)}) collective-permute-start(bf16[16,256]{1,0:T(8,128)(2,1)S(1)} %shard_map.92.mine), channel_id=1, source_target_pairs={{0,1},{1,0},{2,3},{3,2},{4,5},{5,4},{6,7},{7,6},{8,9},{9,8},{10,11... | collective-permute-start | bytes 24584 | tf_op jit(solution)/shard_map/ppermute | solution.py:29
  56.8 6.6 %all-to-all-start.3 = ((f32[8,32,128]{2,1,0:T(8,128)}), f32[8,32,128]{2,1,0:T(8,128)S(1)}, u32[]{:S(2)}, u32[]{:S(2)}) async-start(f32[8,32,128]{2,1,0:T(8,128)} %shard_map.94), calls=%async_computation.3 | async-start | bytes 262144 | tf_op jit(solution)/shard_map/all_to_all | solution.py:25
  63.5 1.9 %collective-permute-start.9 = (bf16[512,128]{1,0:T(8,128)(2,1)S(1)}, bf16[512,128]{1,0:T(8,128)(2,1)S(1)}, u32[]{:S(2)}, u32[]{:S(2)}) collective-permute-start(bf16[512,128]{1,0:T(8,128)(2,1)S(1)} %bitcast.20), channel_id=1, source_target_pairs={{0,16},{8,24},{16,0},{24,8},{1,17},{9,25},{17,1},{25,9},{2,18},{10... | collective-permute-start | bytes 393224 | tf_op jit(solution)/shard_map/ppermute | solution.py:33
  67.1 4.3 %all-to-all-done.3.came = f32[8,32,128]{2,1,0:T(8,128)S(1)} async-done(((f32[8,32,128]{2,1,0:T(8,128)}), f32[8,32,128]{2,1,0:T(8,128)S(1)}, u32[]{:S(2)}, u32[]{:S(2)}) %all-to-all-start.3) | async-done | bytes 131104 | tf_op jit(solution)/shard_map/all_to_all | solution.py:25
  72.0 3.4 %all-to-all-start.4 = ((bf16[8,32,128]{2,1,0:T(8,128)(2,1)}), bf16[8,32,128]{2,1,0:T(8,128)(2,1)S(1)}, u32[]{:S(2)}, u32[]{:S(2)}) async-start(bf16[8,32,128]{2,1,0:T(8,128)(2,1)} %shard_map.95), calls=%async_computation.4 | async-start | bytes 131072 | tf_op jit(solution)/shard_map/all_to_all | solution.py:25
  78.3 4.2 %all-to-all-done.4.refs_0_ = bf16[8,32,128]{2,1,0:T(8,128)(2,1)S(1)} async-done(((bf16[8,32,128]{2,1,0:T(8,128)(2,1)}), bf16[8,32,128]{2,1,0:T(8,128)(2,1)S(1)}, u32[]{:S(2)}, u32[]{:S(2)}) %all-to-all-start.4) | async-done | bytes 65568 | tf_op jit(solution)/shard_map/all_to_all | solution.py:25
  82.6 1.7 %collective-permute-start.23 = (bf16[8,32,128]{2,1,0:T(8,128)(2,1)S(1)}, bf16[8,32,128]{2,1,0:T(8,128)(2,1)S(1)}, u32[]{:S(2)}, u32[]{:S(2)}) collective-permute-start(bf16[8,32,128]{2,1,0:T(8,128)(2,1)S(1)} %all-to-all-done.4.refs_0_), channel_id=1, source_target_pairs={{0,16},{1,5},{2,18},{3,7},{4,20},{5,1},{6,22},{7,3},{8,24},{9,13},... | collective-permute-start | bytes 196616 | tf_op jit(solution)/shard_map/ppermute | solution.py:42
  84.4 6.8 %collective-permute-done.22.refs_1_ = bf16[8,32,128]{2,1,0:T(8,128)(2,1)S(1)} collective-permute-done((bf16[8,32,128]{2,1,0:T(8,128)(2,1)S(1)}, bf16[8,32,128]{2,1,0:T(8,128)(2,1)S(1)}, u32[]{:S(2)}, u32[]{:S(2)}) %collective-permute-start.22) | collective-permute-done | bytes 65568 | tf_op jit(solution)/shard_map/ppermute | solution.py:42
  91.2 3.1 %collective-permute-done.24.refs_3_ = bf16[8,32,128]{2,1,0:T(8,128)(2,1)S(1)} collective-permute-done((bf16[8,32,128]{2,1,0:T(8,128)(2,1)S(1)}, bf16[8,32,128]{2,1,0:T(8,128)(2,1)S(1)}, u32[]{:S(2)}, u32[]{:S(2)}) %collective-permute-start.24) | collective-permute-done | bytes 65568 | tf_op jit(solution)/shard_map/ppermute | solution.py:42
  99.8 4.8 %collective-permute-done.13.refs_7_ = bf16[2,512,128]{2,1,0:T(8,128)(2,1)S(1)} collective-permute-done((bf16[2,512,128]{2,1,0:T(8,128)(2,1)S(1)}, bf16[2,512,128]{2,1,0:T(8,128)(2,1)S(1)}, u32[]{:S(2)}, u32[]{:S(2)}) %collective-permute-start.13) | collective-permute-done | bytes 262176 | tf_op jit(solution)/shard_map/ppermute | solution.py:33
  106.3 6.2 %collective-permute-start.28 = (f32[128,512]{1,0:T(8,128)S(1)}, f32[128,512]{1,0:T(8,128)S(1)}, u32[]{:S(2)}, u32[]{:S(2)}) collective-permute-start(f32[128,512]{1,0:T(8,128)S(1)} %get-tuple-element.37), channel_id=1, source_target_pairs={{0,1},{1,0},{2,3},{3,2},{4,5},{5,4},{6,7},{7,6},{8,9},{9,8},{10,11... | collective-permute-start | bytes 786440 | tf_op jit(solution)/shard_map/ppermute | solution.py:29
  (82 shorter events, 24.3 us)
Async XLA Ops:
  2.4 22.4 %collective-permute-start.6 = (bf16[128,2048]{1,0:T(8,128)(2,1)S(1)}, bf16[128,2048]{1,0:T(8,128)(2,1)S(1)}, u32[]{:S(2)}, u32[]{:S(2)}) collective-permute-start(bf16[128,2048]{1,0:T(8,128)(2,1)S(1)} %bitcast.26), channel_id=1, source_target_pairs={{0,1},{1,0},{2,3},{3,2},{4,5},{5,4},{6,7},{7,6},{8,9},{9,8},{10,11... | collective-permute-start | bytes 1572872 | tf_op jit(solution)/shard_map/ppermute | solution.py:29
  5.7 29.2 %collective-permute-start.16 = (bf16[128,256]{1,0:T(8,128)(2,1)S(1)}, bf16[128,256]{1,0:T(8,128)(2,1)S(1)}, u32[]{:S(2)}, u32[]{:S(2)}) collective-permute-start(bf16[128,256]{1,0:T(8,128)(2,1)S(1)} %pad_maximum_fusion.refs_0_), channel_id=1, source_target_pairs={{0,8},{8,16},{16,24},{24,0},{1,9},{9,17},{17,25},{25,1},{2,10},{10... | collective-permute-start | bytes 196616 | tf_op jit(solution)/shard_map/ppermute | solution.py:33
  5.8 31.8 %collective-permute-start.17 = (bf16[128,256]{1,0:T(8,128)(2,1)S(1)}, bf16[128,256]{1,0:T(8,128)(2,1)S(1)}, u32[]{:S(2)}, u32[]{:S(2)}) collective-permute-start(bf16[128,256]{1,0:T(8,128)(2,1)S(1)} %pad_maximum_fusion.refs_0_), channel_id=1, source_target_pairs={{0,16},{8,24},{16,0},{24,8},{1,17},{9,25},{17,1},{25,9},{2,18},{10... | collective-permute-start | bytes 196616 | tf_op jit(solution)/shard_map/ppermute | solution.py:33
  7.7 29.8 %collective-permute-start.18 = (bf16[128,256]{1,0:T(8,128)(2,1)S(1)}, bf16[128,256]{1,0:T(8,128)(2,1)S(1)}, u32[]{:S(2)}, u32[]{:S(2)}) collective-permute-start(bf16[128,256]{1,0:T(8,128)(2,1)S(1)} %pad_maximum_fusion.refs_0_), channel_id=1, source_target_pairs={{0,24},{8,0},{16,8},{24,16},{1,25},{9,1},{17,9},{25,17},{2,26},{10... | collective-permute-start | bytes 196616 | tf_op jit(solution)/shard_map/ppermute | solution.py:33
  8.9 15.9 %all-to-all-start = ((bf16[8,32,256]{2,1,0:T(8,128)(2,1)}), bf16[8,32,256]{2,1,0:T(8,128)(2,1)S(1)}, u32[]{:S(2)}, u32[]{:S(2)}) async-start(bf16[8,32,256]{2,1,0:T(8,128)(2,1)} %turn.1), calls=%async_computation | async-start | bytes 262144 | tf_op jit(solution)/shard_map/all_to_all | solution.py:25
  25.9 14.4 %all-to-all-start.1 = ((bf16[8,32,256]{2,1,0:T(8,128)(2,1)}), bf16[8,32,256]{2,1,0:T(8,128)(2,1)S(1)}, u32[]{:S(2)}, u32[]{:S(2)}) async-start(bf16[8,32,256]{2,1,0:T(8,128)(2,1)} %shard_map.88), calls=%async_computation.1 | async-start | bytes 262144 | tf_op jit(solution)/shard_map/all_to_all | solution.py:25
  29.6 10.4 %collective-permute-start.14 = (bf16[256,128]{1,0:T(8,128)(2,1)S(1)}, bf16[256,128]{1,0:T(8,128)(2,1)S(1)}, u32[]{:S(2)}, u32[]{:S(2)}) collective-permute-start(bf16[256,128]{1,0:T(8,128)(2,1)S(1)} %bitcast_multiply_fusion.own), channel_id=1, source_target_pairs={{0,1},{1,0},{2,3},{3,2},{4,5},{5,4},{6,7},{7,6},{8,9},{9,8},{10,11... | collective-permute-start | bytes 196616 | tf_op jit(solution)/shard_map/ppermute | solution.py:29
  33.6 31.9 %collective-permute-start = (bf16[8,128,128]{2,1,0:T(8,128)(2,1)S(1)}, bf16[8,128,128]{2,1,0:T(8,128)(2,1)S(1)}, u32[]{:S(2)}, u32[]{:S(2)}) collective-permute-start(bf16[8,128,128]{2,1,0:T(8,128)(2,1)S(1)} %get-tuple-element.22), channel_id=1, source_target_pairs={{0,8},{1,3},{2,10},{3,5},{4,12},{5,7},{6,14},{7,1},{8,16},{9,11},{... | collective-permute-start | bytes 786440 | tf_op jit(solution)/shard_map/ppermute | solution.py:42
  34.9 31.7 %collective-permute-start.1 = (bf16[8,128,128]{2,1,0:T(8,128)(2,1)S(1)}, bf16[8,128,128]{2,1,0:T(8,128)(2,1)S(1)}, u32[]{:S(2)}, u32[]{:S(2)}) collective-permute-start(bf16[8,128,128]{2,1,0:T(8,128)(2,1)S(1)} %get-tuple-element.23), channel_id=1, source_target_pairs={{0,16},{1,5},{2,18},{3,7},{4,20},{5,1},{6,22},{7,3},{8,24},{9,13},... | collective-permute-start | bytes 786440 | tf_op jit(solution)/shard_map/ppermute | solution.py:42
  37.7 12.2 %collective-permute-start.20 = (bf16[2,128,256]{2,1,0:T(8,128)(2,1)S(1)}, bf16[2,128,256]{2,1,0:T(8,128)(2,1)S(1)}, u32[]{:S(2)}, u32[]{:S(2)}) collective-permute-start(bf16[2,128,256]{2,1,0:T(8,128)(2,1)S(1)} %shard_map.93.refs_0_), channel_id=1, source_target_pairs={{0,4},{2,6},{4,0},{6,2},{1,5},{3,7},{5,1},{7,3},{8,12},{10,14},{12... | collective-permute-start | bytes 393224 | tf_op jit(solution)/shard_map/ppermute | solution.py:33
  39.9 12.5 %collective-permute-start.21 = (bf16[2,128,256]{2,1,0:T(8,128)(2,1)S(1)}, bf16[2,128,256]{2,1,0:T(8,128)(2,1)S(1)}, u32[]{:S(2)}, u32[]{:S(2)}) collective-permute-start(bf16[2,128,256]{2,1,0:T(8,128)(2,1)S(1)} %shard_map.93.refs_0_), channel_id=1, source_target_pairs={{0,6},{2,0},{4,2},{6,4},{1,7},{3,1},{5,3},{7,5},{8,14},{10,8},{12,... | collective-permute-start | bytes 393224 | tf_op jit(solution)/shard_map/ppermute | solution.py:33
  41.3 11.2 %all-to-all-start.2 = ((f32[16,16,256]{2,1,0:T(8,128)}), f32[16,16,256]{2,1,0:T(8,128)S(1)}, u32[]{:S(2)}, u32[]{:S(2)}) async-start(f32[16,16,256]{2,1,0:T(8,128)} %shard_map.91), calls=%async_computation.2 | async-start | bytes 524288 | tf_op jit(solution)/shard_map/all_to_all | solution.py:25
  47.2 19.4 %collective-permute-start.2 = (bf16[8,128,128]{2,1,0:T(8,128)(2,1)S(1)}, bf16[8,128,128]{2,1,0:T(8,128)(2,1)S(1)}, u32[]{:S(2)}, u32[]{:S(2)}) collective-permute-start(bf16[8,128,128]{2,1,0:T(8,128)(2,1)S(1)} %get-tuple-element.24), channel_id=1, source_target_pairs={{0,24},{1,7},{2,26},{3,1},{4,28},{5,3},{6,30},{7,5},{8,0},{9,15},{... | collective-permute-start | bytes 786440 | tf_op jit(solution)/shard_map/ppermute | solution.py:42
  49.9 13.5 %collective-permute-start.7 = (bf16[256,128]{1,0:T(8,128)(2,1)S(1)}, bf16[256,128]{1,0:T(8,128)(2,1)S(1)}, u32[]{:S(2)}, u32[]{:S(2)}) collective-permute-start(bf16[256,128]{1,0:T(8,128)(2,1)S(1)} %get-tuple-element.41), channel_id=1, source_target_pairs={{0,1},{1,0},{2,3},{3,2},{4,5},{5,4},{6,7},{7,6},{8,9},{9,8},{10,11... | collective-permute-start | bytes 196616 | tf_op jit(solution)/shard_map/ppermute | solution.py:29
  56.8 14.5 %all-to-all-start.3 = ((f32[8,32,128]{2,1,0:T(8,128)}), f32[8,32,128]{2,1,0:T(8,128)S(1)}, u32[]{:S(2)}, u32[]{:S(2)}) async-start(f32[8,32,128]{2,1,0:T(8,128)} %shard_map.94), calls=%async_computation.3 | async-start | bytes 262144 | tf_op jit(solution)/shard_map/all_to_all | solution.py:25
  63.4 13.0 %collective-permute-start.8 = (bf16[512,128]{1,0:T(8,128)(2,1)S(1)}, bf16[512,128]{1,0:T(8,128)(2,1)S(1)}, u32[]{:S(2)}, u32[]{:S(2)}) collective-permute-start(bf16[512,128]{1,0:T(8,128)(2,1)S(1)} %bitcast.19), channel_id=1, source_target_pairs={{0,8},{8,16},{16,24},{24,0},{1,9},{9,17},{17,25},{25,1},{2,10},{10... | collective-permute-start | bytes 393224 | tf_op jit(solution)/shard_map/ppermute | solution.py:33
  63.5 14.6 %collective-permute-start.9 = (bf16[512,128]{1,0:T(8,128)(2,1)S(1)}, bf16[512,128]{1,0:T(8,128)(2,1)S(1)}, u32[]{:S(2)}, u32[]{:S(2)}) collective-permute-start(bf16[512,128]{1,0:T(8,128)(2,1)S(1)} %bitcast.20), channel_id=1, source_target_pairs={{0,16},{8,24},{16,0},{24,8},{1,17},{9,25},{17,1},{25,9},{2,18},{10... | collective-permute-start | bytes 393224 | tf_op jit(solution)/shard_map/ppermute | solution.py:33
  65.5 12.6 %collective-permute-start.10 = (bf16[512,128]{1,0:T(8,128)(2,1)S(1)}, bf16[512,128]{1,0:T(8,128)(2,1)S(1)}, u32[]{:S(2)}, u32[]{:S(2)}) collective-permute-start(bf16[512,128]{1,0:T(8,128)(2,1)S(1)} %bitcast.21), channel_id=1, source_target_pairs={{0,24},{8,0},{16,8},{24,16},{1,25},{9,1},{17,9},{25,17},{2,26},{10... | collective-permute-start | bytes 393224 | tf_op jit(solution)/shard_map/ppermute | solution.py:33
  66.7 15.9 %collective-permute-start.3 = (bf16[8,128,128]{2,1,0:T(8,128)(2,1)S(1)}, bf16[8,128,128]{2,1,0:T(8,128)(2,1)S(1)}, u32[]{:S(2)}, u32[]{:S(2)}) collective-permute-start(bf16[8,128,128]{2,1,0:T(8,128)(2,1)S(1)} %get-tuple-element.26), channel_id=1, source_target_pairs={{0,2},{1,9},{2,4},{3,11},{4,6},{5,13},{6,0},{7,15},{8,10},{9,17},{... | collective-permute-start | bytes 786440 | tf_op jit(solution)/shard_map/ppermute | solution.py:42
  72.0 10.5 %all-to-all-start.4 = ((bf16[8,32,128]{2,1,0:T(8,128)(2,1)}), bf16[8,32,128]{2,1,0:T(8,128)(2,1)S(1)}, u32[]{:S(2)}, u32[]{:S(2)}) async-start(bf16[8,32,128]{2,1,0:T(8,128)(2,1)} %shard_map.95), calls=%async_computation.4 | async-start | bytes 131072 | tf_op jit(solution)/shard_map/all_to_all | solution.py:25
  75.4 20.2 %collective-permute-start.4 = (bf16[8,128,128]{2,1,0:T(8,128)(2,1)S(1)}, bf16[8,128,128]{2,1,0:T(8,128)(2,1)S(1)}, u32[]{:S(2)}, u32[]{:S(2)}) collective-permute-start(bf16[8,128,128]{2,1,0:T(8,128)(2,1)S(1)} %get-tuple-element.27), channel_id=1, source_target_pairs={{0,4},{1,17},{2,6},{3,19},{4,0},{5,21},{6,2},{7,23},{8,12},{9,25},... | collective-permute-start | bytes 786440 | tf_op jit(solution)/shard_map/ppermute | solution.py:42
  76.5 19.2 %collective-permute-start.5 = (bf16[8,128,128]{2,1,0:T(8,128)(2,1)S(1)}, bf16[8,128,128]{2,1,0:T(8,128)(2,1)S(1)}, u32[]{:S(2)}, u32[]{:S(2)}) collective-permute-start(bf16[8,128,128]{2,1,0:T(8,128)(2,1)S(1)} %get-tuple-element.28), channel_id=1, source_target_pairs={{0,6},{1,25},{2,0},{3,27},{4,2},{5,29},{6,4},{7,31},{8,14},{9,1},{... | collective-permute-start | bytes 786440 | tf_op jit(solution)/shard_map/ppermute | solution.py:42
  78.1 19.0 %collective-permute-start.11 = (bf16[2,512,128]{2,1,0:T(8,128)(2,1)S(1)}, bf16[2,512,128]{2,1,0:T(8,128)(2,1)S(1)}, u32[]{:S(2)}, u32[]{:S(2)}) collective-permute-start(bf16[2,512,128]{2,1,0:T(8,128)(2,1)S(1)} %shard_map.89.refs_4_), channel_id=1, source_target_pairs={{0,2},{2,4},{4,6},{6,0},{1,3},{3,5},{5,7},{7,1},{8,10},{10,12},{12... | collective-permute-start | bytes 786440 | tf_op jit(solution)/shard_map/ppermute | solution.py:33
  94.3 10.3 %collective-permute-start.13 = (bf16[2,512,128]{2,1,0:T(8,128)(2,1)S(1)}, bf16[2,512,128]{2,1,0:T(8,128)(2,1)S(1)}, u32[]{:S(2)}, u32[]{:S(2)}) collective-permute-start(bf16[2,512,128]{2,1,0:T(8,128)(2,1)S(1)} %shard_map.89.refs_4_), channel_id=1, source_target_pairs={{0,6},{2,0},{4,2},{6,4},{1,7},{3,1},{5,3},{7,5},{8,14},{10,8},{12,... | collective-permute-start | bytes 786440 | tf_op jit(solution)/shard_map/ppermute | solution.py:33
  (17 other events, 132.6 us)

commit v5 on v4

--- a/solution.py
+++ b/solution.py
@@ -31,6 +31,18 @@
 
 def shifted(x, axis, step, sources):
     return lax.ppermute(x, axis, [(i, (i + step) % 4) for i in sources])
+
+
+def crossed_groups():
+    groups = []
+    for core in range(2):
+        for other in range(4):
+            group = []
+            for along in range(4):
+                x, y = (along, other) if core == 0 else (other, along)
+                group += [r * 32 + x * 8 + y * 2 + core for r in range(ROWS)]
+            groups.append(group)
+    return groups
 
 
 def crossed(x, step, phase):
@@ -150,20 +162,13 @@
             out[side * 4 + back(y, e)] = dot_nt(due, pieces[e][side])
 
 
-def pack_lines(*refs):
-    came, out = refs[:4], refs[4]
-    u, _, _ = crossed_here()
-    for d in SHIFTS:
-        out[back(u, d)] = came[d][...]
-
-
 def second_sum(came, out):
     total = came[0]
     for r in range(1, ROWS):
         total = total + came[r]
     total = total.astype(BF16)
-    for r in range(ROWS):
-        out[r] = total
+    for place in range(4 * ROWS):
+        out[place] = total
 
 
 def early_part(*refs):
@@ -270,10 +275,10 @@
         flops=2**25,
     )
     part = exchange(part, "row")
-    [solved1] = local(second_sum, [((ROWS, 32, TB), BF16)], part)
-    solved1 = exchange(solved1, "row")
-    came = {d: crossed(solved1, d, 0) for d in (2, 1, 3)}
-    [lines] = local(pack_lines, [((4, ROWS, 32, TB), BF16)], solved1, came[1], came[2], came[3])
+    [solved1] = local(second_sum, [((4 * ROWS, 32, TB), BF16)], part)
+    lines = lax.all_to_all(
+        solved1, ("row", *COL), 0, 0, axis_index_groups=crossed_groups(), tiled=True
+    ).reshape(4, ROWS, 32, TB)
     came = {e: crossed(lines, e, 1) for e in (2, 1, 3)}
     pieces = [lines, came[1], came[2], came[3]]
 

time: 115 us -> 119 us (1.035)
  starting transfers between devices: 64 us -> 74.5 us
  waiting for transfers between devices: 38.9 us -> 31.2 us
    ppermute x12, starting transfers between devices: 10.5 us -> 19.6 us  [shifted(): return lax.ppermute(x, axis, [(i, (i + step) % 4) for i in sources])]
    ppermute x12 -> x9, waiting for transfers between devices: 10.4 us -> 2.31 us  [crossed(): return lax.ppermute(x, COL, pairs)]
    all_to_all x5 -> x4, starting transfers between devices: 25.4 us -> 20.2 us  [exchange(): return lax.all_to_all(x, axis, split_axis=0, concat_axis=0, tiled=True)]
    all_to_all x0 -> x1, starting transfers between devices: none -> 4.91 us  [steps(): lax.all_to_all(solved1, ('row', *COL), 0, 0, axis_index_groups=crossed_gr...]
    ppermute x5, starting transfers between devices: 14.5 us -> 18.5 us  [partner(): return lax.ppermute(x, 'core', [(0, 1), (1, 0)])]
    ppermute x12 -> x9, starting transfers between devices: 13.6 us -> 11.2 us  [crossed(): return lax.ppermute(x, COL, pairs)]
    ppermute x12, waiting for transfers between devices: 9.13 us -> 10.3 us  [shifted(): return lax.ppermute(x, axis, [(i, (i + step) % 4) for i in sources])]
    all_to_all x5 -> x4, waiting for transfers between devices: 18.5 us -> 17.7 us  [exchange(): return lax.all_to_all(x, axis, split_axis=0, concat_axis=0, tiled=True)]
  transfers between devices with their start and end apart: 34 -> 31, of which waited for: 12 -> 15; matrix products, arithmetic and copies ran while one was open for 0% -> 0% of each run, Pallas kernels for 6% -> 4%
where the time goes in v5:
time: 119 us; the launch traced here: 118 us
  starting transfers between devices  74.5 us (63%)
  waiting for transfers between devices  31.2 us (26%)
  Pallas kernels  8.88 us (7%)
  local copies, waits for them, and re-layouts  1.87 us (2%)
    all_to_all x4, starting transfers between devices, exchange(): return lax.all_to_all(x, axis, split_axis=0, concat_axis=0, tiled=True)  20.2 us
    ppermute x12, starting transfers between devices, shifted(): return lax.ppermute(x, axis, [(i, (i + step) % 4) for i in sources])  19.6 us
    ppermute x5, starting transfers between devices, partner(): return lax.ppermute(x, 'core', [(0, 1), (1, 0)])  18.5 us
    all_to_all x4, waiting for transfers between devices, exchange(): return lax.all_to_all(x, axis, split_axis=0, concat_axis=0, tiled=True)  17.7 us
    ppermute x9, starting transfers between devices, crossed(): return lax.ppermute(x, COL, pairs)  11.2 us
    ppermute x12, waiting for transfers between devices, shifted(): return lax.ppermute(x, axis, [(i, (i + step) % 4) for i in sources])  10.3 us
    pallas_call x12, Pallas kernels, local(): pl.pallas_call(kernel, out_shape=[jax.ShapeDtypeStruct(shape, dtype) for...  7.09 us
    all_to_all x1, starting transfers between devices, steps(): lax.all_to_all(solved1, ('row', *COL), 0, 0, axis_index_groups=crossed_gr...  4.91 us
  transfers between devices with their start and end apart: 31, of which 15 were waited for; matrix products, arithmetic and copies ran while one was open for 0% of the time, Pallas kernels for 4%

profile of v5, /device:TPU:1, one launch (start us, length us, event | category | flops | bytes accessed | tf_op | source)
XLA Modules:
  0.0 118.1 jit_solution(6970215897399678204)
XLA Ops:
  0.6 1.8 %turn.1 = bf16[8,32,256]{2,1,0:T(8,128)(2,1)} custom-call(bf16[2,2,1,128,512]{4,3,2,1,0:T(8,128)(2,1)} %given.1), custom_call_target="tpu_custom_call" | custom-call | tf_op jit(solution)/shard_map/turn/pallas_call | solution.py:226
  2.4 3.2 %collective-permute-start.6 = (bf16[128,2048]{1,0:T(8,128)(2,1)S(1)}, bf16[128,2048]{1,0:T(8,128)(2,1)S(1)}, u32[]{:S(2)}, u32[]{:S(2)}) collective-permute-start(bf16[128,2048]{1,0:T(8,128)(2,1)S(1)} %bitcast.31), channel_id=1, source_target_pairs={{0,1},{1,0},{2,3},{3,2},{4,5},{5,4},{6,7},{7,6},{8,9},{9,8},{10,11... | collective-permute-start | bytes 1572872 | tf_op jit(solution)/shard_map/ppermute | solution.py:29
  5.6 6.5 %all-to-all-start = ((bf16[8,32,256]{2,1,0:T(8,128)(2,1)}), bf16[8,32,256]{2,1,0:T(8,128)(2,1)S(1)}, u32[]{:S(2)}, u32[]{:S(2)}) async-start(bf16[8,32,256]{2,1,0:T(8,128)(2,1)} %turn.1), calls=%async_computation | async-start | bytes 262144 | tf_op jit(solution)/shard_map/all_to_all | solution.py:25
  12.2 8.4 %all-to-all-done.due = bf16[8,32,256]{2,1,0:T(8,128)(2,1)S(1)} async-done(((bf16[8,32,256]{2,1,0:T(8,128)(2,1)}), bf16[8,32,256]{2,1,0:T(8,128)(2,1)S(1)}, u32[]{:S(2)}, u32[]{:S(2)}) %all-to-all-start) | async-done | bytes 131104 | tf_op jit(solution)/shard_map/all_to_all | solution.py:25
  21.7 3.5 %all-to-all-start.1 = ((bf16[8,32,256]{2,1,0:T(8,128)(2,1)}), bf16[8,32,256]{2,1,0:T(8,128)(2,1)S(1)}, u32[]{:S(2)}, u32[]{:S(2)}) async-start(bf16[8,32,256]{2,1,0:T(8,128)(2,1)} %shard_map.88), calls=%async_computation.1 | async-start | bytes 262144 | tf_op jit(solution)/shard_map/all_to_all | solution.py:25
  25.3 1.7 %collective-permute-start.14 = (bf16[256,128]{1,0:T(8,128)(2,1)S(1)}, bf16[256,128]{1,0:T(8,128)(2,1)S(1)}, u32[]{:S(2)}, u32[]{:S(2)}) collective-permute-start(bf16[256,128]{1,0:T(8,128)(2,1)S(1)} %bitcast_multiply_fusion.own), channel_id=1, source_target_pairs={{0,1},{1,0},{2,3},{3,2},{4,5},{5,4},{6,7},{7,6},{8,9},{9,8},{10,11... | collective-permute-start | bytes 196616 | tf_op jit(solution)/shard_map/ppermute | solution.py:29
  27.9 5.2 %all-to-all-done.1.solved = bf16[8,32,256]{2,1,0:T(8,128)(2,1)S(1)} async-done(((bf16[8,32,256]{2,1,0:T(8,128)(2,1)}), bf16[8,32,256]{2,1,0:T(8,128)(2,1)S(1)}, u32[]{:S(2)}, u32[]{:S(2)}) %all-to-all-start.1) | async-done | bytes 131104 | tf_op jit(solution)/shard_map/all_to_all | solution.py:25
  34.0 6.9 %all-to-all-start.2 = ((f32[16,16,256]{2,1,0:T(8,128)}), f32[16,16,256]{2,1,0:T(8,128)S(1)}, u32[]{:S(2)}, u32[]{:S(2)}) async-start(f32[16,16,256]{2,1,0:T(8,128)} %shard_map.91), calls=%async_computation.2 | async-start | bytes 524288 | tf_op jit(solution)/shard_map/all_to_all | solution.py:25
  42.3 2.4 %collective-permute-start.17 = (bf16[128,256]{1,0:T(8,128)(2,1)S(1)}, bf16[128,256]{1,0:T(8,128)(2,1)S(1)}, u32[]{:S(2)}, u32[]{:S(2)}) collective-permute-start(bf16[128,256]{1,0:T(8,128)(2,1)S(1)} %pad_maximum_fusion.refs_0_), channel_id=1, source_target_pairs={{0,16},{8,24},{16,0},{24,8},{1,17},{9,25},{17,1},{25,9},{2,18},{10... | collective-permute-start | bytes 196616 | tf_op jit(solution)/shard_map/ppermute | solution.py:33
  50.1 2.4 %collective-permute-start.20 = (bf16[2,128,256]{2,1,0:T(8,128)(2,1)S(1)}, bf16[2,128,256]{2,1,0:T(8,128)(2,1)S(1)}, u32[]{:S(2)}, u32[]{:S(2)}) collective-permute-start(bf16[2,128,256]{2,1,0:T(8,128)(2,1)S(1)} %shard_map.93.refs_0_), channel_id=1, source_target_pairs={{0,4},{2,6},{4,0},{6,2},{1,5},{3,7},{5,1},{7,3},{8,12},{10,14},{12... | collective-permute-start | bytes 393224 | tf_op jit(solution)/shard_map/ppermute | solution.py:33
  54.8 4.9 %collective-permute-start.15 = (bf16[16,256]{1,0:T(8,128)(2,1)S(1)}, bf16[16,256]{1,0:T(8,128)(2,1)S(1)}, u32[]{:S(2)}, u32[]{:S(2)}) collective-permute-start(bf16[16,256]{1,0:T(8,128)(2,1)S(1)} %shard_map.92.mine), channel_id=1, source_target_pairs={{0,1},{1,0},{2,3},{3,2},{4,5},{5,4},{6,7},{7,6},{8,9},{9,8},{10,11... | collective-permute-start | bytes 24584 | tf_op jit(solution)/shard_map/ppermute | solution.py:29
  62.5 3.4 %all-to-all-start.3 = ((f32[8,32,128]{2,1,0:T(8,128)}), f32[8,32,128]{2,1,0:T(8,128)S(1)}, u32[]{:S(2)}, u32[]{:S(2)}) async-start(f32[8,32,128]{2,1,0:T(8,128)} %shard_map.94), calls=%async_computation.3 | async-start | bytes 262144 | tf_op jit(solution)/shard_map/all_to_all | solution.py:25
  66.5 2.1 %collective-permute-start.1 = (bf16[8,128,128]{2,1,0:T(8,128)(2,1)S(1)}, bf16[8,128,128]{2,1,0:T(8,128)(2,1)S(1)}, u32[]{:S(2)}, u32[]{:S(2)}) collective-permute-start(bf16[8,128,128]{2,1,0:T(8,128)(2,1)S(1)} %get-tuple-element.23), channel_id=1, source_target_pairs={{0,16},{1,5},{2,18},{3,7},{4,20},{5,1},{6,22},{7,3},{8,24},{9,13},... | collective-permute-start | bytes 786440 | tf_op jit(solution)/shard_map/ppermute | solution.py:54
  69.9 4.1 %all-to-all-done.3.came = f32[8,32,128]{2,1,0:T(8,128)S(1)} async-done(((f32[8,32,128]{2,1,0:T(8,128)}), f32[8,32,128]{2,1,0:T(8,128)S(1)}, u32[]{:S(2)}, u32[]{:S(2)}) %all-to-all-start.3) | async-done | bytes 131104 | tf_op jit(solution)/shard_map/all_to_all | solution.py:25
  74.8 4.9 %all-to-all-start.4 = ((bf16[32,32,128]{2,1,0:T(8,128)(2,1)}), bf16[32,32,128]{2,1,0:T(8,128)(2,1)S(1)}, u32[]{:S(2)}, u32[]{:S(2)}) async-start(bf16[32,32,128]{2,1,0:T(8,128)(2,1)} %shard_map.95), calls=%async_computation.4 | async-start | bytes 524288 | tf_op jit(solution)/shard_map/all_to_all | solution.py:279
  80.2 3.2 %collective-permute-start.9 = (bf16[512,128]{1,0:T(8,128)(2,1)S(1)}, bf16[512,128]{1,0:T(8,128)(2,1)S(1)}, u32[]{:S(2)}, u32[]{:S(2)}) collective-permute-start(bf16[512,128]{1,0:T(8,128)(2,1)S(1)} %bitcast.21), channel_id=1, source_target_pairs={{0,16},{8,24},{16,0},{24,8},{1,17},{9,25},{17,1},{25,9},{2,18},{10... | collective-permute-start | bytes 393224 | tf_op jit(solution)/shard_map/ppermute | solution.py:33
  83.5 1.5 %collective-permute-start.3 = (bf16[8,128,128]{2,1,0:T(8,128)(2,1)S(1)}, bf16[8,128,128]{2,1,0:T(8,128)(2,1)S(1)}, u32[]{:S(2)}, u32[]{:S(2)}) collective-permute-start(bf16[8,128,128]{2,1,0:T(8,128)(2,1)S(1)} %get-tuple-element.26), channel_id=1, source_target_pairs={{0,2},{1,9},{2,4},{3,11},{4,6},{5,13},{6,0},{7,15},{8,10},{9,17},{... | collective-permute-start | bytes 786440 | tf_op jit(solution)/shard_map/ppermute | solution.py:54
  85.1 2.4 %collective-permute-start.5 = (bf16[8,128,128]{2,1,0:T(8,128)(2,1)S(1)}, bf16[8,128,128]{2,1,0:T(8,128)(2,1)S(1)}, u32[]{:S(2)}, u32[]{:S(2)}) collective-permute-start(bf16[8,128,128]{2,1,0:T(8,128)(2,1)S(1)} %get-tuple-element.28), channel_id=1, source_target_pairs={{0,6},{1,25},{2,0},{3,27},{4,2},{5,29},{6,4},{7,31},{8,14},{9,1},{... | collective-permute-start | bytes 786440 | tf_op jit(solution)/shard_map/ppermute | solution.py:54
  89.5 1.9 %collective-permute-start.11 = (bf16[2,512,128]{2,1,0:T(8,128)(2,1)S(1)}, bf16[2,512,128]{2,1,0:T(8,128)(2,1)S(1)}, u32[]{:S(2)}, u32[]{:S(2)}) collective-permute-start(bf16[2,512,128]{2,1,0:T(8,128)(2,1)S(1)} %shard_map.89.refs_4_), channel_id=1, source_target_pairs={{0,2},{2,4},{4,6},{6,0},{1,3},{3,5},{5,7},{7,1},{8,10},{10,12},{12... | collective-permute-start | bytes 786440 | tf_op jit(solution)/shard_map/ppermute | solution.py:33
  91.4 2.0 %collective-permute-start.12 = (bf16[2,512,128]{2,1,0:T(8,128)(2,1)S(1)}, bf16[2,512,128]{2,1,0:T(8,128)(2,1)S(1)}, u32[]{:S(2)}, u32[]{:S(2)}) collective-permute-start(bf16[2,512,128]{2,1,0:T(8,128)(2,1)S(1)} %shard_map.89.refs_4_), channel_id=1, source_target_pairs={{0,4},{2,6},{4,0},{6,2},{1,5},{3,7},{5,1},{7,3},{8,12},{10,14},{12... | collective-permute-start | bytes 786440 | tf_op jit(solution)/shard_map/ppermute | solution.py:33
  94.0 2.1 %collective-permute-start.13 = (bf16[2,512,128]{2,1,0:T(8,128)(2,1)S(1)}, bf16[2,512,128]{2,1,0:T(8,128)(2,1)S(1)}, u32[]{:S(2)}, u32[]{:S(2)}) collective-permute-start(bf16[2,512,128]{2,1,0:T(8,128)(2,1)S(1)} %shard_map.89.refs_4_), channel_id=1, source_target_pairs={{0,6},{2,0},{4,2},{6,4},{1,7},{3,1},{5,3},{7,5},{8,14},{10,8},{12,... | collective-permute-start | bytes 786440 | tf_op jit(solution)/shard_map/ppermute | solution.py:33
  97.9 2.1 %collective-permute-start.23 = (bf16[4,8,32,128]{3,2,1,0:T(8,128)(2,1)S(1)}, bf16[4,8,32,128]{3,2,1,0:T(8,128)(2,1)S(1)}, u32[]{:S(2)}, u32[]{:S(2)}) collective-permute-start(bf16[4,8,32,128]{3,2,1,0:T(8,128)(2,1)S(1)} %bitcast.27), channel_id=1, source_target_pairs={{0,4},{1,17},{2,6},{3,19},{4,0},{5,21},{6,2},{7,23},{8,12},{9,25},... | collective-permute-start | bytes 786440 | tf_op jit(solution)/shard_map/ppermute | solution.py:54
  100.6 5.0 %collective-permute-done.12.refs_6_ = bf16[2,512,128]{2,1,0:T(8,128)(2,1)S(1)} collective-permute-done((bf16[2,512,128]{2,1,0:T(8,128)(2,1)S(1)}, bf16[2,512,128]{2,1,0:T(8,128)(2,1)S(1)}, u32[]{:S(2)}, u32[]{:S(2)}) %collective-permute-start.12) | collective-permute-done | bytes 262176 | tf_op jit(solution)/shard_map/ppermute | solution.py:33
  107.9 8.3 %collective-permute-start.25 = (f32[128,512]{1,0:T(8,128)S(1)}, f32[128,512]{1,0:T(8,128)S(1)}, u32[]{:S(2)}, u32[]{:S(2)}) collective-permute-start(f32[128,512]{1,0:T(8,128)S(1)} %get-tuple-element.37), channel_id=1, source_target_pairs={{0,1},{1,0},{2,3},{3,2},{4,5},{5,4},{6,7},{7,6},{8,9},{9,8},{10,11... | collective-permute-start | bytes 786440 | tf_op jit(solution)/shard_map/ppermute | solution.py:29
  (75 shorter events, 27.5 us)
Async XLA Ops:
  2.4 18.1 %collective-permute-start.6 = (bf16[128,2048]{1,0:T(8,128)(2,1)S(1)}, bf16[128,2048]{1,0:T(8,128)(2,1)S(1)}, u32[]{:S(2)}, u32[]{:S(2)}) collective-permute-start(bf16[128,2048]{1,0:T(8,128)(2,1)S(1)} %bitcast.31), channel_id=1, source_target_pairs={{0,1},{1,0},{2,3},{3,2},{4,5},{5,4},{6,7},{7,6},{8,9},{9,8},{10,11... | collective-permute-start | bytes 1572872 | tf_op jit(solution)/shard_map/ppermute | solution.py:29
  5.6 14.9 %all-to-all-start = ((bf16[8,32,256]{2,1,0:T(8,128)(2,1)}), bf16[8,32,256]{2,1,0:T(8,128)(2,1)S(1)}, u32[]{:S(2)}, u32[]{:S(2)}) async-start(bf16[8,32,256]{2,1,0:T(8,128)(2,1)} %turn.1), calls=%async_computation | async-start | bytes 262144 | tf_op jit(solution)/shard_map/all_to_all | solution.py:25
  21.7 11.4 %all-to-all-start.1 = ((bf16[8,32,256]{2,1,0:T(8,128)(2,1)}), bf16[8,32,256]{2,1,0:T(8,128)(2,1)S(1)}, u32[]{:S(2)}, u32[]{:S(2)}) async-start(bf16[8,32,256]{2,1,0:T(8,128)(2,1)} %shard_map.88), calls=%async_computation.1 | async-start | bytes 262144 | tf_op jit(solution)/shard_map/all_to_all | solution.py:25
  34.0 20.8 %all-to-all-start.2 = ((f32[16,16,256]{2,1,0:T(8,128)}), f32[16,16,256]{2,1,0:T(8,128)S(1)}, u32[]{:S(2)}, u32[]{:S(2)}) async-start(f32[16,16,256]{2,1,0:T(8,128)} %shard_map.91), calls=%async_computation.2 | async-start | bytes 524288 | tf_op jit(solution)/shard_map/all_to_all | solution.py:25
  48.9 12.7 %collective-permute-start.19 = (bf16[2,128,256]{2,1,0:T(8,128)(2,1)S(1)}, bf16[2,128,256]{2,1,0:T(8,128)(2,1)S(1)}, u32[]{:S(2)}, u32[]{:S(2)}) collective-permute-start(bf16[2,128,256]{2,1,0:T(8,128)(2,1)S(1)} %shard_map.93.refs_0_), channel_id=1, source_target_pairs={{0,2},{2,4},{4,6},{6,0},{1,3},{3,5},{5,7},{7,1},{8,10},{10,12},{12... | collective-permute-start | bytes 393224 | tf_op jit(solution)/shard_map/ppermute | solution.py:33
  50.1 11.5 %collective-permute-start.20 = (bf16[2,128,256]{2,1,0:T(8,128)(2,1)S(1)}, bf16[2,128,256]{2,1,0:T(8,128)(2,1)S(1)}, u32[]{:S(2)}, u32[]{:S(2)}) collective-permute-start(bf16[2,128,256]{2,1,0:T(8,128)(2,1)S(1)} %shard_map.93.refs_0_), channel_id=1, source_target_pairs={{0,4},{2,6},{4,0},{6,2},{1,5},{3,7},{5,1},{7,3},{8,12},{10,14},{12... | collective-permute-start | bytes 393224 | tf_op jit(solution)/shard_map/ppermute | solution.py:33
  52.5 9.1 %collective-permute-start.21 = (bf16[2,128,256]{2,1,0:T(8,128)(2,1)S(1)}, bf16[2,128,256]{2,1,0:T(8,128)(2,1)S(1)}, u32[]{:S(2)}, u32[]{:S(2)}) collective-permute-start(bf16[2,128,256]{2,1,0:T(8,128)(2,1)S(1)} %shard_map.93.refs_0_), channel_id=1, source_target_pairs={{0,6},{2,0},{4,2},{6,4},{1,7},{3,1},{5,3},{7,5},{8,14},{10,8},{12,... | collective-permute-start | bytes 393224 | tf_op jit(solution)/shard_map/ppermute | solution.py:33
  61.2 22.2 %collective-permute-start = (bf16[8,128,128]{2,1,0:T(8,128)(2,1)S(1)}, bf16[8,128,128]{2,1,0:T(8,128)(2,1)S(1)}, u32[]{:S(2)}, u32[]{:S(2)}) collective-permute-start(bf16[8,128,128]{2,1,0:T(8,128)(2,1)S(1)} %get-tuple-element.22), channel_id=1, source_target_pairs={{0,8},{1,3},{2,10},{3,5},{4,12},{5,7},{6,14},{7,1},{8,16},{9,11},{... | collective-permute-start | bytes 786440 | tf_op jit(solution)/shard_map/ppermute | solution.py:54
  62.5 11.5 %all-to-all-start.3 = ((f32[8,32,128]{2,1,0:T(8,128)}), f32[8,32,128]{2,1,0:T(8,128)S(1)}, u32[]{:S(2)}, u32[]{:S(2)}) async-start(f32[8,32,128]{2,1,0:T(8,128)} %shard_map.94), calls=%async_computation.3 | async-start | bytes 262144 | tf_op jit(solution)/shard_map/all_to_all | solution.py:25
  65.9 13.7 %collective-permute-start.7 = (bf16[256,128]{1,0:T(8,128)(2,1)S(1)}, bf16[256,128]{1,0:T(8,128)(2,1)S(1)}, u32[]{:S(2)}, u32[]{:S(2)}) collective-permute-start(bf16[256,128]{1,0:T(8,128)(2,1)S(1)} %get-tuple-element.41), channel_id=1, source_target_pairs={{0,1},{1,0},{2,3},{3,2},{4,5},{5,4},{6,7},{7,6},{8,9},{9,8},{10,11... | collective-permute-start | bytes 196616 | tf_op jit(solution)/shard_map/ppermute | solution.py:29
  66.5 16.9 %collective-permute-start.1 = (bf16[8,128,128]{2,1,0:T(8,128)(2,1)S(1)}, bf16[8,128,128]{2,1,0:T(8,128)(2,1)S(1)}, u32[]{:S(2)}, u32[]{:S(2)}) collective-permute-start(bf16[8,128,128]{2,1,0:T(8,128)(2,1)S(1)} %get-tuple-element.23), channel_id=1, source_target_pairs={{0,16},{1,5},{2,18},{3,7},{4,20},{5,1},{6,22},{7,3},{8,24},{9,13},... | collective-permute-start | bytes 786440 | tf_op jit(solution)/shard_map/ppermute | solution.py:54
  68.5 14.9 %collective-permute-start.2 = (bf16[8,128,128]{2,1,0:T(8,128)(2,1)S(1)}, bf16[8,128,128]{2,1,0:T(8,128)(2,1)S(1)}, u32[]{:S(2)}, u32[]{:S(2)}) collective-permute-start(bf16[8,128,128]{2,1,0:T(8,128)(2,1)S(1)} %get-tuple-element.24), channel_id=1, source_target_pairs={{0,24},{1,7},{2,26},{3,1},{4,28},{5,3},{6,30},{7,5},{8,0},{9,15},{... | collective-permute-start | bytes 786440 | tf_op jit(solution)/shard_map/ppermute | solution.py:54
  74.8 22.5 %all-to-all-start.4 = ((bf16[32,32,128]{2,1,0:T(8,128)(2,1)}), bf16[32,32,128]{2,1,0:T(8,128)(2,1)S(1)}, u32[]{:S(2)}, u32[]{:S(2)}) async-start(bf16[32,32,128]{2,1,0:T(8,128)(2,1)} %shard_map.95), calls=%async_computation.4 | async-start | bytes 524288 | tf_op jit(solution)/shard_map/all_to_all | solution.py:279
  80.2 8.6 %collective-permute-start.9 = (bf16[512,128]{1,0:T(8,128)(2,1)S(1)}, bf16[512,128]{1,0:T(8,128)(2,1)S(1)}, u32[]{:S(2)}, u32[]{:S(2)}) collective-permute-start(bf16[512,128]{1,0:T(8,128)(2,1)S(1)} %bitcast.21), channel_id=1, source_target_pairs={{0,16},{8,24},{16,0},{24,8},{1,17},{9,25},{17,1},{25,9},{2,18},{10... | collective-permute-start | bytes 393224 | tf_op jit(solution)/shard_map/ppermute | solution.py:33
  83.5 10.5 %collective-permute-start.3 = (bf16[8,128,128]{2,1,0:T(8,128)(2,1)S(1)}, bf16[8,128,128]{2,1,0:T(8,128)(2,1)S(1)}, u32[]{:S(2)}, u32[]{:S(2)}) collective-permute-start(bf16[8,128,128]{2,1,0:T(8,128)(2,1)S(1)} %get-tuple-element.26), channel_id=1, source_target_pairs={{0,2},{1,9},{2,4},{3,11},{4,6},{5,13},{6,0},{7,15},{8,10},{9,17},{... | collective-permute-start | bytes 786440 | tf_op jit(solution)/shard_map/ppermute | solution.py:54
  85.0 12.3 %collective-permute-start.4 = (bf16[8,128,128]{2,1,0:T(8,128)(2,1)S(1)}, bf16[8,128,128]{2,1,0:T(8,128)(2,1)S(1)}, u32[]{:S(2)}, u32[]{:S(2)}) collective-permute-start(bf16[8,128,128]{2,1,0:T(8,128)(2,1)S(1)} %get-tuple-element.27), channel_id=1, source_target_pairs={{0,4},{1,17},{2,6},{3,19},{4,0},{5,21},{6,2},{7,23},{8,12},{9,25},... | collective-permute-start | bytes 786440 | tf_op jit(solution)/shard_map/ppermute | solution.py:54
  85.1 12.8 %collective-permute-start.5 = (bf16[8,128,128]{2,1,0:T(8,128)(2,1)S(1)}, bf16[8,128,128]{2,1,0:T(8,128)(2,1)S(1)}, u32[]{:S(2)}, u32[]{:S(2)}) collective-permute-start(bf16[8,128,128]{2,1,0:T(8,128)(2,1)S(1)} %get-tuple-element.28), channel_id=1, source_target_pairs={{0,6},{1,25},{2,0},{3,27},{4,2},{5,29},{6,4},{7,31},{8,14},{9,1},{... | collective-permute-start | bytes 786440 | tf_op jit(solution)/shard_map/ppermute | solution.py:54
  89.5 10.5 %collective-permute-start.11 = (bf16[2,512,128]{2,1,0:T(8,128)(2,1)S(1)}, bf16[2,512,128]{2,1,0:T(8,128)(2,1)S(1)}, u32[]{:S(2)}, u32[]{:S(2)}) collective-permute-start(bf16[2,512,128]{2,1,0:T(8,128)(2,1)S(1)} %shard_map.89.refs_4_), channel_id=1, source_target_pairs={{0,2},{2,4},{4,6},{6,0},{1,3},{3,5},{5,7},{7,1},{8,10},{10,12},{12... | collective-permute-start | bytes 786440 | tf_op jit(solution)/shard_map/ppermute | solution.py:33
  91.4 14.3 %collective-permute-start.12 = (bf16[2,512,128]{2,1,0:T(8,128)(2,1)S(1)}, bf16[2,512,128]{2,1,0:T(8,128)(2,1)S(1)}, u32[]{:S(2)}, u32[]{:S(2)}) collective-permute-start(bf16[2,512,128]{2,1,0:T(8,128)(2,1)S(1)} %shard_map.89.refs_4_), channel_id=1, source_target_pairs={{0,4},{2,6},{4,0},{6,2},{1,5},{3,7},{5,1},{7,3},{8,12},{10,14},{12... | collective-permute-start | bytes 786440 | tf_op jit(solution)/shard_map/ppermute | solution.py:33
  94.0 12.0 %collective-permute-start.13 = (bf16[2,512,128]{2,1,0:T(8,128)(2,1)S(1)}, bf16[2,512,128]{2,1,0:T(8,128)(2,1)S(1)}, u32[]{:S(2)}, u32[]{:S(2)}) collective-permute-start(bf16[2,512,128]{2,1,0:T(8,128)(2,1)S(1)} %shard_map.89.refs_4_), channel_id=1, source_target_pairs={{0,6},{2,0},{4,2},{6,4},{1,7},{3,1},{5,3},{7,5},{8,14},{10,8},{12,... | collective-permute-start | bytes 786440 | tf_op jit(solution)/shard_map/ppermute | solution.py:33
  97.3 9.5 %collective-permute-start.22 = (bf16[4,8,32,128]{3,2,1,0:T(8,128)(2,1)S(1)}, bf16[4,8,32,128]{3,2,1,0:T(8,128)(2,1)S(1)}, u32[]{:S(2)}, u32[]{:S(2)}) collective-permute-start(bf16[4,8,32,128]{3,2,1,0:T(8,128)(2,1)S(1)} %bitcast.26), channel_id=1, source_target_pairs={{0,2},{1,9},{2,4},{3,11},{4,6},{5,13},{6,0},{7,15},{8,10},{9,17},{... | collective-permute-start | bytes 786440 | tf_op jit(solution)/shard_map/ppermute | solution.py:54
  97.9 8.9 %collective-permute-start.23 = (bf16[4,8,32,128]{3,2,1,0:T(8,128)(2,1)S(1)}, bf16[4,8,32,128]{3,2,1,0:T(8,128)(2,1)S(1)}, u32[]{:S(2)}, u32[]{:S(2)}) collective-permute-start(bf16[4,8,32,128]{3,2,1,0:T(8,128)(2,1)S(1)} %bitcast.27), channel_id=1, source_target_pairs={{0,4},{1,17},{2,6},{3,19},{4,0},{5,21},{6,2},{7,23},{8,12},{9,25},... | collective-permute-start | bytes 786440 | tf_op jit(solution)/shard_map/ppermute | solution.py:54
  100.0 7.4 %collective-permute-start.24 = (bf16[4,8,32,128]{3,2,1,0:T(8,128)(2,1)S(1)}, bf16[4,8,32,128]{3,2,1,0:T(8,128)(2,1)S(1)}, u32[]{:S(2)}, u32[]{:S(2)}) collective-permute-start(bf16[4,8,32,128]{3,2,1,0:T(8,128)(2,1)S(1)} %bitcast.28), channel_id=1, source_target_pairs={{0,6},{1,25},{2,0},{3,27},{4,2},{5,29},{6,4},{7,31},{8,14},{9,1},{... | collective-permute-start | bytes 786440 | tf_op jit(solution)/shard_map/ppermute | solution.py:54
  107.9 9.4 %collective-permute-start.25 = (f32[128,512]{1,0:T(8,128)S(1)}, f32[128,512]{1,0:T(8,128)S(1)}, u32[]{:S(2)}, u32[]{:S(2)}) collective-permute-start(f32[128,512]{1,0:T(8,128)S(1)} %get-tuple-element.37), channel_id=1, source_target_pairs={{0,1},{1,0},{2,3},{3,2},{4,5},{5,4},{6,7},{7,6},{8,9},{9,8},{10,11... | collective-permute-start | bytes 786440 | tf_op jit(solution)/shard_map/ppermute | solution.py:29
  (14 other events, 87.3 us)

commit v6 on v5

--- a/solution.py
+++ b/solution.py
@@ -90,7 +90,7 @@
 
 
 def turned(given, out):
-    lines = jnp.concatenate([given[0, 0, 0].T, given[0, 1, 0].T], axis=1)
+    lines = jnp.concatenate([given[0].T, given[1].T], axis=1)
     lines = lines.reshape(16, 2, 16, 2 * TB)
     lines = jnp.where(lax.axis_index("core") == 0, lines[:, 0], lines[:, 1])
     out[...] = lines.reshape(ROWS, 32, 2 * TB)
@@ -223,15 +223,7 @@
     core = lax.axis_index("core")
     chip = lax.axis_index(CHIP)
 
-    rhs0 = pl.pallas_call(
-        turned,
-        grid=(1,),
-        out_shape=jax.ShapeDtypeStruct((ROWS, 32, 2 * TB), BF16),
-        in_specs=[pl.BlockSpec((1, 2, 1, TB, K), lambda i: (0, 0, 0, 0, 0))],
-        out_specs=pl.BlockSpec((ROWS, 32, 2 * TB), lambda i: (0, 0, 0)),
-        compiler_params=pltpu.CompilerParams(vmem_limit_bytes=62 * 2**20),
-        name="turn",
-    )(rhs_super)
+    [rhs0] = local(turned, [((ROWS, 32, 2 * TB), BF16)], rhs_super[0].reshape(2, TB, K))
     rhs0, dinv, factor_trail, rhs_super = lax.optimization_barrier(
         (rhs0, dinv_rows[0, 0], factor_trail, rhs_super)
     )

time: 119 us -> 118 us (level)
  starting transfers between devices: 74.5 us -> 76.2 us
  waiting for transfers between devices: 31.2 us -> 29.6 us
    pallas_call x1 -> x0, Pallas kernels: 1.79 us -> none  [steps(): pl.pallas_call(turned, grid=(1,), out_shape=jax.ShapeDtypeStruct((ROWS, 3...]
    all_to_all x4, waiting for transfers between devices: 17.7 us -> 16.4 us  [exchange(): return lax.all_to_all(x, axis, split_axis=0, concat_axis=0, tiled=True)]
    pallas_call x12 -> x13, Pallas kernels: 7.09 us -> 7.88 us  [local(): pl.pallas_call(kernel, out_shape=[jax.ShapeDtypeStruct(shape, dtype) for...]
  transfers between devices with their start and end apart: 31 -> 31, of which waited for: 15 -> 14; matrix products, arithmetic and copies ran while one was open for 0% -> 0% of each run, Pallas kernels for 4% -> 4%
where the time goes in v6:
time: 118 us; the launch traced here: 117 us
  starting transfers between devices  76.2 us (65%)
  waiting for transfers between devices  29.6 us (25%)
  Pallas kernels  7.88 us (7%)
  local copies, waits for them, and re-layouts  1.98 us (2%)
    all_to_all x4, starting transfers between devices, exchange(): return lax.all_to_all(x, axis, split_axis=0, concat_axis=0, tiled=True)  20.2 us
    ppermute x12, starting transfers between devices, shifted(): return lax.ppermute(x, axis, [(i, (i + step) % 4) for i in sources])  19.9 us
    ppermute x5, starting transfers between devices, partner(): return lax.ppermute(x, 'core', [(0, 1), (1, 0)])  19.6 us
    all_to_all x4, waiting for transfers between devices, exchange(): return lax.all_to_all(x, axis, split_axis=0, concat_axis=0, tiled=True)  16.4 us
    ppermute x9, starting transfers between devices, crossed(): return lax.ppermute(x, COL, pairs)  11.2 us
    ppermute x12, waiting for transfers between devices, shifted(): return lax.ppermute(x, axis, [(i, (i + step) % 4) for i in sources])  10.4 us
    pallas_call x13, Pallas kernels, local(): pl.pallas_call(kernel, out_shape=[jax.ShapeDtypeStruct(shape, dtype) for...  7.88 us
    all_to_all x1, starting transfers between devices, steps(): lax.all_to_all(solved1, ('row', *COL), 0, 0, axis_index_groups=crossed_gr...  5.21 us
  transfers between devices with their start and end apart: 31, of which 14 were waited for; matrix products, arithmetic and copies ran while one was open for 0% of the time, Pallas kernels for 4%

profile of v6, /device:TPU:1, one launch (start us, length us, event | category | flops | bytes accessed | tf_op | source)
XLA Modules:
  0.0 117.3 jit_solution(15672181059645489562)
XLA Ops:
  2.5 3.2 %collective-permute-start.6 = (bf16[128,2048]{1,0:T(8,128)(2,1)S(1)}, bf16[128,2048]{1,0:T(8,128)(2,1)S(1)}, u32[]{:S(2)}, u32[]{:S(2)}) collective-permute-start(bf16[128,2048]{1,0:T(8,128)(2,1)S(1)} %bitcast.34), channel_id=1, source_target_pairs={{0,1},{1,0},{2,3},{3,2},{4,5},{5,4},{6,7},{7,6},{8,9},{9,8},{10,11... | collective-permute-start | bytes 1572872 | tf_op jit(solution)/shard_map/ppermute | solution.py:29
  5.7 6.5 %all-to-all-start = ((bf16[8,32,256]{2,1,0:T(8,128)(2,1)}), bf16[8,32,256]{2,1,0:T(8,128)(2,1)S(1)}, u32[]{:S(2)}, u32[]{:S(2)}) async-start(bf16[8,32,256]{2,1,0:T(8,128)(2,1)} %shard_map.86), calls=%async_computation | async-start | bytes 262144 | tf_op jit(solution)/shard_map/all_to_all | solution.py:25
  12.2 8.3 %all-to-all-done.due = bf16[8,32,256]{2,1,0:T(8,128)(2,1)S(1)} async-done(((bf16[8,32,256]{2,1,0:T(8,128)(2,1)}), bf16[8,32,256]{2,1,0:T(8,128)(2,1)S(1)}, u32[]{:S(2)}, u32[]{:S(2)}) %all-to-all-start) | async-done | bytes 131104 | tf_op jit(solution)/shard_map/all_to_all | solution.py:25
  21.6 3.5 %all-to-all-start.1 = ((bf16[8,32,256]{2,1,0:T(8,128)(2,1)}), bf16[8,32,256]{2,1,0:T(8,128)(2,1)S(1)}, u32[]{:S(2)}, u32[]{:S(2)}) async-start(bf16[8,32,256]{2,1,0:T(8,128)(2,1)} %shard_map.89), calls=%async_computation.1 | async-start | bytes 262144 | tf_op jit(solution)/shard_map/all_to_all | solution.py:25
  25.2 1.7 %collective-permute-start.14 = (bf16[256,128]{1,0:T(8,128)(2,1)S(1)}, bf16[256,128]{1,0:T(8,128)(2,1)S(1)}, u32[]{:S(2)}, u32[]{:S(2)}) collective-permute-start(bf16[256,128]{1,0:T(8,128)(2,1)S(1)} %bitcast_multiply_fusion.own), channel_id=1, source_target_pairs={{0,1},{1,0},{2,3},{3,2},{4,5},{5,4},{6,7},{7,6},{8,9},{9,8},{10,11... | collective-permute-start | bytes 196616 | tf_op jit(solution)/shard_map/ppermute | solution.py:29
  27.9 5.1 %all-to-all-done.1.solved = bf16[8,32,256]{2,1,0:T(8,128)(2,1)S(1)} async-done(((bf16[8,32,256]{2,1,0:T(8,128)(2,1)}), bf16[8,32,256]{2,1,0:T(8,128)(2,1)S(1)}, u32[]{:S(2)}, u32[]{:S(2)}) %all-to-all-start.1) | async-done | bytes 131104 | tf_op jit(solution)/shard_map/all_to_all | solution.py:25
  33.9 6.9 %all-to-all-start.2 = ((f32[16,16,256]{2,1,0:T(8,128)}), f32[16,16,256]{2,1,0:T(8,128)S(1)}, u32[]{:S(2)}, u32[]{:S(2)}) async-start(f32[16,16,256]{2,1,0:T(8,128)} %shard_map.92), calls=%async_computation.2 | async-start | bytes 524288 | tf_op jit(solution)/shard_map/all_to_all | solution.py:25
  42.3 2.4 %collective-permute-start.17 = (bf16[128,256]{1,0:T(8,128)(2,1)S(1)}, bf16[128,256]{1,0:T(8,128)(2,1)S(1)}, u32[]{:S(2)}, u32[]{:S(2)}) collective-permute-start(bf16[128,256]{1,0:T(8,128)(2,1)S(1)} %pad_maximum_fusion.refs_0_), channel_id=1, source_target_pairs={{0,16},{8,24},{16,0},{24,8},{1,17},{9,25},{17,1},{25,9},{2,18},{10... | collective-permute-start | bytes 196616 | tf_op jit(solution)/shard_map/ppermute | solution.py:33
  50.1 2.4 %collective-permute-start.20 = (bf16[2,128,256]{2,1,0:T(8,128)(2,1)S(1)}, bf16[2,128,256]{2,1,0:T(8,128)(2,1)S(1)}, u32[]{:S(2)}, u32[]{:S(2)}) collective-permute-start(bf16[2,128,256]{2,1,0:T(8,128)(2,1)S(1)} %shard_map.94.refs_0_), channel_id=1, source_target_pairs={{0,4},{2,6},{4,0},{6,2},{1,5},{3,7},{5,1},{7,3},{8,12},{10,14},{12... | collective-permute-start | bytes 393224 | tf_op jit(solution)/shard_map/ppermute | solution.py:33
  53.9 5.0 %collective-permute-start.15 = (bf16[16,256]{1,0:T(8,128)(2,1)S(1)}, bf16[16,256]{1,0:T(8,128)(2,1)S(1)}, u32[]{:S(2)}, u32[]{:S(2)}) collective-permute-start(bf16[16,256]{1,0:T(8,128)(2,1)S(1)} %shard_map.93.mine), channel_id=1, source_target_pairs={{0,1},{1,0},{2,3},{3,2},{4,5},{5,4},{6,7},{7,6},{8,9},{9,8},{10,11... | collective-permute-start | bytes 24584 | tf_op jit(solution)/shard_map/ppermute | solution.py:29
  61.7 3.4 %all-to-all-start.3 = ((f32[8,32,128]{2,1,0:T(8,128)}), f32[8,32,128]{2,1,0:T(8,128)S(1)}, u32[]{:S(2)}, u32[]{:S(2)}) async-start(f32[8,32,128]{2,1,0:T(8,128)} %shard_map.95), calls=%async_computation.3 | async-start | bytes 262144 | tf_op jit(solution)/shard_map/all_to_all | solution.py:25
  66.5 2.1 %collective-permute-start.1 = (bf16[8,128,128]{2,1,0:T(8,128)(2,1)S(1)}, bf16[8,128,128]{2,1,0:T(8,128)(2,1)S(1)}, u32[]{:S(2)}, u32[]{:S(2)}) collective-permute-start(bf16[8,128,128]{2,1,0:T(8,128)(2,1)S(1)} %get-tuple-element.23), channel_id=1, source_target_pairs={{0,16},{1,5},{2,18},{3,7},{4,20},{5,1},{6,22},{7,3},{8,24},{9,13},... | collective-permute-start | bytes 786440 | tf_op jit(solution)/shard_map/ppermute | solution.py:54
  70.0 3.0 %all-to-all-done.3.came = f32[8,32,128]{2,1,0:T(8,128)S(1)} async-done(((f32[8,32,128]{2,1,0:T(8,128)}), f32[8,32,128]{2,1,0:T(8,128)S(1)}, u32[]{:S(2)}, u32[]{:S(2)}) %all-to-all-start.3) | async-done | bytes 131104 | tf_op jit(solution)/shard_map/all_to_all | solution.py:25
  73.7 5.2 %all-to-all-start.4 = ((bf16[32,32,128]{2,1,0:T(8,128)(2,1)}), bf16[32,32,128]{2,1,0:T(8,128)(2,1)S(1)}, u32[]{:S(2)}, u32[]{:S(2)}) async-start(bf16[32,32,128]{2,1,0:T(8,128)(2,1)} %shard_map.96), calls=%async_computation.4 | async-start | bytes 524288 | tf_op jit(solution)/shard_map/all_to_all | solution.py:271
  79.4 3.2 %collective-permute-start.9 = (bf16[512,128]{1,0:T(8,128)(2,1)S(1)}, bf16[512,128]{1,0:T(8,128)(2,1)S(1)}, u32[]{:S(2)}, u32[]{:S(2)}) collective-permute-start(bf16[512,128]{1,0:T(8,128)(2,1)S(1)} %bitcast.24), channel_id=1, source_target_pairs={{0,16},{8,24},{16,0},{24,8},{1,17},{9,25},{17,1},{25,9},{2,18},{10... | collective-permute-start | bytes 393224 | tf_op jit(solution)/shard_map/ppermute | solution.py:33
  82.7 1.5 %collective-permute-start.3 = (bf16[8,128,128]{2,1,0:T(8,128)(2,1)S(1)}, bf16[8,128,128]{2,1,0:T(8,128)(2,1)S(1)}, u32[]{:S(2)}, u32[]{:S(2)}) collective-permute-start(bf16[8,128,128]{2,1,0:T(8,128)(2,1)S(1)} %get-tuple-element.26), channel_id=1, source_target_pairs={{0,2},{1,9},{2,4},{3,11},{4,6},{5,13},{6,0},{7,15},{8,10},{9,17},{... | collective-permute-start | bytes 786440 | tf_op jit(solution)/shard_map/ppermute | solution.py:54
  84.4 2.4 %collective-permute-start.5 = (bf16[8,128,128]{2,1,0:T(8,128)(2,1)S(1)}, bf16[8,128,128]{2,1,0:T(8,128)(2,1)S(1)}, u32[]{:S(2)}, u32[]{:S(2)}) collective-permute-start(bf16[8,128,128]{2,1,0:T(8,128)(2,1)S(1)} %get-tuple-element.28), channel_id=1, source_target_pairs={{0,6},{1,25},{2,0},{3,27},{4,2},{5,29},{6,4},{7,31},{8,14},{9,1},{... | collective-permute-start | bytes 786440 | tf_op jit(solution)/shard_map/ppermute | solution.py:54
  88.7 1.6 %collective-permute-start.11 = (bf16[2,512,128]{2,1,0:T(8,128)(2,1)S(1)}, bf16[2,512,128]{2,1,0:T(8,128)(2,1)S(1)}, u32[]{:S(2)}, u32[]{:S(2)}) collective-permute-start(bf16[2,512,128]{2,1,0:T(8,128)(2,1)S(1)} %shard_map.90.refs_4_), channel_id=1, source_target_pairs={{0,2},{2,4},{4,6},{6,0},{1,3},{3,5},{5,7},{7,1},{8,10},{10,12},{12... | collective-permute-start | bytes 786440 | tf_op jit(solution)/shard_map/ppermute | solution.py:33
  90.3 2.4 %collective-permute-start.12 = (bf16[2,512,128]{2,1,0:T(8,128)(2,1)S(1)}, bf16[2,512,128]{2,1,0:T(8,128)(2,1)S(1)}, u32[]{:S(2)}, u32[]{:S(2)}) collective-permute-start(bf16[2,512,128]{2,1,0:T(8,128)(2,1)S(1)} %shard_map.90.refs_4_), channel_id=1, source_target_pairs={{0,4},{2,6},{4,0},{6,2},{1,5},{3,7},{5,1},{7,3},{8,12},{10,14},{12... | collective-permute-start | bytes 786440 | tf_op jit(solution)/shard_map/ppermute | solution.py:33
  93.3 2.4 %collective-permute-start.13 = (bf16[2,512,128]{2,1,0:T(8,128)(2,1)S(1)}, bf16[2,512,128]{2,1,0:T(8,128)(2,1)S(1)}, u32[]{:S(2)}, u32[]{:S(2)}) collective-permute-start(bf16[2,512,128]{2,1,0:T(8,128)(2,1)S(1)} %shard_map.90.refs_4_), channel_id=1, source_target_pairs={{0,6},{2,0},{4,2},{6,4},{1,7},{3,1},{5,3},{7,5},{8,14},{10,8},{12,... | collective-permute-start | bytes 786440 | tf_op jit(solution)/shard_map/ppermute | solution.py:33
  96.5 1.8 %collective-permute-start.23 = (bf16[4,8,32,128]{3,2,1,0:T(8,128)(2,1)S(1)}, bf16[4,8,32,128]{3,2,1,0:T(8,128)(2,1)S(1)}, u32[]{:S(2)}, u32[]{:S(2)}) collective-permute-start(bf16[4,8,32,128]{3,2,1,0:T(8,128)(2,1)S(1)} %bitcast.30), channel_id=1, source_target_pairs={{0,4},{1,17},{2,6},{3,19},{4,0},{5,21},{6,2},{7,23},{8,12},{9,25},... | collective-permute-start | bytes 786440 | tf_op jit(solution)/shard_map/ppermute | solution.py:54
  98.4 1.5 %collective-permute-start.24 = (bf16[4,8,32,128]{3,2,1,0:T(8,128)(2,1)S(1)}, bf16[4,8,32,128]{3,2,1,0:T(8,128)(2,1)S(1)}, u32[]{:S(2)}, u32[]{:S(2)}) collective-permute-start(bf16[4,8,32,128]{3,2,1,0:T(8,128)(2,1)S(1)} %bitcast.31), channel_id=1, source_target_pairs={{0,6},{1,25},{2,0},{3,27},{4,2},{5,29},{6,4},{7,31},{8,14},{9,1},{... | collective-permute-start | bytes 786440 | tf_op jit(solution)/shard_map/ppermute | solution.py:54
  99.9 5.0 %collective-permute-done.12.refs_6_ = bf16[2,512,128]{2,1,0:T(8,128)(2,1)S(1)} collective-permute-done((bf16[2,512,128]{2,1,0:T(8,128)(2,1)S(1)}, bf16[2,512,128]{2,1,0:T(8,128)(2,1)S(1)}, u32[]{:S(2)}, u32[]{:S(2)}) %collective-permute-start.12) | collective-permute-done | bytes 262176 | tf_op jit(solution)/shard_map/ppermute | solution.py:33
  107.2 8.3 %collective-permute-start.25 = (f32[128,512]{1,0:T(8,128)S(1)}, f32[128,512]{1,0:T(8,128)S(1)}, u32[]{:S(2)}, u32[]{:S(2)}) collective-permute-start(f32[128,512]{1,0:T(8,128)S(1)} %get-tuple-element.37), channel_id=1, source_target_pairs={{0,1},{1,0},{2,3},{3,2},{4,5},{5,4},{6,7},{7,6},{8,9},{9,8},{10,11... | collective-permute-start | bytes 786440 | tf_op jit(solution)/shard_map/ppermute | solution.py:29
  (77 shorter events, 27.6 us)
Async XLA Ops:
  2.5 18.1 %collective-permute-start.6 = (bf16[128,2048]{1,0:T(8,128)(2,1)S(1)}, bf16[128,2048]{1,0:T(8,128)(2,1)S(1)}, u32[]{:S(2)}, u32[]{:S(2)}) collective-permute-start(bf16[128,2048]{1,0:T(8,128)(2,1)S(1)} %bitcast.34), channel_id=1, source_target_pairs={{0,1},{1,0},{2,3},{3,2},{4,5},{5,4},{6,7},{7,6},{8,9},{9,8},{10,11... | collective-permute-start | bytes 1572872 | tf_op jit(solution)/shard_map/ppermute | solution.py:29
  5.7 14.8 %all-to-all-start = ((bf16[8,32,256]{2,1,0:T(8,128)(2,1)}), bf16[8,32,256]{2,1,0:T(8,128)(2,1)S(1)}, u32[]{:S(2)}, u32[]{:S(2)}) async-start(bf16[8,32,256]{2,1,0:T(8,128)(2,1)} %shard_map.86), calls=%async_computation | async-start | bytes 262144 | tf_op jit(solution)/shard_map/all_to_all | solution.py:25
  21.6 11.4 %all-to-all-start.1 = ((bf16[8,32,256]{2,1,0:T(8,128)(2,1)}), bf16[8,32,256]{2,1,0:T(8,128)(2,1)S(1)}, u32[]{:S(2)}, u32[]{:S(2)}) async-start(bf16[8,32,256]{2,1,0:T(8,128)(2,1)} %shard_map.89), calls=%async_computation.1 | async-start | bytes 262144 | tf_op jit(solution)/shard_map/all_to_all | solution.py:25
  33.9 19.9 %all-to-all-start.2 = ((f32[16,16,256]{2,1,0:T(8,128)}), f32[16,16,256]{2,1,0:T(8,128)S(1)}, u32[]{:S(2)}, u32[]{:S(2)}) async-start(f32[16,16,256]{2,1,0:T(8,128)} %shard_map.92), calls=%async_computation.2 | async-start | bytes 524288 | tf_op jit(solution)/shard_map/all_to_all | solution.py:25
  48.8 11.9 %collective-permute-start.19 = (bf16[2,128,256]{2,1,0:T(8,128)(2,1)S(1)}, bf16[2,128,256]{2,1,0:T(8,128)(2,1)S(1)}, u32[]{:S(2)}, u32[]{:S(2)}) collective-permute-start(bf16[2,128,256]{2,1,0:T(8,128)(2,1)S(1)} %shard_map.94.refs_0_), channel_id=1, source_target_pairs={{0,2},{2,4},{4,6},{6,0},{1,3},{3,5},{5,7},{7,1},{8,10},{10,12},{12... | collective-permute-start | bytes 393224 | tf_op jit(solution)/shard_map/ppermute | solution.py:33
  50.1 10.6 %collective-permute-start.20 = (bf16[2,128,256]{2,1,0:T(8,128)(2,1)S(1)}, bf16[2,128,256]{2,1,0:T(8,128)(2,1)S(1)}, u32[]{:S(2)}, u32[]{:S(2)}) collective-permute-start(bf16[2,128,256]{2,1,0:T(8,128)(2,1)S(1)} %shard_map.94.refs_0_), channel_id=1, source_target_pairs={{0,4},{2,6},{4,0},{6,2},{1,5},{3,7},{5,1},{7,3},{8,12},{10,14},{12... | collective-permute-start | bytes 393224 | tf_op jit(solution)/shard_map/ppermute | solution.py:33
  52.4 8.3 %collective-permute-start.21 = (bf16[2,128,256]{2,1,0:T(8,128)(2,1)S(1)}, bf16[2,128,256]{2,1,0:T(8,128)(2,1)S(1)}, u32[]{:S(2)}, u32[]{:S(2)}) collective-permute-start(bf16[2,128,256]{2,1,0:T(8,128)(2,1)S(1)} %shard_map.94.refs_0_), channel_id=1, source_target_pairs={{0,6},{2,0},{4,2},{6,4},{1,7},{3,1},{5,3},{7,5},{8,14},{10,8},{12,... | collective-permute-start | bytes 393224 | tf_op jit(solution)/shard_map/ppermute | solution.py:33
  60.3 22.3 %collective-permute-start = (bf16[8,128,128]{2,1,0:T(8,128)(2,1)S(1)}, bf16[8,128,128]{2,1,0:T(8,128)(2,1)S(1)}, u32[]{:S(2)}, u32[]{:S(2)}) collective-permute-start(bf16[8,128,128]{2,1,0:T(8,128)(2,1)S(1)} %get-tuple-element.22), channel_id=1, source_target_pairs={{0,8},{1,3},{2,10},{3,5},{4,12},{5,7},{6,14},{7,1},{8,16},{9,11},{... | collective-permute-start | bytes 786440 | tf_op jit(solution)/shard_map/ppermute | solution.py:54
  61.7 11.3 %all-to-all-start.3 = ((f32[8,32,128]{2,1,0:T(8,128)}), f32[8,32,128]{2,1,0:T(8,128)S(1)}, u32[]{:S(2)}, u32[]{:S(2)}) async-start(f32[8,32,128]{2,1,0:T(8,128)} %shard_map.95), calls=%async_computation.3 | async-start | bytes 262144 | tf_op jit(solution)/shard_map/all_to_all | solution.py:25
  65.1 13.9 %collective-permute-start.7 = (bf16[256,128]{1,0:T(8,128)(2,1)S(1)}, bf16[256,128]{1,0:T(8,128)(2,1)S(1)}, u32[]{:S(2)}, u32[]{:S(2)}) collective-permute-start(bf16[256,128]{1,0:T(8,128)(2,1)S(1)} %get-tuple-element.41), channel_id=1, source_target_pairs={{0,1},{1,0},{2,3},{3,2},{4,5},{5,4},{6,7},{7,6},{8,9},{9,8},{10,11... | collective-permute-start | bytes 196616 | tf_op jit(solution)/shard_map/ppermute | solution.py:29
  66.5 16.1 %collective-permute-start.1 = (bf16[8,128,128]{2,1,0:T(8,128)(2,1)S(1)}, bf16[8,128,128]{2,1,0:T(8,128)(2,1)S(1)}, u32[]{:S(2)}, u32[]{:S(2)}) collective-permute-start(bf16[8,128,128]{2,1,0:T(8,128)(2,1)S(1)} %get-tuple-element.23), channel_id=1, source_target_pairs={{0,16},{1,5},{2,18},{3,7},{4,20},{5,1},{6,22},{7,3},{8,24},{9,13},... | collective-permute-start | bytes 786440 | tf_op jit(solution)/shard_map/ppermute | solution.py:54
  68.6 14.1 %collective-permute-start.2 = (bf16[8,128,128]{2,1,0:T(8,128)(2,1)S(1)}, bf16[8,128,128]{2,1,0:T(8,128)(2,1)S(1)}, u32[]{:S(2)}, u32[]{:S(2)}) collective-permute-start(bf16[8,128,128]{2,1,0:T(8,128)(2,1)S(1)} %get-tuple-element.24), channel_id=1, source_target_pairs={{0,24},{1,7},{2,26},{3,1},{4,28},{5,3},{6,30},{7,5},{8,0},{9,15},{... | collective-permute-start | bytes 786440 | tf_op jit(solution)/shard_map/ppermute | solution.py:54
  73.7 22.8 %all-to-all-start.4 = ((bf16[32,32,128]{2,1,0:T(8,128)(2,1)}), bf16[32,32,128]{2,1,0:T(8,128)(2,1)S(1)}, u32[]{:S(2)}, u32[]{:S(2)}) async-start(bf16[32,32,128]{2,1,0:T(8,128)(2,1)} %shard_map.96), calls=%async_computation.4 | async-start | bytes 524288 | tf_op jit(solution)/shard_map/all_to_all | solution.py:271
  79.4 8.6 %collective-permute-start.9 = (bf16[512,128]{1,0:T(8,128)(2,1)S(1)}, bf16[512,128]{1,0:T(8,128)(2,1)S(1)}, u32[]{:S(2)}, u32[]{:S(2)}) collective-permute-start(bf16[512,128]{1,0:T(8,128)(2,1)S(1)} %bitcast.24), channel_id=1, source_target_pairs={{0,16},{8,24},{16,0},{24,8},{1,17},{9,25},{17,1},{25,9},{2,18},{10... | collective-permute-start | bytes 393224 | tf_op jit(solution)/shard_map/ppermute | solution.py:33
  82.7 10.6 %collective-permute-start.3 = (bf16[8,128,128]{2,1,0:T(8,128)(2,1)S(1)}, bf16[8,128,128]{2,1,0:T(8,128)(2,1)S(1)}, u32[]{:S(2)}, u32[]{:S(2)}) collective-permute-start(bf16[8,128,128]{2,1,0:T(8,128)(2,1)S(1)} %get-tuple-element.26), channel_id=1, source_target_pairs={{0,2},{1,9},{2,4},{3,11},{4,6},{5,13},{6,0},{7,15},{8,10},{9,17},{... | collective-permute-start | bytes 786440 | tf_op jit(solution)/shard_map/ppermute | solution.py:54
  84.3 12.3 %collective-permute-start.4 = (bf16[8,128,128]{2,1,0:T(8,128)(2,1)S(1)}, bf16[8,128,128]{2,1,0:T(8,128)(2,1)S(1)}, u32[]{:S(2)}, u32[]{:S(2)}) collective-permute-start(bf16[8,128,128]{2,1,0:T(8,128)(2,1)S(1)} %get-tuple-element.27), channel_id=1, source_target_pairs={{0,4},{1,17},{2,6},{3,19},{4,0},{5,21},{6,2},{7,23},{8,12},{9,25},... | collective-permute-start | bytes 786440 | tf_op jit(solution)/shard_map/ppermute | solution.py:54
  84.4 12.2 %collective-permute-start.5 = (bf16[8,128,128]{2,1,0:T(8,128)(2,1)S(1)}, bf16[8,128,128]{2,1,0:T(8,128)(2,1)S(1)}, u32[]{:S(2)}, u32[]{:S(2)}) collective-permute-start(bf16[8,128,128]{2,1,0:T(8,128)(2,1)S(1)} %get-tuple-element.28), channel_id=1, source_target_pairs={{0,6},{1,25},{2,0},{3,27},{4,2},{5,29},{6,4},{7,31},{8,14},{9,1},{... | collective-permute-start | bytes 786440 | tf_op jit(solution)/shard_map/ppermute | solution.py:54
  88.7 9.7 %collective-permute-start.11 = (bf16[2,512,128]{2,1,0:T(8,128)(2,1)S(1)}, bf16[2,512,128]{2,1,0:T(8,128)(2,1)S(1)}, u32[]{:S(2)}, u32[]{:S(2)}) collective-permute-start(bf16[2,512,128]{2,1,0:T(8,128)(2,1)S(1)} %shard_map.90.refs_4_), channel_id=1, source_target_pairs={{0,2},{2,4},{4,6},{6,0},{1,3},{3,5},{5,7},{7,1},{8,10},{10,12},{12... | collective-permute-start | bytes 786440 | tf_op jit(solution)/shard_map/ppermute | solution.py:33
  90.3 14.6 %collective-permute-start.12 = (bf16[2,512,128]{2,1,0:T(8,128)(2,1)S(1)}, bf16[2,512,128]{2,1,0:T(8,128)(2,1)S(1)}, u32[]{:S(2)}, u32[]{:S(2)}) collective-permute-start(bf16[2,512,128]{2,1,0:T(8,128)(2,1)S(1)} %shard_map.90.refs_4_), channel_id=1, source_target_pairs={{0,4},{2,6},{4,0},{6,2},{1,5},{3,7},{5,1},{7,3},{8,12},{10,14},{12... | collective-permute-start | bytes 786440 | tf_op jit(solution)/shard_map/ppermute | solution.py:33
  93.3 12.1 %collective-permute-start.13 = (bf16[2,512,128]{2,1,0:T(8,128)(2,1)S(1)}, bf16[2,512,128]{2,1,0:T(8,128)(2,1)S(1)}, u32[]{:S(2)}, u32[]{:S(2)}) collective-permute-start(bf16[2,512,128]{2,1,0:T(8,128)(2,1)S(1)} %shard_map.90.refs_4_), channel_id=1, source_target_pairs={{0,6},{2,0},{4,2},{6,4},{1,7},{3,1},{5,3},{7,5},{8,14},{10,8},{12,... | collective-permute-start | bytes 786440 | tf_op jit(solution)/shard_map/ppermute | solution.py:33
  96.5 9.7 %collective-permute-start.22 = (bf16[4,8,32,128]{3,2,1,0:T(8,128)(2,1)S(1)}, bf16[4,8,32,128]{3,2,1,0:T(8,128)(2,1)S(1)}, u32[]{:S(2)}, u32[]{:S(2)}) collective-permute-start(bf16[4,8,32,128]{3,2,1,0:T(8,128)(2,1)S(1)} %bitcast.29), channel_id=1, source_target_pairs={{0,2},{1,9},{2,4},{3,11},{4,6},{5,13},{6,0},{7,15},{8,10},{9,17},{... | collective-permute-start | bytes 786440 | tf_op jit(solution)/shard_map/ppermute | solution.py:54
  96.5 9.7 %collective-permute-start.23 = (bf16[4,8,32,128]{3,2,1,0:T(8,128)(2,1)S(1)}, bf16[4,8,32,128]{3,2,1,0:T(8,128)(2,1)S(1)}, u32[]{:S(2)}, u32[]{:S(2)}) collective-permute-start(bf16[4,8,32,128]{3,2,1,0:T(8,128)(2,1)S(1)} %bitcast.30), channel_id=1, source_target_pairs={{0,4},{1,17},{2,6},{3,19},{4,0},{5,21},{6,2},{7,23},{8,12},{9,25},... | collective-permute-start | bytes 786440 | tf_op jit(solution)/shard_map/ppermute | solution.py:54
  98.4 8.3 %collective-permute-start.24 = (bf16[4,8,32,128]{3,2,1,0:T(8,128)(2,1)S(1)}, bf16[4,8,32,128]{3,2,1,0:T(8,128)(2,1)S(1)}, u32[]{:S(2)}, u32[]{:S(2)}) collective-permute-start(bf16[4,8,32,128]{3,2,1,0:T(8,128)(2,1)S(1)} %bitcast.31), channel_id=1, source_target_pairs={{0,6},{1,25},{2,0},{3,27},{4,2},{5,29},{6,4},{7,31},{8,14},{9,1},{... | collective-permute-start | bytes 786440 | tf_op jit(solution)/shard_map/ppermute | solution.py:54
  107.2 9.5 %collective-permute-start.25 = (f32[128,512]{1,0:T(8,128)S(1)}, f32[128,512]{1,0:T(8,128)S(1)}, u32[]{:S(2)}, u32[]{:S(2)}) collective-permute-start(f32[128,512]{1,0:T(8,128)S(1)} %get-tuple-element.37), channel_id=1, source_target_pairs={{0,1},{1,0},{2,3},{3,2},{4,5},{5,4},{6,7},{7,6},{8,9},{9,8},{10,11... | collective-permute-start | bytes 786440 | tf_op jit(solution)/shard_map/ppermute | solution.py:29
  (14 other events, 106.3 us)
